TPU v7x, 32 devices: a whole 2x2x4 slice. The times are simulated.
32 devices in a mesh: fsdp: 8 (over z, x), seq: 4 (over y, core).
Axes of the slice: x: 2, y: 2, z: 4, core: 2. Of those that a mesh axis runs over, the one named last changes fastest.
Arguments:
- states: bfloat16 [24576, 768], P(('fsdp', 'seq')), may hold values from -6 to 6
- query_weight: bfloat16 [768, 768], P('fsdp'), may hold values from -0.21875 to 0.21875
- key_weight: bfloat16 [768, 768], P('fsdp'), may hold values from -0.21875 to 0.21875
- value_weight: bfloat16 [768, 768], P('fsdp'), may hold values from -0.21875 to 0.21875
- out_weight: bfloat16 [768, 768], P('fsdp'), may hold values from -3 to 3
- query_bias: bfloat16 [768], P('fsdp'), may hold values from -4 to 4
- value_bias: bfloat16 [768], P('fsdp'), may hold values from -0.3125 to 0.3125
- out_bias: bfloat16 [768], P('fsdp'), may hold values from -1.5 to 1.5
- first_gain: bfloat16 [768], P('fsdp'), may hold values from 0.5 to 1.5
- first_shift: bfloat16 [768], P('fsdp'), may hold values from -4 to 4
- up_weight: bfloat16 [768, 3072], P('fsdp'), may hold values from -0.21875 to 0.21875
- up_bias: bfloat16 [3072], P('fsdp'), may hold values from -4 to 4
- down_weight: bfloat16 [3072, 768], P('fsdp'), may hold values from -0.109375 to 0.109375
- down_bias: bfloat16 [768], P('fsdp'), may hold values from -1.5 to 1.5
- second_gain: bfloat16 [768], P('fsdp'), may hold values from 0.5 to 1.5
- second_shift: bfloat16 [768], P('fsdp'), may hold values from -6 to 6
- lengths: int32 [8], P('fsdp'), may hold values from 1536 to 3072, as said below
- cotangent: bfloat16 [24576, 768], P(('fsdp', 'seq')), may hold values from -6 to 6
Outputs:
- output: bfloat16 [24576, 768], P(('fsdp', 'seq'))
- states_grad: bfloat16 [24576, 768], P(('fsdp', 'seq'))
- query_weight_grad: float32 [768, 768], P('fsdp')
- key_weight_grad: float32 [768, 768], P('fsdp')
- value_weight_grad: float32 [768, 768], P('fsdp')
- out_weight_grad: float32 [768, 768], P('fsdp')
- query_bias_grad: float32 [768], P('fsdp')
- value_bias_grad: float32 [768], P('fsdp')
- out_bias_grad: float32 [768], P('fsdp')
- first_gain_grad: float32 [768], P('fsdp')
- first_shift_grad: float32 [768], P('fsdp')
- up_weight_grad: float32 [768, 3072], P('fsdp')
- up_bias_grad: float32 [3072], P('fsdp')
- down_weight_grad: float32 [3072, 768], P('fsdp')
- down_bias_grad: float32 [768], P('fsdp')
- second_gain_grad: float32 [768], P('fsdp')
- second_shift_grad: float32 [768], P('fsdp')
Inputs may be any that keep to these rules, and one draw needn't show every extreme that they name: Each group's real tokens fill its first lengths slots; the rest of its 3072 slots are padding. Some group is full in every draw.
All inputs are finite; a program needn't handle non-finite values.
Results may differ from a plain program's by a relative error of at most 0.017.
Values may be sent and summed in bfloat16 or wider, within the bound.
A program may use at most 192 MiB of HBM per device.

v0:
```python
import jax
import jax.numpy as jnp
from jax import lax
from jax.sharding import PartitionSpec as P

HEAD_DIM = 64


eps = 1e-12


def product(left, right):
    return jnp.dot(left, right, preferred_element_type=jnp.float32)


def left_product(left, right):
    return lax.dot_general(
        left, right, (((0,), (0,)), ((), ())), preferred_element_type=jnp.float32
    )


def right_product(left, right):
    return lax.dot_general(
        left, right, (((1,), (1,)), ((), ())), preferred_element_type=jnp.float32
    )


def layer_norm(values, gain, shift):
    average = jnp.mean(values, axis=-1, keepdims=True)
    centred = values - average
    spread = jnp.mean(centred * centred, axis=-1, keepdims=True)
    return centred * lax.rsqrt(spread + eps) * gain + shift


def gelu_exact(values):
    return jax.nn.gelu(values, approximate=False)


def column_sums(values):
    return jnp.sum(values.astype(jnp.float32), axis=0)


def per_device(
    states,
    query_weight,
    key_weight,
    value_weight,
    out_weight,
    query_bias,
    value_bias,
    out_bias,
    first_gain,
    first_shift,
    up_weight,
    up_bias,
    down_weight,
    down_bias,
    second_gain,
    second_shift,
    lengths,
    cotangent,
):
    f32 = jnp.float32
    bf16 = jnp.bfloat16
    (
        query_mat,
        key_mat,
        value_mat,
        out_mat,
        query_add,
        value_add,
        out_add,
        gain_first,
        shift_first,
    ) = (
        lax.all_gather(query_weight, "fsdp", axis=0, tiled=True),
        lax.all_gather(key_weight, "fsdp", axis=0, tiled=True),
        lax.all_gather(value_weight, "fsdp", axis=0, tiled=True),
        lax.all_gather(out_weight, "fsdp", axis=0, tiled=True),
        lax.all_gather(query_bias, "fsdp", axis=0, tiled=True),
        lax.all_gather(value_bias, "fsdp", axis=0, tiled=True),
        lax.all_gather(out_bias, "fsdp", axis=0, tiled=True),
        lax.all_gather(first_gain, "fsdp", axis=0, tiled=True),
        lax.all_gather(first_shift, "fsdp", axis=0, tiled=True),
    )
    up_mat, up_add, down_mat, down_add, gain_second, shift_second = (
        lax.all_gather(up_weight, "fsdp", axis=0, tiled=True),
        lax.all_gather(up_bias, "fsdp", axis=0, tiled=True),
        lax.all_gather(down_weight, "fsdp", axis=0, tiled=True),
        lax.all_gather(down_bias, "fsdp", axis=0, tiled=True),
        lax.all_gather(second_gain, "fsdp", axis=0, tiled=True),
        lax.all_gather(second_shift, "fsdp", axis=0, tiled=True),
    )
    tokens = states.shape[0]
    slot_rows = tokens * lax.axis_size("seq")
    length = lengths[0]
    places = lax.axis_index("seq") * tokens + lax.iota(jnp.int32, tokens)
    valid_rows = (places < length).astype(f32)[:, None]
    queries = (product(states, query_mat) + query_add).astype(bf16)
    keys_in = product(states, key_mat).astype(bf16)
    values = (product(states, value_mat) + value_add).astype(bf16)
    head_queries, head_keys, head_values = (
        lax.all_to_all(queries, "seq", split_axis=1, concat_axis=0, tiled=True),
        lax.all_to_all(keys_in, "seq", split_axis=1, concat_axis=0, tiled=True),
        lax.all_to_all(values, "seq", split_axis=1, concat_axis=0, tiled=True),
    )
    local_width = head_queries.shape[1]
    head_count = local_width // HEAD_DIM
    block_rows = min(512, slot_rows)
    blocks = slot_rows // block_rows
    scaling = HEAD_DIM ** (-0.5)
    key_valid = lax.iota(jnp.int32, slot_rows) < length
    keys_heads = head_keys.reshape(slot_rows, head_count, HEAD_DIM)
    values_heads = head_values.reshape(slot_rows, head_count, HEAD_DIM)
    query_blocks = head_queries.reshape(blocks, block_rows, head_count, HEAD_DIM)

    def block_scores(query_block):
        scores = (
            jnp.einsum("qhd,khd->hqk", query_block, keys_heads, preferred_element_type=f32)
            * scaling
        )
        return jnp.where(key_valid[None, None, :], scores, -1000000000.0)

    def forward_block(query_block):
        scores = block_scores(query_block)
        highest = jnp.max(scores, axis=-1, keepdims=True)
        exponent = jnp.exp(scores - highest)
        totals = jnp.sum(exponent, axis=-1, keepdims=True)
        weights_soft = (exponent / totals).astype(bf16)
        context_part = jnp.einsum(
            "hqk,khd->qhd", weights_soft, values_heads, preferred_element_type=f32
        )
        return (context_part.astype(bf16), (highest + jnp.log(totals))[:, :, 0])

    context_blocks, log_totals = lax.map(forward_block, query_blocks)
    context = lax.all_to_all(
        context_blocks.reshape(slot_rows, local_width),
        "seq",
        split_axis=0,
        concat_axis=1,
        tiled=True,
    )
    hidden = states.astype(f32)
    first_sum = hidden + (product(context, out_mat) + out_add)
    first_norm, first_back = jax.vjp(
        layer_norm, first_sum, gain_first.astype(f32), shift_first.astype(f32)
    )
    first_low = first_norm.astype(bf16)
    pre_act = product(first_low, up_mat) + up_add
    activated = gelu_exact(pre_act).astype(bf16)
    second_sum = first_norm + (product(activated, down_mat) + down_add)
    normed, second_back = jax.vjp(
        layer_norm, second_sum, gain_second.astype(f32), shift_second.astype(f32)
    )
    output = (normed * valid_rows).astype(bf16)
    out_grad = cotangent.astype(f32) * valid_rows
    second_grad, gain_second_grad, shift_second_grad = second_back(out_grad)
    down_in = second_grad.astype(bf16)
    down_weight_grad = left_product(activated, down_in)
    down_bias_grad = column_sums(down_in)
    act_grad = right_product(down_in, down_mat)
    pre_grad = jax.vjp(gelu_exact, pre_act)[1](act_grad)[0].astype(bf16)
    up_weight_grad = left_product(first_low, pre_grad)
    up_bias_grad = column_sums(pre_grad)
    norm_grad = second_grad + right_product(pre_grad, up_mat)
    first_grad, gain_first_grad, shift_first_grad = first_back(norm_grad)
    branch_grad = first_grad.astype(bf16)
    out_weight_grad = left_product(context, branch_grad)
    out_bias_grad = column_sums(branch_grad)
    context_grad = right_product(branch_grad, out_mat).astype(bf16)
    head_grad = lax.all_to_all(context_grad, "seq", split_axis=1, concat_axis=0, tiled=True)
    grad_blocks = head_grad.reshape(blocks, block_rows, head_count, HEAD_DIM)

    def backward_step(carry, packed):
        key_acc, value_acc = carry
        query_block, grad_block, log_block = packed
        scores = block_scores(query_block)
        probs_full = jnp.exp(scores - log_block[:, :, None])
        probs_low = probs_full.astype(bf16)
        prob_grad = jnp.einsum("qhd,khd->hqk", grad_block, values_heads, preferred_element_type=f32)
        centre = jnp.sum(prob_grad * probs_full, axis=-1, keepdims=True)
        score_grad = (probs_full * (prob_grad - centre)).astype(bf16)
        query_part = (
            jnp.einsum("hqk,khd->qhd", score_grad, keys_heads, preferred_element_type=f32) * scaling
        )
        key_acc = (
            key_acc
            + jnp.einsum("hqk,qhd->khd", score_grad, query_block, preferred_element_type=f32)
            * scaling
        )
        value_acc = value_acc + jnp.einsum(
            "hqk,qhd->khd", probs_low, grad_block, preferred_element_type=f32
        )
        return ((key_acc, value_acc), query_part.astype(bf16))

    zeros_heads = jnp.zeros((slot_rows, head_count, HEAD_DIM), f32)
    (key_total, value_total), query_parts = lax.scan(
        backward_step, (zeros_heads, zeros_heads), (query_blocks, grad_blocks, log_totals)
    )
    query_back, key_back, value_back = (
        lax.all_to_all(
            query_parts.reshape(slot_rows, local_width),
            "seq",
            split_axis=0,
            concat_axis=1,
            tiled=True,
        ),
        lax.all_to_all(
            key_total.reshape(slot_rows, local_width).astype(bf16),
            "seq",
            split_axis=0,
            concat_axis=1,
            tiled=True,
        ),
        lax.all_to_all(
            value_total.reshape(slot_rows, local_width).astype(bf16),
            "seq",
            split_axis=0,
            concat_axis=1,
            tiled=True,
        ),
    )
    query_weight_grad = left_product(states, query_back)
    key_weight_grad = left_product(states, key_back)
    value_weight_grad = left_product(states, value_back)
    query_bias_grad = column_sums(query_back)
    value_bias_grad = column_sums(value_back)
    states_grad = (
        first_grad
        + right_product(query_back, query_mat)
        + right_product(key_back, key_mat)
        + right_product(value_back, value_mat)
    ).astype(bf16)
    attend_parts = (
        lax.psum_scatter(query_weight_grad, "fsdp", scatter_dimension=0, tiled=True),
        lax.psum_scatter(key_weight_grad, "fsdp", scatter_dimension=0, tiled=True),
        lax.psum_scatter(value_weight_grad, "fsdp", scatter_dimension=0, tiled=True),
        lax.psum_scatter(out_weight_grad, "fsdp", scatter_dimension=0, tiled=True),
        lax.psum_scatter(query_bias_grad, "fsdp", scatter_dimension=0, tiled=True),
        lax.psum_scatter(value_bias_grad, "fsdp", scatter_dimension=0, tiled=True),
        lax.psum_scatter(out_bias_grad, "fsdp", scatter_dimension=0, tiled=True),
        lax.psum_scatter(gain_first_grad, "fsdp", scatter_dimension=0, tiled=True),
        lax.psum_scatter(shift_first_grad, "fsdp", scatter_dimension=0, tiled=True),
    )
    feed_parts = (
        lax.psum_scatter(up_weight_grad, "fsdp", scatter_dimension=0, tiled=True),
        lax.psum_scatter(up_bias_grad, "fsdp", scatter_dimension=0, tiled=True),
        lax.psum_scatter(down_weight_grad, "fsdp", scatter_dimension=0, tiled=True),
        lax.psum_scatter(down_bias_grad, "fsdp", scatter_dimension=0, tiled=True),
        lax.psum_scatter(gain_second_grad, "fsdp", scatter_dimension=0, tiled=True),
        lax.psum_scatter(shift_second_grad, "fsdp", scatter_dimension=0, tiled=True),
    )
    summed = (
        lax.psum(attend_parts[0].astype(jnp.bfloat16), "seq").astype(jnp.float32),
        lax.psum(attend_parts[1].astype(jnp.bfloat16), "seq").astype(jnp.float32),
        lax.psum(attend_parts[2].astype(jnp.bfloat16), "seq").astype(jnp.float32),
        lax.psum(attend_parts[3].astype(jnp.bfloat16), "seq").astype(jnp.float32),
        lax.psum(attend_parts[4].astype(jnp.bfloat16), "seq").astype(jnp.float32),
        lax.psum(attend_parts[5].astype(jnp.bfloat16), "seq").astype(jnp.float32),
        lax.psum(attend_parts[6].astype(jnp.bfloat16), "seq").astype(jnp.float32),
        lax.psum(attend_parts[7].astype(jnp.bfloat16), "seq").astype(jnp.float32),
        lax.psum(attend_parts[8].astype(jnp.bfloat16), "seq").astype(jnp.float32),
        lax.psum(feed_parts[0].astype(jnp.bfloat16), "seq").astype(jnp.float32),
        lax.psum(feed_parts[1].astype(jnp.bfloat16), "seq").astype(jnp.float32),
        lax.psum(feed_parts[2].astype(jnp.bfloat16), "seq").astype(jnp.float32),
        lax.psum(feed_parts[3].astype(jnp.bfloat16), "seq").astype(jnp.float32),
        lax.psum(feed_parts[4].astype(jnp.bfloat16), "seq").astype(jnp.float32),
        lax.psum(feed_parts[5].astype(jnp.bfloat16), "seq").astype(jnp.float32),
    )
    return (
        output,
        states_grad,
        summed[0],
        summed[1],
        summed[2],
        summed[3],
        summed[4],
        summed[5],
        summed[6],
        summed[7],
        summed[8],
        summed[9],
        summed[10],
        summed[11],
        summed[12],
        summed[13],
        summed[14],
    )


def solution(mesh):
    return jax.shard_map(
        per_device,
        mesh=mesh,
        in_specs=(
            P(("fsdp", "seq"), None),
            P("fsdp", None),
            P("fsdp", None),
            P("fsdp", None),
            P("fsdp", None),
            P("fsdp"),
            P("fsdp"),
            P("fsdp"),
            P("fsdp"),
            P("fsdp"),
            P("fsdp", None),
            P("fsdp"),
            P("fsdp", None),
            P("fsdp"),
            P("fsdp"),
            P("fsdp"),
            P("fsdp"),
            P(("fsdp", "seq"), None),
        ),
        out_specs=(
            P(("fsdp", "seq"), None),
            P(("fsdp", "seq"), None),
            P("fsdp", None),
            P("fsdp", None),
            P("fsdp", None),
            P("fsdp", None),
            P("fsdp"),
            P("fsdp"),
            P("fsdp"),
            P("fsdp"),
            P("fsdp"),
            P("fsdp", None),
            P("fsdp"),
            P("fsdp", None),
            P("fsdp"),
            P("fsdp"),
            P("fsdp"),
        ),
        check_vma=False,
    )
```

profile of v0, /device:TPU:0, one launch (start us, length us, event | category | flops | bytes accessed | tf_op | source)
XLA Modules:
  0.0 1477.9 jit_solution(3227947510034130360)
XLA Ops:
  19.3 39.9 %all-reduce.18 = (bf16[768]{0:T(1024)(128)(2,1)S(1)}, bf16[768]{0:T(1024)(128)(2,1)S(1)}, bf16[768]{0:T(1024)(128)(2,1)}, bf16[768]{0:T(1024)(128)(2,1)}, bf16[7...) all-reduce(bf16[768]{0:T(1024)(128)(2,1)S(1)} %dynamic-update-slice, ...), channel_id=1, replica_groups=mesh['fsdp'=8,'seq'=4] {'fsdp'}, use_global_device_ids=true, to_apply=%add | all-reduce | flops 6144 | bytes 24576
  66.6 29.8 %all-gather.8.cloned.1.call-done = bf16[768,768]{1,0:T(8,128)(2,1)} async-done(((bf16[96,768]{1,0:T(8,128)(2,1)}), bf16[768,768]{1,0:T(8,128)(2,1)}) %all-gather.8.cloned.1.call-update) | async-done | bytes 1179664 | tf_op jit(solution)/shard_map/all_gather | solution.py:76
  103.3 35.1 %all-gather.10.cloned.1.call-done = bf16[768,768]{1,0:T(8,128)(2,1)} async-done(((bf16[96,768]{1,0:T(8,128)(2,1)}), bf16[768,768]{1,0:T(8,128)(2,1)}) %all-gather.10.cloned.1.call-update) | async-done | bytes 1179664 | tf_op jit(solution)/shard_map/all_gather | solution.py:77
  169.0 190.7 %while.28 = (s32[]{:T(128)}, bf16[6,512,3,64]{1,3,2,0:T(8,128)(2,1)}, f32[6,3,512]{2,1,0:T(4,128)}, bf16[6,512,3,64]{1,3,2,0:T(8,128)(2,1)S(1)}, bf16[3072,3,64]...) while((s32[]{:T(128)}, bf16[6,512,3,64]{1,3,2,0:T(8,128)(2,1)}, ...), condition=%wide.region_3.4_spmd.clone, body=%wide.region_0.3_spmd.clone.sunk | while | flops 1264682496 | bytes 59465864 | solution.py:135
  379.8 25.9 %all-gather = bf16[8,1,384]{2,1,0:T(2,128)(2,1)S(1)} all-gather(bf16[1,1,384]{2,1,0:T(2,128)(2,1)S(1)} %reshape.217), channel_id=1, replica_groups=mesh['fsdp'=8,'seq'=4] {'fsdp'}, dimensions={0}, use_global_device_ids=true | all-gather | bytes 6912 | tf_op jit(solution)/shard_map/all_gather | solution.py:88
  412.2 29.8 %multiply_convert_fusion.1 = (bf16[768,3072]{1,0:T(8,128)(2,1)}, f32[768,3072]{1,0:T(8,128)}, f32[768,3072]{1,0:T(8,128)}) fusion(f32[3072]{0:T(1024)S(1)} %bitcast.180, bf16[768,3072]{1,0:T(8,128)(2,1)} %all-gather.16.cloned.1.call-done, f32[768,768]{0,1:T(8,128)} %copy-done.5, f32[768]{0:T(1024)S(1)} %convert_element_type.223, ...), kind=kOutput, calls=%fused_computation.56 | convolution fusion | flops 3782541312 | bytes 30695424 | tf_op jit(solution)/shard_map/dot_general | solution.py:13
  457.1 15.0 %convert_reduce_fusion = (f32[3072]{0:T(1024)}, bf16[768,3072]{1,0:T(8,128)(2,1)}) fusion(f32[768,3072]{1,0:T(8,128)} %get-tuple-element.403, f32[768,3072]{1,0:T(8,128)} %get-tuple-element.415, f32[3072]{0:T(1024)S(1)} %bitcast.181, bf16[768,768]{0,1:T(8,128)(2,1)S(1)} %get-tuple-element.395, bf16[3072,768]{1,0:T(8,128)(2,1)} %all-gather.18.cloned.1.call-done), kind=kOutput, calls=%fused_computation.54 | convolution fusion | flops 3663983616 | bytes 29515776 | tf_op jit(solution)/shard_map/dot_general | solution.py:23
  516.2 313.4 %while.29 = (s32[]{:T(128)}, f32[3072,3,64]{0,2,1:T(8,128)S(1)}, f32[3072,3,64]{0,2,1:T(8,128)}, bf16[6,512,3,64]{1,3,2,0:T(8,128)(2,1)}, bf16[6,512,3,64]{1,3,2...) while((s32[]{:T(128)}, f32[3072,3,64]{0,2,1:T(8,128)S(1)}, ...), condition=%wide.region_14.15_spmd.clone, body=%wide.region_12.14_spmd.clone.sunk | while | flops 3093825024 | bytes 231069888 | solution.py:197
  534.2 13.5 multiply_reduce_fusion.8
  547.7 13.7 multiply_convert_fusion.4
  586.8 13.2 multiply_reduce_fusion.8
  600.1 13.6 multiply_convert_fusion.4
  652.3 13.6 multiply_convert_fusion.4
  704.6 13.6 multiply_convert_fusion.4
  756.9 13.6 multiply_convert_fusion.4
  809.1 13.6 multiply_convert_fusion.4
  835.8 18.4 %all_to_all.134 = bf16[4,768,192]{1,2,0:T(8,128)(2,1)S(1)} all-to-all(bf16[4,768,192]{1,2,0:T(8,128)(2,1)S(1)} %copy.133), channel_id=1, replica_groups=mesh['fsdp'=8,'seq'=4] {'seq'}, dimensions={0} | all-to-all | bytes 2359296 | tf_op jit(solution)/shard_map/all_to_all | solution.py:201
  862.2 18.4 %all_to_all.135 = bf16[4,768,192]{1,2,0:T(8,128)(2,1)S(1)} all-to-all(bf16[4,768,192]{1,2,0:T(8,128)(2,1)S(1)} %copy.135), channel_id=1, replica_groups=mesh['fsdp'=8,'seq'=4] {'seq'}, dimensions={0} | all-to-all | bytes 2359296 | tf_op jit(solution)/shard_map/all_to_all | solution.py:208
  887.6 18.4 %all_to_all.136 = bf16[4,768,192]{1,2,0:T(8,128)(2,1)S(1)} all-to-all(bf16[4,768,192]{1,2,0:T(8,128)(2,1)S(1)} %copy.137), channel_id=1, replica_groups=mesh['fsdp'=8,'seq'=4] {'seq'}, dimensions={0} | all-to-all | bytes 2359296 | tf_op jit(solution)/shard_map/all_to_all | solution.py:215
  943.1 55.3 %reduce-scatter.21.cloned.1.call-done = f32[96,768]{1,0:T(8,128)} async-done(((f32[768,768]{1,0:T(8,128)}), f32[96,768]{1,0:T(8,128)}) %reduce-scatter.21.cloned.1.call-update) | async-done | bytes 294928
  1000.2 69.7 %reduce-scatter.23.cloned.1.call-done = f32[96,768]{1,0:T(8,128)} async-done(((f32[768,768]{1,0:T(8,128)}), f32[96,768]{1,0:T(8,128)}) %reduce-scatter.23.cloned.1.call-update) | async-done | bytes 294928
  1071.6 164.3 %reduce-scatter.15.cloned.1.call-done = f32[96,3072]{1,0:T(8,128)} async-done(((f32[768,3072]{1,0:T(8,128)}), f32[96,3072]{1,0:T(8,128)}) %reduce-scatter.15.cloned.1.call-update) | async-done | bytes 1179664 | tf_op jit(solution)/shard_map/reduce_scatter | solution.py:246
  1238.1 163.9 %reduce-scatter.17.cloned.1.call-done = f32[384,768]{1,0:T(8,128)} async-done(((f32[3072,768]{1,0:T(8,128)}), f32[384,768]{1,0:T(8,128)}) %reduce-scatter.17.cloned.1.call-update) | async-done | bytes 1179664 | tf_op jit(solution)/shard_map/reduce_scatter | solution.py:248
  1413.4 35.6 %all-reduce.17 = (bf16[768]{0:T(1024)(128)(2,1)S(1)}, bf16[768]{0:T(1024)(128)(2,1)S(1)}, bf16[768]{0:T(1024)(128)(2,1)S(1)}, bf16[768]{0:T(1024)(128)(2,1)S(1)}...) all-reduce(f32[768]{0:T(1024)S(1)} %reduce_sum.216, ...), channel_id=6, replica_groups=mesh['fsdp'=8,'seq'=4] {'fsdp'}, use_global_device_ids=true, to_apply=%region_24.25.clone | all-reduce | flops 9216 | bytes 55296
  (364 shorter events, 631.0 us)
Async XLA Ops:
  7.2 52.0 %all-gather.12.cloned.1.call-start = ((), (), s32[]{:S(2)}) async-start(), calls=%async_computation.16 | async-start | bytes 1327104 | tf_op jit(solution)/shard_map/all_gather | solution.py:78
  7.9 88.5 %all-gather.8.cloned.1.call-start = ((), (), s32[]{:S(2)}) async-start(), calls=%async_computation.14 | async-start | bytes 1327104 | tf_op jit(solution)/shard_map/all_gather | solution.py:76
  8.7 129.8 %all-gather.10.cloned.1.call-start = ((), (), s32[]{:S(2)}) async-start(), calls=%async_computation.15 | async-start | bytes 1327104 | tf_op jit(solution)/shard_map/all_gather | solution.py:77
  9.4 397.8 %all-gather.14.cloned.1.call-start = ((), (), s32[]{:S(2)}) async-start(), calls=%async_computation.17 | async-start | bytes 1327104 | tf_op jit(solution)/shard_map/all_gather | solution.py:79
  10.0 402.2 %all-gather.16.cloned.1.call-start = ((), (), s32[]{:S(2)}) async-start(), calls=%async_computation.18 | async-start | bytes 5308416 | tf_op jit(solution)/shard_map/all_gather | solution.py:87
  62.9 36.9 %all-to-all-start.2 = ((bf16[768,4,192]{0,2,1:T(8,128)(2,1)}), bf16[768,4,192]{0,2,1:T(8,128)(2,1)S(1)}, u32[]{:S(2)}, u32[]{:S(2)}) async-start(bf16[768,4,192]{0,2,1:T(8,128)(2,1)} %bitcast.5), calls=%async_computation.2 | async-start | bytes 2359296 | tf_op jit(solution)/shard_map/all_to_all | solution.py:105
  99.8 42.1 %all-to-all-start = ((bf16[768,4,192]{0,2,1:T(8,128)(2,1)}), bf16[768,4,192]{0,2,1:T(8,128)(2,1)S(1)}, u32[]{:S(2)}, u32[]{:S(2)}) async-start(bf16[768,4,192]{0,2,1:T(8,128)(2,1)} %bitcast.179), calls=%async_computation | async-start | bytes 2359296 | tf_op jit(solution)/shard_map/all_to_all | solution.py:103
  141.9 20.2 %all-to-all-start.1 = ((bf16[768,4,192]{0,2,1:T(8,128)(2,1)}), bf16[768,4,192]{0,2,1:T(8,128)(2,1)}, u32[]{:S(2)}, u32[]{:S(2)}) async-start(bf16[768,4,192]{0,2,1:T(8,128)(2,1)} %bitcast.178), calls=%async_computation.1 | async-start | bytes 2359296 | tf_op jit(solution)/shard_map/all_to_all | solution.py:104
  146.2 295.8 %all-gather.18.cloned.1.call-start = ((), (), s32[]{:S(2)}) async-start(), calls=%async_computation.19 | async-start | bytes 5308416 | tf_op jit(solution)/shard_map/all_gather | solution.py:89
  370.0 37.2 %all-to-all-start.3 = ((bf16[4,768,192]{1,2,0:T(8,128)(2,1)}), bf16[4,768,192]{1,2,0:T(8,128)(2,1)}, u32[]{:S(2)}, u32[]{:S(2)}) async-start(bf16[4,768,192]{1,2,0:T(8,128)(2,1)} %copy.126), calls=%async_computation.3 | async-start | bytes 2359296 | tf_op jit(solution)/shard_map/all_to_all | solution.py:136
  376.6 103.6 %copy-start.29 = (f32[768]{0:T(1024)}, f32[768]{0:T(1024)S(1)}, u32[]{:S(2)}) copy-start(f32[768]{0:T(1024)S(1)} %convert_element_type.222) | copy-start | bytes 9220
  377.3 64.7 %copy-start.39 = (f32[768]{0:T(1024)}, f32[768]{0:T(1024)S(1)}, u32[]{:S(2)}) copy-start(f32[768]{0:T(1024)S(1)} %convert_element_type.223) | copy-start | bytes 9220
  410.5 69.7 %copy-start.27 = (f32[768]{0:T(1024)}, f32[768]{0:T(1024)S(1)}, u32[]{:S(2)}) copy-start(f32[768]{0:T(1024)S(1)} %broadcast_multiply_fusion.1) | copy-start | bytes 9220
  412.1 68.0 %copy-start.31 = (f32[768]{0:T(1024)}, f32[768]{0:T(1024)S(1)}, u32[]{:S(2)}) copy-start(f32[768]{0:T(1024)S(1)} %fusion.57) | copy-start | bytes 9220
  485.1 20.2 %all-to-all-start.4 = ((bf16[768,4,192]{0,2,1:T(8,128)(2,1)}), bf16[768,4,192]{0,2,1:T(8,128)(2,1)}, u32[]{:S(2)}, u32[]{:S(2)}) async-start(bf16[768,4,192]{0,2,1:T(8,128)(2,1)} %bitcast.11), calls=%async_computation.4 | async-start | bytes 2359296 | tf_op jit(solution)/shard_map/all_to_all | solution.py:171
  489.4 450.3 %reduce-scatter.13.cloned.1.call-start = ((), (), s32[]{:S(2)}) async-start(), calls=%async_computation.20 | async-start | bytes 2654208 | tf_op jit(solution)/shard_map/reduce_scatter | solution.py:238
  493.7 447.6 %reduce-scatter.19.cloned.1.call-start = ((), (), s32[]{:S(2)}) async-start(), calls=%async_computation.23 | async-start | bytes 2654208
  860.9 137.5 %reduce-scatter.21.cloned.1.call-start = ((), (), s32[]{:S(2)}) async-start(), calls=%async_computation.24 | async-start | bytes 2654208
  884.8 185.1 %reduce-scatter.23.cloned.1.call-start = ((), (), s32[]{:S(2)}) async-start(), calls=%async_computation.25 | async-start | bytes 2654208
  909.2 326.8 %reduce-scatter.15.cloned.1.call-start = ((), (), s32[]{:S(2)}) async-start(), calls=%async_computation.21 | async-start | bytes 10616832 | tf_op jit(solution)/shard_map/reduce_scatter | solution.py:246
  919.9 482.1 %reduce-scatter.17.cloned.1.call-start = ((), (), s32[]{:S(2)}) async-start(), calls=%async_computation.22 | async-start | bytes 10616832 | tf_op jit(solution)/shard_map/reduce_scatter | solution.py:248
  930.1 530.6 %all-reduce.23.cloned.1.call-start = ((), (), s32[]{:S(2)}) async-start(), calls=%async_computation.26 | async-start | bytes 3833856 | tf_op jit(solution)/shard_map/psum | solution.py:254
  1238.1 167.6 %copy-start.3 = (f32[768,768]{0,1:T(8,128)S(1)}, f32[768,768]{0,1:T(8,128)}, u32[]{:S(2)}) copy-start(f32[768,768]{0,1:T(8,128)} %copy-done.2) | copy-start | bytes 7077892
  1238.1 167.6 %copy-start.26 = (f32[768]{0:T(1024)S(1)}, f32[768]{0:T(1024)}, u32[]{:S(2)}) copy-start(f32[768]{0:T(1024)} %copy-done.25) | copy-start | bytes 9220
  (56 other events, 448.8 us)
Sparse Core Ops, SparseCore 0:
  10.2 44.0 all-gather.11
  56.4 39.8 all-gather.7
  98.6 39.8 all-gather.9
  140.5 39.8 all-gather.13
  182.5 78.6 all-gather.15
  263.2 77.9 all-gather.17
  493.8 66.7 reduce-scatter.12
  861.0 65.7 reduce-scatter.18
  930.3 68.0 reduce-scatter.20
  1001.8 68.0 reduce-scatter.22
  1073.5 162.4 reduce-scatter.14
  1239.4 162.5 reduce-scatter.16
  1405.9 48.8 all-reduce.22
where the time goes:
time: 1490 us; the launch traced here: 1480 us
  waiting for transfers between devices  540 us (36%)
  matrix products  417 us (28%)
  other arithmetic  188 us (13%)
  blocking collectives  163 us (11%)
  local copies, waits for them, and re-layouts  130 us (9%)
  starting transfers between devices  20.7 us (1%)
  between operations  17.8 us (1%)
    reduce_scatter x1, waiting for transfers between devices, per_device(): lax.psum_scatter(up_weight_grad, 'fsdp', scatter_dimension=0, tiled=True)  164 us
    reduce_scatter x1, waiting for transfers between devices, per_device(): lax.psum_scatter(down_weight_grad, 'fsdp', scatter_dimension=0, tiled=True)  164 us
    unnamed x16, waiting for transfers between devices  129 us
    convert_element_type x6, other arithmetic, backward_step(): score_grad = (probs_full * (prob_grad - centre)).astype(bf16)  81.5 us
    dot_general x6, matrix products, backward_step(): jnp.einsum('qhd,khd->hqk', grad_block, values_heads, preferred_element_ty...  79.6 us
    unnamed x2, blocking collectives  75.5 us
    dot_general x12, matrix products, block_scores(): jnp.einsum('qhd,khd->hqk', query_block, keys_heads, preferred_element_typ...  70.1 us
    dot_general x6, matrix products, forward_block(): jnp.einsum('hqk,khd->qhd', weights_soft, values_heads, preferred_element_...  67.8 us
  transfers between devices with their start and end apart: 18, of which 8 were waited for; matrix products, arithmetic and copies ran while one was open for 42% of the time, Pallas kernels for 0%

commit v1 on v0

--- a/solution.py
+++ b/solution.py
@@ -1,6 +1,11 @@
+import functools
+import math
+
 import jax
 import jax.numpy as jnp
 from jax import lax
+from jax.experimental import pallas as pl
+from jax.experimental.pallas import tpu as pltpu
 from jax.sharding import PartitionSpec as P
 
 HEAD_DIM = 64
@@ -288,9 +293,1084 @@
     )
 
 
+LANE = 128
+LOG2E = math.log2(math.e)
+LN2 = math.log(2.0)
+NT = (((1,), (1,)), ((), ()))
+NN = (((1,), (0,)), ((), ()))
+TN = (((0,), (0,)), ((), ()))
+VMEM_BYTES = 66 * 1024 * 1024 - 2 * 1024 * 1024
+f32 = jnp.float32
+bf16 = jnp.bfloat16
+ANY = pl.BlockSpec(memory_space=pl.ANY)
+IN_VMEM = pl.BlockSpec(memory_space=pltpu.VMEM)
+IN_SMEM = pl.BlockSpec(memory_space=pltpu.SMEM)
+DMA = pltpu.SemaphoreType.DMA
+
+
+def dims(left, right, numbers):
+    return lax.dot_general(left, right, numbers, preferred_element_type=f32)
+
+
+def remote(src, dst, send_sem, recv_sem, **where):
+    return pltpu.make_async_remote_copy(
+        src_ref=src,
+        dst_ref=dst,
+        send_sem=send_sem,
+        recv_sem=recv_sem,
+        device_id=where,
+        device_id_type=pl.DeviceIdType.MESH,
+    )
+
+
+def greet(partners):
+    barrier = pltpu.get_barrier_semaphore()
+    for where in partners:
+        pl.semaphore_signal(barrier, inc=1, device_id=where, device_id_type=pl.DeviceIdType.MESH)
+    pl.semaphore_wait(barrier, len(partners))
+
+
+def seq_peers():
+    me = lax.axis_index("seq")
+    across = (me + 2) % 4
+    return me, me + 1 - 2 * (me % 2), across, across + 1 - 2 * (across % 2)
+
+
+def place_of(index, count):
+    half = index // 2
+    return half + (index % 2) * (count - 1 - 2 * half)
+
+
+def index_at(place, count):
+    upper = place // (count // 2)
+    return (1 - upper) * 2 * place + upper * (2 * (count - 1 - place) + 1)
+
+
+def thirds(values):
+    high = values.astype(bf16)
+    rest = values - high.astype(f32)
+    middle = rest.astype(bf16)
+    low = (rest - middle.astype(f32)).astype(bf16)
+    return high.astype(f32), middle.astype(f32), low.astype(f32)
+
+
+def with_lanes(base, columns):
+    lane = lax.broadcasted_iota(jnp.int32, base.shape, 1)
+    for place, values in columns:
+        base = jnp.where(lane == place, values, base)
+    return base
+
+
+def params(collective_id=None):
+    if collective_id is None:
+        return pltpu.CompilerParams(vmem_limit_bytes=VMEM_BYTES)
+    return pltpu.CompilerParams(
+        vmem_limit_bytes=VMEM_BYTES, collective_id=collective_id, has_side_effects=True
+    )
+
+
+def project_kernel(
+    nf, pieces, length_ref, states, wq, wk, wv, vec, q_ref, k_ref, v_ref, x_out, vec_out,
+    x_buf, w_buf, vec_buf, local_sem, out_sem, vec_send, vec_recv, w_send, w_recv,
+    near_send, near_recv, far_send, far_recv, pass_send, pass_recv,
+):
+    f = lax.axis_index("fsdp")
+    s, near, far, cross = seq_peers()
+    tokens, width = states.shape
+    heads = q_ref.shape[0]
+    rows = wq.shape[0]
+    window = w_buf.shape[3]
+    own_width = heads * 64
+    fine = pieces
+    chunk = tokens // fine
+    first_lane = pl.multiple_of((own_width * s // LANE) * LANE, LANE)
+    weights = (wq, wk, wv)
+    greet(
+        [{"fsdp": (f + d) % nf} for d in range(1, nf)]
+        + [{"seq": near}, {"seq": far}]
+    )
+    sends = []
+    for d in range(1, nf):
+        to = (f + d) % nf
+        copy = remote(vec, vec_buf.at[f], vec_send.at[d - 1], vec_recv.at[d - 1], fsdp=to)
+        copy.start()
+        sends.append(copy)
+        for m in range(3):
+            copy = remote(
+                weights[m].at[:, pl.ds(first_lane, window)],
+                w_buf.at[m, f],
+                w_send.at[d - 1, m],
+                w_recv.at[d - 1, m],
+                fsdp=to,
+            )
+            copy.start()
+            sends.append(copy)
+    for c in range(fine):
+        part = pl.ds(c * chunk, chunk)
+        copy = remote(
+            states.at[part], x_buf.at[2, part], far_send.at[c], far_recv.at[c], seq=far
+        )
+        copy.start()
+        sends.append(copy)
+    near_copy = remote(states, x_buf.at[1], near_send, near_recv, seq=near)
+    near_copy.start()
+    sends.append(near_copy)
+    locals_ = [
+        pltpu.make_async_copy(states, x_buf.at[0], local_sem.at[0]),
+        pltpu.make_async_copy(vec, vec_buf.at[f], local_sem.at[1]),
+    ]
+    for m in range(3):
+        locals_.append(
+            pltpu.make_async_copy(
+                weights[m].at[:, pl.ds(first_lane, window)], w_buf.at[m, f], local_sem.at[2 + m]
+            )
+        )
+    for copy in locals_:
+        copy.start()
+    for copy in locals_:
+        copy.wait()
+
+    def pass_on(c):
+        part = pl.ds(c * chunk, chunk)
+        remote(
+            states.at[part], x_buf.at[2, part], far_send.at[c], far_recv.at[c], seq=far
+        ).wait_recv()
+        copy = remote(
+            x_buf.at[2, part], x_buf.at[3, part], pass_send.at[c], pass_recv.at[c], seq=near
+        )
+        copy.start()
+        sends.append(copy)
+
+    outs = []
+
+    def keep(slot, index):
+        copy = pltpu.make_async_copy(x_buf.at[slot], x_out.at[index], out_sem.at[slot])
+        copy.start()
+        outs.append(copy)
+
+    keep(0, s)
+    early = fine // 2
+    for c in range(early):
+        pass_on(c)
+    for d in range(1, nf):
+        frm = (f + nf - d) % nf
+        remote(vec, vec_buf.at[f], vec_send.at[d - 1], vec_recv.at[d - 1], fsdp=frm).wait_recv()
+        for m in range(3):
+            remote(
+                weights[m].at[:, pl.ds(first_lane, window)],
+                w_buf.at[m, f],
+                w_send.at[d - 1, m],
+                w_recv.at[d - 1, m],
+                fsdp=frm,
+            ).wait_recv()
+
+    turn = (window - (own_width * s) % LANE) % window
+    share = own_width // rows
+    wide = lax.broadcasted_iota(jnp.int32, (1, window), 1)
+    biases = []
+    for row in (0, 1):
+        line = jnp.zeros((1, window), f32)
+        for i in range(share):
+            piece = vec_buf[share * s + i][row : row + 1, :].astype(f32)
+            piece = jnp.concatenate([piece, jnp.zeros((1, window - LANE), f32)], axis=1)
+            if i:
+                piece = pltpu.roll(piece, i * rows, 1)
+            line = jnp.where((wide >= i * rows) & (wide < (i + 1) * rows), piece, line)
+        biases.append(line)
+    length = length_ref[0]
+    block = min(256, tokens)
+    mats = [w_buf[m].reshape(nf * rows, window) for m in range(3)]
+    lane = lax.broadcasted_iota(jnp.int32, (block, LANE), 1)
+
+    def heads_of(values, tail):
+        found = []
+        for h in range(heads):
+            tile = values[:, (h // 2) * LANE : (h // 2 + 1) * LANE]
+            if h % 2:
+                tile = pltpu.roll(tile, 64, 1)
+            found.append(jnp.where(lane < 64, tile, tail).astype(bf16))
+        return found
+
+    def compute(slot, index, part):
+        x = x_buf[slot, pl.ds(part * block, block), :]
+        start = pl.multiple_of(index * tokens + part * block, block)
+        place = start + lax.broadcasted_iota(jnp.int32, (block, LANE), 0)
+        queries = pltpu.roll(dims(x, mats[0], NN), turn, 1) + biases[0]
+        q_tail = jnp.where(lane == 64, 1.0, 0.0)
+        keys = pltpu.roll(dims(x, mats[1], NN), turn, 1)
+        k_tail = jnp.where(
+            lane == 64,
+            jnp.where(place < length, 0.0, -1e9),
+            jnp.where((lane > 64) & (lane < 68), 1.0, 0.0),
+        )
+        values = pltpu.roll(dims(x, mats[2], NN), turn, 1) + biases[1]
+        v_tail = jnp.where((lane >= 64) & (lane < 67), 1.0, 0.0)
+        at = pl.ds(start, block)
+        for ref, found in (
+            (q_ref, heads_of(queries * (LOG2E * 0.125), q_tail)),
+            (k_ref, heads_of(keys, k_tail)),
+            (v_ref, heads_of(values, v_tail)),
+        ):
+            for h in range(heads):
+                ref[h, at, :] = found[h]
+
+    def whole(slot, index):
+        def body(part, carry):
+            compute(slot, index, part)
+            return carry
+
+        lax.fori_loop(0, tokens // block, body, 0)
+
+    whole(0, s)
+    for c in range(early, fine - 1):
+        pass_on(c)
+    near_copy.wait_recv()
+    keep(1, near)
+    whole(1, near)
+    pass_on(fine - 1)
+    keep(2, far)
+    whole(2, far)
+    for c in range(fine):
+        part = pl.ds(c * chunk, chunk)
+        remote(
+            x_buf.at[2, part], x_buf.at[3, part], pass_send.at[c], pass_recv.at[c], seq=near
+        ).wait_recv()
+    keep(3, cross)
+    whole(3, cross)
+    copy = pltpu.make_async_copy(vec_buf, vec_out, local_sem.at[0])
+    copy.start()
+    outs.append(copy)
+    for copy in sends:
+        copy.wait_send()
+    for copy in outs:
+        copy.wait()
+
+
+def project(nf, heads, length, states, wq, wk, wv, vec):
+    tokens, width = states.shape
+    rows = wq.shape[0]
+    pieces = 4
+    window = 256
+    slots = 4 * tokens
+    head_shape = jax.ShapeDtypeStruct((heads, slots, LANE), bf16)
+    return pl.pallas_call(
+        functools.partial(project_kernel, nf, pieces),
+        out_shape=[head_shape] * 3
+        + [
+            jax.ShapeDtypeStruct((4, tokens, width), bf16),
+            jax.ShapeDtypeStruct((nf,) + vec.shape, bf16),
+        ],
+        in_specs=[IN_SMEM] + [ANY] * 5,
+        out_specs=[IN_VMEM] * 3 + [ANY] * 2,
+        scratch_shapes=[
+            pltpu.VMEM((4, tokens, width), bf16),
+            pltpu.VMEM((3, nf, rows, window), bf16),
+            pltpu.VMEM((nf,) + vec.shape, bf16),
+            DMA((5,)),
+            DMA((4,)),
+            DMA((nf - 1,)),
+            DMA((nf - 1,)),
+            DMA((nf - 1, 3)),
+            DMA((nf - 1, 3)),
+            DMA(()),
+            DMA(()),
+            DMA((pieces,)),
+            DMA((pieces,)),
+            DMA((pieces,)),
+            DMA((pieces,)),
+        ],
+        compiler_params=params(1),
+        name="project",
+    )(length, states, wq, wk, wv, vec)
+
+
+def ring_gather(nf, shards, halves, outs, ring_send, ring_recv, pair_send, pair_recv):
+    f = lax.axis_index("fsdp")
+    s, near, _, _ = seq_peers()
+    side = s % 2
+    step = 1 - 2 * side
+    place = place_of(f, nf)
+    ahead = index_at((place + step + nf) % nf, nf)
+    behind = index_at((place - step + nf) % nf, nf)
+
+    def half(ref, w):
+        axis, size = halves[w]
+        cut = pl.ds(pl.multiple_of(side * size, size), size)
+        return ref.at[cut, :] if axis == 0 else ref.at[:, cut]
+
+    def slot(hop):
+        return index_at((place + nf - step * (hop + 1)) % nf, nf)
+
+    def ring(w, hop, owner, source):
+        return remote(
+            half(source, w),
+            half(outs[w].at[owner], w),
+            ring_send.at[w, hop],
+            ring_recv.at[w, hop],
+            fsdp=ahead,
+        )
+
+    def pair(w, hop):
+        piece = half(outs[w].at[slot(hop)], w)
+        return remote(piece, piece, pair_send.at[w, hop], pair_recv.at[w, hop], seq=near)
+
+    def start(w):
+        ring(w, 0, f, shards[w]).start()
+
+    def hop(w, h):
+        owner = slot(h)
+        ring(w, h, owner, outs[w].at[owner]).wait_recv()
+
+        @pl.when(h < nf - 2)
+        def _():
+            ring(w, h + 1, owner, outs[w].at[owner]).start()
+
+        pair(w, h).start()
+
+    def finish(w, h):
+        ring(w, h, f, shards[w]).wait_send()
+        pair(w, h).wait()
+
+    return (ahead, behind), start, hop, finish
+
+
+def attend_kernel(nf, block, key_chunk, gap, halves, *refs):
+    count = len(halves)
+    q_ref, k_ref, v_ref = refs[:3]
+    shards = refs[3 : 3 + count]
+    refs = refs[3 + count :]
+    qb_ref, o_ref, ctx_out = refs[:3]
+    outs = refs[3 : 3 + count]
+    (
+        ctx_buf, ring_send, ring_recv, pair_send, pair_recv, ctx_send, ctx_recv, own_sem, copy_sem,
+    ) = refs[3 + count :]
+    heads, slots, _ = k_ref.shape
+    tokens = slots // 4
+    per = tokens // block
+    f = lax.axis_index("fsdp")
+    s, near, far, cross = seq_peers()
+    neighbours, ring_start, ring_hop, ring_finish = ring_gather(
+        nf, shards, halves, outs, ring_send, ring_recv, pair_send, pair_recv
+    )
+    greet([{"fsdp": i} for i in neighbours] + [{"seq": near}, {"seq": far}, {"seq": cross}])
+    mine = []
+    for w in range(count):
+        ring_start(w)
+        mine.append(pltpu.make_async_copy(shards[w], outs[w].at[f], copy_sem.at[w]))
+        mine[-1].start()
+    lane = lax.broadcasted_iota(jnp.int32, (block, LANE), 1)
+
+    def partner(turn):
+        relation = 3 - turn
+        return ((s // 2 + relation // 2) % 2) * 2 + (s % 2 + relation % 2) % 2
+
+    def ctx_copy(step):
+        turn = step // per
+        part = pl.ds(pl.multiple_of(step % per * block, block), block)
+        return remote(
+            ctx_buf.at[step],
+            ctx_out.at[s, part],
+            ctx_send.at[step],
+            ctx_recv.at[step],
+            seq=partner(turn),
+        )
+
+    def body(step, carry):
+        base = partner(step // per) * tokens + step % per * block
+        at = pl.ds(pl.multiple_of(base, block), block)
+        parts = []
+        for h in range(heads):
+            q = q_ref[h, at, :]
+            scores = []
+            top = None
+            for c in range(slots // key_chunk):
+                scores.append(dims(q, k_ref[h, c * key_chunk : (c + 1) * key_chunk, :], NT))
+                for j in range(key_chunk // LANE):
+                    tile = scores[-1][:, j * LANE : (j + 1) * LANE]
+                    top = tile if top is None else jnp.maximum(top, tile)
+            top = jnp.max(top, axis=1, keepdims=True)
+            total = None
+            for c in range(slots // key_chunk):
+                probs = jnp.exp2(scores[c] - top).astype(bf16)
+                part = dims(probs, v_ref[h, c * key_chunk : (c + 1) * key_chunk, :], NN)
+                total = part if total is None else total + part
+            weight = total[:, 64:65]
+            result = jnp.where(lane < 64, total * (1.0 / weight), 0.0)
+            o_ref[h, at, :] = result.astype(bf16)
+            high, middle, low = thirds(-(top + jnp.log2(weight)))
+            qb_ref[h, at, :] = with_lanes(
+                q.astype(f32), ((65, high), (66, middle), (67, low))
+            ).astype(bf16)
+            parts.append(result)
+        for t in range((heads + 1) // 2):
+            tile = parts[2 * t]
+            if 2 * t + 1 < heads:
+                tile = tile + pltpu.roll(parts[2 * t + 1], 64, 1)
+            ctx_buf[step, :, t * LANE : (t + 1) * LANE] = tile.astype(bf16)
+
+        @pl.when(step < 3 * per)
+        def _():
+            ctx_copy(step).start()
+
+        @pl.when((step % gap == gap - 1) & (step // gap < nf - 1))
+        def _():
+            for w in range(count):
+                ring_hop(w, step // gap)
+
+        return carry
+
+    lax.fori_loop(0, 4 * per, body, 0)
+    owns = []
+    for i in range(per):
+        owns.append(
+            pltpu.make_async_copy(
+                ctx_buf.at[3 * per + i], ctx_out.at[s, pl.ds(i * block, block)], own_sem.at[i]
+            )
+        )
+        owns[-1].start()
+
+    def rest(h, carry):
+        for w in range(count):
+            ring_hop(w, h)
+        return carry
+
+    lax.fori_loop(min(4 * per // gap, nf - 1), nf - 1, rest, 0)
+
+    def settle(step, carry):
+        ctx_copy(step).wait()
+        return carry
+
+    lax.fori_loop(0, 3 * per, settle, 0)
+    for copy in owns + mine:
+        copy.wait()
+
+    def close(h, carry):
+        for w in range(count):
+            ring_finish(w, h)
+        return carry
+
+    lax.fori_loop(0, nf - 1, close, 0)
+
+
+def attend(nf, q, k, v, shards, halves, block, key_chunk, gap):
+    heads, slots, _ = q.shape
+    tokens = slots // 4
+    count = len(shards)
+    ctx_width = -(-heads // 2) * LANE
+    hops = DMA((count, nf - 1))
+    steps = slots // block
+    return pl.pallas_call(
+        functools.partial(attend_kernel, nf, block, key_chunk, gap, halves),
+        out_shape=[jax.ShapeDtypeStruct(q.shape, bf16)] * 2
+        + [jax.ShapeDtypeStruct((4, tokens, ctx_width), bf16)]
+        + [jax.ShapeDtypeStruct((nf,) + w.shape, bf16) for w in shards],
+        in_specs=[IN_VMEM] * (3 + count),
+        out_specs=[IN_VMEM] * 2 + [ANY] * (1 + count),
+        scratch_shapes=[
+            pltpu.VMEM((steps, block, ctx_width), bf16),
+            hops,
+            hops,
+            hops,
+            hops,
+            DMA((steps,)),
+            DMA((steps,)),
+            DMA((tokens // block,)),
+            DMA((count,)),
+        ],
+        compiler_params=params(2),
+        name="attend",
+    )(q, k, v, *shards)
+
+
+def feed_kernel(
+    block, part, length_ref, states, cot, ctx, wout, up, down, vec, upb,
+    out, first_grad_out, gctx, gup, gdn, gout, gvec,
+    act_buf, pre_buf, slope_buf, low_t, down_t, branch_buf, g_buf, g_send, g_recv, own_sem,
+):
+    s, near, far, cross = seq_peers()
+    tokens, width = states.shape
+    hidden = up.shape[1]
+    own = wout.shape[0] // 4
+    steps = tokens // block
+    wide = ctx.shape[2]
+    greet([{"seq": near}, {"seq": far}, {"seq": cross}])
+    length = length_ref[0]
+    gvec[...] = jnp.zeros_like(gvec)
+    peers = (s, near, far, cross)
+
+    def line(row):
+        return vec[row : row + 1, :]
+
+    def add_line(row, values):
+        gvec[row : row + 1, :] += jnp.sum(values, axis=0, keepdims=True)
+
+    def norm(values):
+        centred = values - jnp.mean(values, axis=1, keepdims=True)
+        scale = lax.rsqrt(jnp.mean(centred * centred, axis=1, keepdims=True) + eps)
+        return centred * scale, scale
+
+    def norm_back(grad, gain, normed, scale):
+        grad = grad * gain
+        return scale * (
+            grad
+            - jnp.mean(grad, axis=1, keepdims=True)
+            - normed * jnp.mean(grad * normed, axis=1, keepdims=True)
+        )
+
+    def send(relation, i):
+        at = pl.ds(pl.multiple_of(i * block, block), block)
+        return remote(
+            g_buf.at[relation, at],
+            gctx.at[s, at],
+            g_send.at[relation - 1, i],
+            g_recv.at[relation - 1, i],
+            seq=peers[relation],
+        )
+
+    def body(i, carry):
+        at = pl.ds(pl.multiple_of(i * block, block), block)
+        attended = None
+        for j in range(4):
+            term = dims(ctx[j, at, :own], wout[own * j : own * (j + 1), :], NN)
+            attended = term if attended is None else attended + term
+        normed_first, scale_first = norm(states[at, :].astype(f32) + (attended + line(2)))
+        first = normed_first * line(3) + line(4)
+        low = first.astype(bf16)
+        low_t[:, at] = jnp.transpose(low)
+        fed = None
+        for c in range(hidden // part):
+            cut = slice(c * part, (c + 1) * part)
+            pre = dims(low, up[:, cut], NN) + upb[:, cut]
+            share = 0.5 + 0.5 * lax.erf(pre * (2.0**-0.5))
+            slope_buf[:, cut] = share + pre * jnp.exp(-0.5 * pre * pre) * (2.0 * math.pi) ** -0.5
+            act = (pre * share).astype(bf16)
+            act_buf[at, cut] = act
+            term = dims(act, down[cut, :], NN)
+            fed = term if fed is None else fed + term
+        normed, scale = norm(first + (fed + line(5)))
+        place = s * tokens + i * block + lax.broadcasted_iota(jnp.int32, (block, 1), 0)
+        valid = jnp.where(place < length, 1.0, 0.0)
+        out[at, :] = ((normed * line(6) + line(7)) * valid).astype(bf16)
+        grad = cot[at, :].astype(f32) * valid
+        add_line(6, grad * normed)
+        add_line(7, grad)
+        second_grad = norm_back(grad, line(6), normed, scale)
+        down_in = second_grad.astype(bf16)
+        add_line(5, down_in.astype(f32))
+        down_t[:, at] = jnp.transpose(down_in)
+        back = second_grad
+        for c in range(hidden // part):
+            cut = slice(c * part, (c + 1) * part)
+            pre_grad = (dims(down_in, down[cut, :], NT) * slope_buf[:, cut]).astype(bf16)
+            pre_buf[at, cut] = pre_grad
+            row = 8 + c * part // width
+            col = c * part % width
+            gvec[row : row + 1, col : col + part] += jnp.sum(
+                pre_grad.astype(f32), axis=0, keepdims=True
+            )
+            back = back + dims(pre_grad, up[:, cut], NT)
+        add_line(3, back * normed_first)
+        add_line(4, back)
+        first_grad = norm_back(back, line(3), normed_first, scale_first)
+        first_grad_out[at, :] = first_grad
+        branch = first_grad.astype(bf16)
+        branch_buf[at, :] = branch
+        add_line(2, branch.astype(f32))
+        for relation in range(4):
+            rows = pl.ds(pl.multiple_of(peers[relation] * own, 64), own)
+            g_buf[relation, at, :own] = dims(branch, wout[rows, :], NT).astype(bf16)
+            if wide > own:
+                g_buf[relation, at, own:] = jnp.zeros((block, wide - own), bf16)
+            if relation:
+                send(relation, i).start()
+        return carry
+
+    lax.fori_loop(0, steps, body, 0)
+    mine = pltpu.make_async_copy(g_buf.at[0], gctx.at[s], own_sem)
+    mine.start()
+    for j in range(4):
+        gout[own * j : own * (j + 1), :] = dims(ctx[j, :, :own], branch_buf[...], TN).astype(bf16)
+    cut_size = 512
+
+    def grads(c, carry):
+        cut = pl.ds(pl.multiple_of(c * cut_size, cut_size), cut_size)
+        gup[:, cut] = dims(low_t[...], pre_buf[:, cut], NN).astype(bf16)
+        gdn[:, cut] = dims(down_t[...], act_buf[:, cut], NN).astype(bf16)
+        return carry
+
+    lax.fori_loop(0, hidden // cut_size, grads, 0)
+    for relation in range(1, 4):
+        for i in range(steps):
+            send(relation, i).wait()
+    mine.wait()
+
+
+def feed(length, states, cot, ctx, wout, up, down, vec, upb, block=256, part=768):
+    tokens, width = states.shape
+    hidden = up.shape[1]
+    wide = ctx.shape[2]
+    shape = jax.ShapeDtypeStruct
+    return pl.pallas_call(
+        functools.partial(feed_kernel, block, part),
+        out_shape=[
+            shape((tokens, width), bf16),
+            shape((tokens, width), f32),
+            shape((4, tokens, wide), bf16),
+            shape((width, hidden), bf16),
+            shape((width, hidden), bf16),
+            shape((width, width), bf16),
+            shape((16, width), f32),
+        ],
+        in_specs=[IN_SMEM] + [IN_VMEM] * 8,
+        out_specs=[IN_VMEM] * 2 + [ANY] + [IN_VMEM] * 4,
+        scratch_shapes=[
+            pltpu.VMEM((tokens, hidden), bf16),
+            pltpu.VMEM((tokens, hidden), bf16),
+            pltpu.VMEM((block, hidden), f32),
+            pltpu.VMEM((width, tokens), bf16),
+            pltpu.VMEM((width, tokens), bf16),
+            pltpu.VMEM((tokens, width), bf16),
+            pltpu.VMEM((4, tokens, wide), bf16),
+            DMA((3, tokens // block)),
+            DMA((3, tokens // block)),
+            DMA(()),
+        ],
+        compiler_params=params(3),
+        name="feed",
+    )(length, states, cot, ctx, wout, up, down, vec, upb)
+
+
+def backward_kernel(
+    nf, key_block, gap, q_ref, k_ref, v_ref, o_ref, gctx_ref, gup, gdn, gout,
+    d_out, g_out, up_out, down_out, wout_out,
+    k_t, k_acc, v_acc, own_up, own_dn, own_wo, far_up, far_dn, far_wo,
+    ring_up, ring_dn, ring_wo, send_up, send_dn, send_wo, y_up, y_dn, y_wo, z_up, z_dn, z_wo,
+    load_sem, pair_send, pair_recv, hop_send, hop_recv, y_send, y_recv, z_send, z_recv,
+    d_send, d_recv, d_own,
+):
+    h, i = pl.program_id(0), pl.program_id(1)
+    heads, blocks = pl.num_programs(0), pl.num_programs(1)
+    step = h * blocks + i
+    f = lax.axis_index("fsdp")
+    s, near, far, cross = seq_peers()
+    side = s % 2
+    way = 1 - 2 * side
+    place = place_of(f, nf)
+    ahead = index_at((place + way + nf) % nf, nf)
+    behind = index_at((place - way + nf) % nf, nf)
+    block = q_ref.shape[1]
+    slots = k_ref.shape[1]
+    tokens = slots // 4
+    own = (own_up, own_dn, own_wo)
+    other = (far_up, far_dn, far_wo)
+    came = (ring_up, ring_dn, ring_wo)
+    goes = (send_up, send_dn, send_wo)
+    y_buf = (y_up, y_dn, y_wo)
+    z_buf = (z_up, z_dn, z_wo)
+    full = (gup, gdn, gout)
+    by_rows = (False, True, False)
+
+    def half(w, which):
+        if by_rows[w]:
+            size = full[w].shape[0] // 2
+            return full[w].at[pl.ds(pl.multiple_of(which * size, size), size), :]
+        size = full[w].shape[1] // 2
+        return full[w].at[:, pl.ds(pl.multiple_of(which * size, size), size)]
+
+    def load(w):
+        return pltpu.make_async_copy(half(w, side), own[w], load_sem.at[w])
+
+    def pair(w):
+        return remote(half(w, 1 - side), other[w], pair_send.at[w], pair_recv.at[w], seq=near)
+
+    def summed(w, chunk):
+        if by_rows[w]:
+            size = goes[w].shape[2]
+            at = (slice(None), pl.ds(pl.multiple_of(chunk * size, size), size))
+        else:
+            size = goes[w].shape[1]
+            at = (pl.ds(pl.multiple_of(chunk * size, size), size), slice(None))
+        return own[w][at].astype(f32) + other[w][at].astype(f32)
+
+    def hop(w, t):
+        return remote(goes[w].at[t], came[w].at[t], hop_send.at[w, t], hop_recv.at[w, t], fsdp=ahead)
+
+    def to_far(w):
+        return remote(goes[w].at[nf - 1], y_buf[w], y_send.at[w], y_recv.at[w], seq=far)
+
+    def to_near(w):
+        return remote(goes[w].at[0], z_buf[w], z_send.at[w], z_recv.at[w], seq=near)
+
+    @pl.when(step == 0)
+    def _():
+        greet(
+            [{"fsdp": ahead}, {"fsdp": behind}, {"seq": near}, {"seq": far}, {"seq": cross}]
+        )
+        for w in range(3):
+            pair(w).start()
+            load(w).start()
+
+    @pl.when(i == 0)
+    def _():
+        k_acc[...] = jnp.zeros_like(k_acc)
+        v_acc[...] = jnp.zeros_like(v_acc)
+        k_t[...] = jnp.transpose(k_ref[0])[:64, :]
+
+    lane = lax.broadcasted_iota(jnp.int32, (block, LANE), 1)
+    first = gctx_ref[:, :LANE].astype(f32)
+    second = gctx_ref[:, LANE:].astype(f32)
+    grad = jnp.where(h == 0, first, jnp.where(h == 1, pltpu.roll(first, 64, 1), second))
+    grad = jnp.where(lane < 64, grad, 0.0)
+    delta = jnp.sum(grad * o_ref[0].astype(f32), axis=1, keepdims=True)
+    high, middle, low = thirds(-delta)
+    grad = with_lanes(grad, ((64, high), (65, middle), (66, low))).astype(bf16)
+    q = q_ref[0]
+    q_total = None
+    for c in range(slots // key_block):
+        ks = slice(c * key_block, (c + 1) * key_block)
+        probs = jnp.exp2(dims(k_ref[0, ks, :], q, NT))
+        score = (probs * dims(v_ref[0, ks, :], grad, NT)).astype(bf16)
+        v_acc[ks, :] += dims(probs.astype(bf16), grad, NN)
+        k_acc[ks, :] += dims(score, q, NN)
+        term = dims(k_t[:, ks], score, NN)
+        q_total = term if q_total is None else q_total + term
+    at_head = pl.ds(pl.multiple_of(h * 64, 64), 64)
+    d_out[0, at_head, pl.ds(pl.multiple_of(i * block, block), block)] = (q_total * 0.125).astype(bf16)
+
+    peers = (s, near, far, cross)
+    width_own = heads * 64
+
+    def part(relation, m):
+        to = peers[relation]
+        source = d_out.at[m, at_head, pl.ds(pl.multiple_of(to * tokens, tokens), tokens)]
+        target = g_out.at[m, pl.ds(pl.multiple_of(s * width_own + h * 64, 64), 64), :]
+        return source, target
+
+    def d_copy(relation, m):
+        source, target = part(relation, m)
+        return remote(
+            source, target, d_send.at[relation - 1, m, h], d_recv.at[relation - 1, m, h],
+            seq=peers[relation],
+        )
+
+    @pl.when(i == blocks - 1)
+    def _():
+        d_out[1, at_head, :] = jnp.transpose((k_acc[...] * LN2).astype(bf16))[:64, :]
+        d_out[2, at_head, :] = jnp.transpose(v_acc[...].astype(bf16))[:64, :]
+        for m in range(3):
+            for relation in (3, 2, 1):
+                d_copy(relation, m).start()
+            source, target = part(0, m)
+            pltpu.make_async_copy(source, target, d_own.at[m, h]).start()
+
+    @pl.when(step == gap)
+    def _():
+        for w in range(3):
+            load(w).wait()
+            pair(w).wait_recv()
+            goes[w][0] = summed(w, index_at((place + nf - way) % nf, nf)).astype(bf16)
+            hop(w, 0).start()
+
+    turn = step // gap - 1
+
+    @pl.when((step % gap == 0) & (turn > 0) & (turn < nf - 1))
+    def _():
+        for w in range(3):
+            hop(w, turn - 1).wait_recv()
+            chunk = index_at((place + 2 * nf - way * (1 + turn)) % nf, nf)
+            goes[w][turn] = (summed(w, chunk) + came[w][turn - 1].astype(f32)).astype(bf16)
+            hop(w, turn).start()
+
+    @pl.when(step == nf * gap)
+    def _():
+        for w in range(3):
+            hop(w, nf - 2).wait_recv()
+            goes[w][nf - 1] = (summed(w, f) + came[w][nf - 2].astype(f32)).astype(bf16)
+            to_far(w).start()
+
+    @pl.when(step == heads * blocks - 1)
+    def _():
+        for w in range(3):
+            to_far(w).wait()
+            hop(w, 0).wait_send()
+            goes[w][0] = (goes[w][nf - 1].astype(f32) + y_buf[w][...].astype(f32)).astype(bf16)
+            to_near(w).start()
+        for w in range(3):
+            pair(w).wait_send()
+            for t in range(1, nf - 1):
+                hop(w, t).wait_send()
+            to_near(w).wait()
+            mine = goes[w][0].astype(f32)
+            theirs = z_buf[w][...].astype(f32)
+            out = (up_out, down_out, wout_out)[w]
+            size = out.shape[1] // 2
+            if by_rows[w]:
+                mine, theirs = jnp.transpose(mine), jnp.transpose(theirs)
+            out[:, pl.ds(pl.multiple_of(side * size, size), size)] = mine
+            out[:, pl.ds(pl.multiple_of((1 - side) * size, size), size)] = theirs
+
+        def settle(head, carry):
+            for m in range(3):
+                for relation in range(1, 4):
+                    source, target = part(relation, m)
+                    remote(
+                        source, target, d_send.at[relation - 1, m, head],
+                        d_recv.at[relation - 1, m, head], seq=peers[relation],
+                    ).wait()
+                source, target = part(0, m)
+                pltpu.make_async_copy(source, target, d_own.at[m, head]).wait()
+            return carry
+
+        lax.fori_loop(0, heads, settle, 0)
+
+
+def backward(nf, qb, k, v, o, gctx, gup, gdn, gout, block, key_block, gap):
+    heads, slots, _ = qb.shape
+    tokens = slots // 4
+    width, hidden = gup.shape
+    rows, cols = width // nf, hidden // nf
+    shape = jax.ShapeDtypeStruct
+    per_block = pl.BlockSpec((1, block, LANE), lambda h, i: (h, i, 0))
+    per_head = pl.BlockSpec((1, slots, LANE), lambda h, i: (h, 0, 0))
+    fixed = lambda n: (lambda h, i: (0,) * n)
+    chunk = ((rows, hidden // 2), (width // 2, cols), (rows, width // 2))
+    halves = ((width, hidden // 2), (width // 2, hidden), (width, width // 2))
+    vmem = lambda *dims_: pltpu.VMEM(dims_, bf16)
+    pairs = DMA((3,))
+    hops = DMA((3, nf - 1))
+    return pl.pallas_call(
+        functools.partial(backward_kernel, nf, key_block, gap),
+        grid=(heads, slots // block),
+        out_shape=[
+            shape((3, heads * 64, slots), bf16),
+            shape((3, width, tokens), bf16),
+            shape((rows, hidden), f32),
+            shape((cols, width), f32),
+            shape((rows, width), f32),
+        ],
+        in_specs=[
+            per_block,
+            per_head,
+            per_head,
+            per_block,
+            pl.BlockSpec((block, gctx.shape[1]), lambda h, i: (i, 0)),
+        ]
+        + [ANY] * 3,
+        out_specs=[
+            pl.BlockSpec((3, heads * 64, slots), fixed(3)),
+            ANY,
+            pl.BlockSpec((rows, hidden), fixed(2)),
+            pl.BlockSpec((cols, width), fixed(2)),
+            pl.BlockSpec((rows, width), fixed(2)),
+        ],
+        scratch_shapes=[
+            pltpu.VMEM((64, slots), bf16),
+            pltpu.VMEM((slots, LANE), f32),
+            pltpu.VMEM((slots, LANE), f32),
+        ]
+        + [vmem(*x) for x in halves]
+        + [vmem(*x) for x in halves]
+        + [vmem(nf - 1, *x) for x in chunk]
+        + [vmem(nf, *x) for x in chunk]
+        + [vmem(*x) for x in chunk]
+        + [vmem(*x) for x in chunk]
+        + [pairs, pairs, pairs, hops, hops, pairs, pairs, pairs, pairs]
+        + [DMA((3, 3, heads)), DMA((3, 3, heads)), DMA((3, heads))],
+        compiler_params=params(4),
+        name="backward",
+    )(qb, k, v, o, gctx, gup, gdn, gout)
+
+
+def last_kernel(
+    nf, x_all, d_own, g_all, wq, wk, wv, first_grad, gvec,
+    states_grad, q_out, k_out, v_out, vec_out, upb_out,
+    w_buf, w_came, w_sum, w_parts, v_own, v_came, v_sum, v_parts,
+    w_send, w_recv, p_send, p_recv, l_send, l_recv, m_send, m_recv,
+):
+    f = lax.axis_index("fsdp")
+    s, near, far, cross = seq_peers()
+    peers = (s, near, far, cross)
+    tokens, width = first_grad.shape
+    own = d_own.shape[1]
+    rows = width // nf
+    greet(
+        [{"fsdp": (f + d) % nf} for d in range(1, nf)]
+        + [{"seq": near}, {"seq": far}, {"seq": cross}]
+    )
+    ones = jnp.ones((8, tokens), bf16)
+    v_own[...] = gvec[...]
+    v_own[0:1, :] = dims(ones, g_all[0], NT)[0:1, :]
+    v_own[1:2, :] = dims(ones, g_all[2], NT)[0:1, :]
+
+    def v_copy(d, to):
+        return remote(v_own, v_came.at[d], l_send.at[d - 1], l_recv.at[d - 1], fsdp=to)
+
+    def w_copy(d, to):
+        at = pl.ds(pl.multiple_of(to * rows, rows), rows)
+        return remote(w_buf.at[at], w_came.at[d], w_send.at[d - 1], w_recv.at[d - 1], fsdp=to)
+
+    for d in range(1, nf):
+        v_copy(d, (f + d) % nf).start()
+    for m in range(3):
+        total = None
+        for j in range(4):
+            term = dims(d_own[m, :, j * tokens : (j + 1) * tokens], x_all[j], NN)
+            total = term if total is None else total + term
+        w_buf[:, m * own : (m + 1) * own] = jnp.transpose(total).astype(bf16)
+    for d in range(1, nf):
+        w_copy(d, (f + d) % nf).start()
+    block = 256
+    for c in range(width // block):
+        cut = slice(c * block, (c + 1) * block)
+        total = None
+        for w, m in ((wq, 0), (wk, 1), (wv, 2)):
+            term = dims(w[cut, :], g_all[m], NN)
+            total = term if total is None else total + term
+        states_grad[:, cut] = (first_grad[:, cut] + jnp.transpose(total)).astype(bf16)
+    for d in range(1, nf):
+        v_copy(d, (f + d) % nf).wait()
+    v_came[0] = v_own[...]
+    total = None
+    for j in range(nf):
+        term = v_came[(f + nf - j) % nf]
+        total = term if total is None else total + term
+    v_sum[...] = total
+
+    def m_copy(relation):
+        return remote(
+            v_sum, v_parts.at[s], m_send.at[relation - 1], m_recv.at[relation - 1],
+            seq=peers[relation],
+        )
+
+    for relation in range(1, 4):
+        m_copy(relation).start()
+    v_parts[s] = total
+    for d in range(1, nf):
+        w_copy(d, (f + d) % nf).wait()
+    total = w_buf[pl.ds(pl.multiple_of(f * rows, rows), rows), :].astype(f32)
+    for d in range(1, nf):
+        total = total + w_came[d].astype(f32)
+    w_sum[...] = total.astype(bf16)
+
+    def p_copy(relation):
+        return remote(
+            w_sum, w_parts.at[s], p_send.at[relation - 1], p_recv.at[relation - 1],
+            seq=peers[relation],
+        )
+
+    for relation in range(1, 4):
+        p_copy(relation).start()
+    w_parts[s] = total.astype(bf16)
+    for relation in range(1, 4):
+        m_copy(relation).wait()
+    total = v_parts[0] + v_parts[1] + v_parts[2] + v_parts[3]
+    mine = pltpu.roll(total, (width - rows * f) % width, 1)
+    vec_out[...] = mine[:, :LANE]
+    cols = 4 * rows
+    lead = f * cols // width
+    line = jnp.zeros((1, width), f32)
+    for r in range(4):
+        line = jnp.where(lead == r, total[8 + r : 9 + r, :], line)
+    line = jnp.broadcast_to(line, (8, width))
+    upb_out[...] = pltpu.roll(line, (width - f * cols % width) % width, 1)[:, :cols]
+    for relation in range(1, 4):
+        p_copy(relation).wait()
+    for m, out in enumerate((q_out, k_out, v_out)):
+        out[...] = jnp.concatenate(
+            [w_parts[j][:, m * own : (m + 1) * own].astype(f32) for j in range(4)], axis=1
+        )
+
+
+def last(nf, x_all, d_own, g_all, wq, wk, wv, first_grad, gvec):
+    tokens, width = first_grad.shape
+    own = d_own.shape[1]
+    rows = width // nf
+    shape = jax.ShapeDtypeStruct
+    peers, others = DMA((nf - 1,)), DMA((3,))
+    return pl.pallas_call(
+        functools.partial(last_kernel, nf),
+        out_shape=[shape((tokens, width), bf16)]
+        + [shape((rows, width), f32)] * 3
+        + [shape((16, LANE), f32), shape((8, 4 * rows), f32)],
+        in_specs=[IN_VMEM] * 8,
+        out_specs=[IN_VMEM] * 6,
+        scratch_shapes=[
+            pltpu.VMEM((width, 3 * own), bf16),
+            pltpu.VMEM((nf, rows, 3 * own), bf16),
+            pltpu.VMEM((rows, 3 * own), bf16),
+            pltpu.VMEM((4, rows, 3 * own), bf16),
+            pltpu.VMEM((16, width), f32),
+            pltpu.VMEM((nf, 16, width), f32),
+            pltpu.VMEM((16, width), f32),
+            pltpu.VMEM((4, 16, width), f32),
+            peers, peers, others, others, peers, peers, others, others,
+        ],
+        compiler_params=params(5),
+        name="last",
+    )(x_all, d_own, g_all, wq, wk, wv, first_grad, gvec)
+
+
+def fused_device(
+    nf, states, query_weight, key_weight, value_weight, out_weight, query_bias, value_bias,
+    out_bias, first_gain, first_shift, up_weight, up_bias, down_weight, down_bias, second_gain,
+    second_shift, lengths, cotangent,
+):
+    tokens, width = states.shape
+    rows = width // nf
+    hidden = up_weight.shape[1]
+    heads = width // 4 // 64
+    lines = jnp.concatenate(
+        [
+            x.reshape(-1, rows)
+            for x in (
+                query_bias, value_bias, out_bias, first_gain, first_shift, down_bias, second_gain,
+                second_shift, up_bias,
+            )
+        ],
+        axis=0,
+    )
+    vec = jnp.pad(lines, ((0, 16 - lines.shape[0]), (0, LANE - rows)))
+    q, k, v, x_all, vec_all = project(
+        nf, heads, lengths, states, query_weight, key_weight, value_weight, vec
+    )
+    shards = (out_weight, up_weight, down_weight, query_weight, key_weight, value_weight)
+    halves = ((1, width // 2), (1, hidden // 2), (1, width // 2)) + ((1, width // 2),) * 3
+    qb, o, ctx, wout, up, down, wq, wk, wv = attend(
+        nf, q, k, v, shards, halves, block=min(256, tokens), key_chunk=1024, gap=2
+    )
+    vec_all = vec_all[:, :, :rows].astype(f32)
+    full = vec_all[:, :8].transpose(1, 0, 2).reshape(8, width)
+    full_up = vec_all[:, 8:12].reshape(1, hidden)
+    output, first_grad, gctx, gup, gdn, gout, gvec = feed(
+        lengths, states, cotangent, ctx, wout.reshape(width, width), up.reshape(width, hidden),
+        down.reshape(hidden, width), full, full_up,
+    )
+    d_own, g_all, up_grad, down_grad, out_grad = backward(
+        nf, qb, k, v, o, gctx.reshape(4 * tokens, -1), gup, gdn, gout,
+        block=min(512, tokens), key_block=512, gap=2,
+    )
+    square = lambda w: w.reshape(width, width)
+    states_grad, q_grad, k_grad, v_grad, vec_grad, upb_grad = last(
+        nf, x_all, d_own, g_all, square(wq), square(wk), square(wv), first_grad, gvec
+    )
+    line = lambda r: vec_grad[r, :rows]
+    return (
+        output, states_grad, q_grad, k_grad, v_grad, out_grad, line(0), line(1), line(2), line(3),
+        line(4), up_grad, upb_grad[0], down_grad, line(5), line(6), line(7),
+    )
+
+
 def solution(mesh):
+    nf, ns = mesh.shape["fsdp"], mesh.shape["seq"]
+
+    def choose(states, query_weight, *rest):
+        rows, width = query_weight.shape
+        fits = ns == 4 and nf % 2 == 0 and rows % 16 == 0 and width == 768 and states.shape[0] % 768 == 0
+        device = functools.partial(fused_device, nf) if fits else per_device
+        return device(states, query_weight, *rest)
+
     return jax.shard_map(
-        per_device,
+        choose,
         mesh=mesh,
         in_specs=(
             P(("fsdp", "seq"), None),

time: 1490 us -> 349 us (0.23)
  waiting for transfers between devices: 540 us -> 0 us
  matrix products: 417 us -> 0 us
  Pallas kernels: 0 us -> 325 us
  other arithmetic: 188 us -> 0.76 us
  blocking collectives: 163 us -> 0 us
  local copies, waits for them, and re-layouts: 130 us -> 14.8 us
  starting transfers between devices: 20.7 us -> 0 us
  between operations: 17.8 us -> 1.39 us
    dot_general x60 -> x0, matrix products: 417 us -> none  [the longest x6 79.6 us: backward_step(): jnp.einsum('qhd,khd->hqk', grad_block, values_heads, preferred_element_ty...]
    reduce_scatter x3 -> x0, waiting for transfers between devices: 328 us -> none  [the longest x1 164 us: per_device(): lax.psum_scatter(up_weight_grad, 'fsdp', scatter_dimension=0, tiled=True)]
    pallas_call x0 -> x5, Pallas kernels: none -> 325 us  [the longest x1 112 us: backward(): pl.pallas_call(functools.partial(backward_kernel, nf, key_block, gap), gr...]
    unnamed x16 -> x0, waiting for transfers between devices: 129 us -> none
    convert_element_type x33 -> x1, other arithmetic: 101 us -> 0.76 us  [fused_device(): vec_all = vec_all[:, :, :rows].astype(f32)]
    reduce_sum x14 -> x0, other arithmetic: 75.7 us -> none  [the longest x6 66.1 us: forward_block(): totals = jnp.sum(exponent, axis=-1, keepdims=True)]
    unnamed x2 -> x0, blocking collectives: 75.5 us -> none
    all_gather x6 -> x0, waiting for transfers between devices: 65 us -> none  [the longest x1 35.1 us: per_device(): lax.all_gather(key_weight, 'fsdp', axis=0, tiled=True)]
  transfers between devices with their start and end apart: 18 -> 0, of which waited for: 8 -> 0; matrix products, arithmetic and copies ran while one was open for 42% -> 0% of each run, Pallas kernels for 0% -> 0%
where the time goes in v1:
time: 349 us; the launch traced here: 342 us
  Pallas kernels  325 us (93%)
  local copies, waits for them, and re-layouts  14.8 us (4%)
    pallas_call x1, Pallas kernels, backward(): pl.pallas_call(functools.partial(backward_kernel, nf, key_block, gap), gr...  112 us
    pallas_call x1, Pallas kernels, attend(): pl.pallas_call(functools.partial(attend_kernel, nf, block, key_chunk, gap...  84.1 us
    pallas_call x1, Pallas kernels, feed(): pl.pallas_call(functools.partial(feed_kernel, block, part), out_shape=[sh...  46.9 us
    pallas_call x1, Pallas kernels, project(): pl.pallas_call(functools.partial(project_kernel, nf, pieces), out_shape=[...  41.1 us
    pallas_call x1, Pallas kernels, last(): pl.pallas_call(functools.partial(last_kernel, nf), out_shape=[shape((toke...  40.7 us
    unnamed x22, local copies, waits for them, and re-layouts  8.32 us

profile of v1, /device:TPU:0, one launch (start us, length us, event | category | flops | bytes accessed | tf_op | source)
XLA Modules:
  0.0 342.1 jit_solution(17405226683763492058)
XLA Ops:
  1.3 0.8 reshape.96
  2.1 0.8 concatenate.3
  2.9 0.6 pad.4.vec
  3.5 41.1 %project.1 = (bf16[3,3072,128]{2,1,0:T(8,128)(2,1)}, bf16[3,3072,128]{2,1,0:T(8,128)(2,1)}, bf16[3,3072,128]{2,1,0:T(8,128)(2,1)}, bf16[4,768,768]{2,1,0:T(8,128)(2,1)}, bf16[8,16,128]{2,1,0:T(8,128)(2,1)}) custom-call(s32[1]{0:T(128)S(6)} %copy.44.length_ref, bf16[768,768]{1,0:T(8,128)(2,1)} %states.3, bf16[96,768]{1,0:T(8,128)(2,1)} %refs_6_.1, ...), custom_call_target="tpu_custom_call" | custom-call | tf_op jit(solution)/shard_map/project/pallas_call | solution.py:556
  44.6 0.8 slice_convert_fusion
  45.4 0.7 reshape.101.upb
  46.1 0.7 reshape.100.vec
  46.8 84.1 %attend.1 = (bf16[3,3072,128]{2,1,0:T(8,128)(2,1)}, bf16[3,3072,128]{2,1,0:T(8,128)(2,1)}, bf16[4,768,256]{2,1,0:T(8,128)(2,1)}, bf16[8,96,768]{2,1,0:T(8,128)(2...) custom-call(bf16[3,3072,128]{2,1,0:T(8,128)(2,1)} %get-tuple-element, ...), custom_call_target="tpu_custom_call" | custom-call | tf_op jit(solution)/shard_map/attend/pallas_call | solution.py:762
  130.9 46.9 %feed.1 = (bf16[768,768]{1,0:T(8,128)(2,1)}, f32[768,768]{1,0:T(8,128)}, bf16[4,768,256]{2,1,0:T(8,128)(2,1)}, bf16[768,3072]{1,0:T(8,128)(2,1)}, bf16[768,3072]...) custom-call(s32[1]{0:T(128)S(6)} %copy.44.length_ref, bf16[768,768]{1,0:T(8,128)(2,1)} %states.3, ...), custom_call_target="tpu_custom_call" | custom-call | tf_op jit(solution)/shard_map/feed/pallas_call | solution.py:913
  177.9 112.2 %backward.1 = (bf16[3,192,3072]{2,1,0:T(8,128)(2,1)}, bf16[3,768,768]{2,1,0:T(8,128)(2,1)}, f32[96,3072]{1,0:T(8,128)}, f32[384,768]{1,0:T(8,128)}, f32[96,768]{1,0:T(8,128)}) custom-call(bf16[3,3072,128]{2,1,0:T(8,128)(2,1)} %get-tuple-element.59.q_ref, bf16[3,3072,128]{2,1,0:T(8,128)(2,1)} %get-tuple-element.50.refs_1_.k_ref, ...), custom_call_target="tpu_custom_call" | custom-call | tf_op jit(solution)/shard_map/backward/pallas_call | solution.py:1141
  290.1 40.7 %last.1 = (bf16[768,768]{1,0:T(8,128)(2,1)}, f32[96,768]{1,0:T(8,128)}, f32[96,768]{1,0:T(8,128)}, f32[96,768]{1,0:T(8,128)}, f32[16,128]{1,0:T(8,128)}, /*index=5*/f32[8,384]{1,0:T(8,128)}) custom-call(bf16[4,768,768]{2,1,0:T(8,128)(2,1)} %get-tuple-element.58.x_all, bf16[3,192,3072]{2,1,0:T(8,128)(2,1)} %get-tuple-element.65.d_own, ...), custom_call_target="tpu_custom_call" | custom-call | tf_op jit(solution)/shard_map/last/pallas_call | solution.py:1290
  330.8 1.4 slice_reduce_fusion
  332.2 1.5 slice_bitcast_fusion.1
  333.7 2.4 copy.45
  336.1 0.0 copy-start.3
  336.1 1.0 copy.46
  337.1 0.0 copy-done.6
  337.2 0.7 copy.47
  337.9 0.7 copy.48
  338.6 0.7 copy.49
  339.3 0.7 copy.50
  340.0 0.0 copy-done.1
  340.0 1.0 copy.51
  341.1 1.0 copy.52
  (14 shorter events, 0.0 us)
Async XLA Ops:
  330.8 5.3 %copy-start.2 = (bf16[768,768]{1,0:T(8,128)(2,1)S(1)}, bf16[768,768]{1,0:T(8,128)(2,1)}, u32[]{:S(2)}) copy-start(bf16[768,768]{1,0:T(8,128)(2,1)} %get-tuple-element.107) | copy-start | bytes 3538948
  336.1 1.1 copy-start.6
  336.1 1.8 copy-start.5
  336.1 2.5 copy-start.4
  336.1 3.2 copy-start.3
  337.2 2.9 copy-start.1
  339.3 1.7 copy-start

commit v2 on v0

--- a/solution.py
+++ b/solution.py
@@ -1,6 +1,11 @@
+import functools
+import math
+
 import jax
 import jax.numpy as jnp
 from jax import lax
+from jax.experimental import pallas as pl
+from jax.experimental.pallas import tpu as pltpu
 from jax.sharding import PartitionSpec as P
 
 HEAD_DIM = 64
@@ -288,9 +293,1301 @@
     )
 
 
+LANE = 128
+LOG2E = math.log2(math.e)
+LN2 = math.log(2.0)
+NT = (((1,), (1,)), ((), ()))
+NN = (((1,), (0,)), ((), ()))
+TN = (((0,), (0,)), ((), ()))
+VMEM_BYTES = 66 * 1024 * 1024 - 2 * 1024 * 1024
+f32 = jnp.float32
+bf16 = jnp.bfloat16
+ANY = pl.BlockSpec(memory_space=pl.ANY)
+IN_VMEM = pl.BlockSpec(memory_space=pltpu.VMEM)
+IN_SMEM = pl.BlockSpec(memory_space=pltpu.SMEM)
+DMA = pltpu.SemaphoreType.DMA
+
+
+def dims(left, right, numbers):
+    return lax.dot_general(left, right, numbers, preferred_element_type=f32)
+
+
+def remote(src, dst, send_sem, recv_sem, **where):
+    return pltpu.make_async_remote_copy(
+        src_ref=src,
+        dst_ref=dst,
+        send_sem=send_sem,
+        recv_sem=recv_sem,
+        device_id=where,
+        device_id_type=pl.DeviceIdType.MESH,
+    )
+
+
+def greet(partners):
+    barrier = pltpu.get_barrier_semaphore()
+    for where in partners:
+        pl.semaphore_signal(barrier, inc=1, device_id=where, device_id_type=pl.DeviceIdType.MESH)
+    pl.semaphore_wait(barrier, len(partners))
+
+
+def seq_peers():
+    me = lax.axis_index("seq")
+    across = (me + 2) % 4
+    return me, me + 1 - 2 * (me % 2), across, across + 1 - 2 * (across % 2)
+
+
+def place_of(index, count):
+    half = index // 2
+    return half + (index % 2) * (count - 1 - 2 * half)
+
+
+def index_at(place, count):
+    upper = place // (count // 2)
+    return (1 - upper) * 2 * place + upper * (2 * (count - 1 - place) + 1)
+
+
+def thirds(values):
+    high = values.astype(bf16)
+    rest = values - high.astype(f32)
+    middle = rest.astype(bf16)
+    low = (rest - middle.astype(f32)).astype(bf16)
+    return high.astype(f32), middle.astype(f32), low.astype(f32)
+
+
+def with_lanes(base, columns):
+    lane = lax.broadcasted_iota(jnp.int32, base.shape, 1)
+    for place, values in columns:
+        base = jnp.where(lane == place, values, base)
+    return base
+
+
+def params(collective_id=None):
+    if collective_id is None:
+        return pltpu.CompilerParams(vmem_limit_bytes=VMEM_BYTES)
+    return pltpu.CompilerParams(
+        vmem_limit_bytes=VMEM_BYTES, collective_id=collective_id, has_side_effects=True
+    )
+
+
+def ring_gather(nf, shards, halves, outs, ring_send, ring_recv, pair_send, pair_recv):
+    f = lax.axis_index("fsdp")
+    s, near, _, _ = seq_peers()
+    side = s % 2
+    step = 1 - 2 * side
+    place = place_of(f, nf)
+    ahead = index_at((place + step + nf) % nf, nf)
+
+    def half(ref, w):
+        axis, size = halves[w]
+        cut = pl.ds(pl.multiple_of(side * size, size), size)
+        return ref.at[cut, :] if axis == 0 else ref.at[:, cut]
+
+    def slot(hop):
+        return index_at((place + nf - step * (hop + 1)) % nf, nf)
+
+    def ring(w, hop, owner, source):
+        return remote(
+            half(source, w),
+            half(outs[w].at[owner], w),
+            ring_send.at[w, hop],
+            ring_recv.at[w, hop],
+            fsdp=ahead,
+        )
+
+    def pair(w, hop):
+        piece = half(outs[w].at[slot(hop)], w)
+        return remote(piece, piece, pair_send.at[w, hop], pair_recv.at[w, hop], seq=near)
+
+    def start(w):
+        ring(w, 0, f, shards[w]).start()
+
+    def hop(w, h):
+        owner = slot(h)
+        ring(w, h, owner, outs[w].at[owner]).wait_recv()
+
+        @pl.when(h < nf - 2)
+        def _():
+            ring(w, h + 1, owner, outs[w].at[owner]).start()
+
+        pair(w, h).start()
+
+    def finish(w, h):
+        ring(w, h, f, shards[w]).wait_send()
+        pair(w, h).wait()
+
+    return start, hop, finish
+
+
+def front_kernel(
+    nf, block, key_chunk, halves, groups,
+    length_ref, states, wq, wk, wv, vec, wout_s, up_s, down_s,
+    qb_out, o_out, k_out, v_out, x_out, vec_out, ctx_out, wout, up, down,
+    q_buf, k_buf, v_buf, qb_buf, o_buf, ctx_buf, x_buf, w_buf, vec_buf,
+    local_sem, x_sem, kv_sem, keep_sem, vec_send, vec_recv, z_send, z_recv, h_send, h_recv,
+    near_send, near_recv, far_send, far_recv, pass_send, pass_recv,
+    ring_send, ring_recv, pair_send, pair_recv, ctx_send, ctx_recv, own_sem, copy_sem,
+):
+    f = lax.axis_index("fsdp")
+    s, near, far, cross = seq_peers()
+    tokens, width = states.shape
+    heads, slots, _ = q_buf.shape
+    rows = wq.shape[0]
+    window = w_buf.shape[3]
+    own_width = heads * 64
+    parts = far_send.shape[0]
+    chunk = tokens // parts
+    per = tokens // block
+    beside = f + 1 - 2 * (f % 2)
+    stages = nf // 2
+    first_lane = pl.multiple_of((own_width * s // LANE) * LANE, LANE)
+    weights = (wq, wk, wv)
+    shards, outs = (wout_s, up_s, down_s), (wout, up, down)
+    ring_start, ring_hop, ring_finish = ring_gather(
+        nf, shards, halves, outs, ring_send, ring_recv, pair_send, pair_recv
+    )
+    greet(
+        [{"fsdp": (f + d) % nf} for d in range(1, nf)]
+        + [{"seq": near}, {"seq": far}, {"seq": cross}]
+    )
+
+    def windowed(m):
+        return weights[m].at[:, pl.ds(first_lane, window)]
+
+    def along(d, m):
+        to = (f + 2 * d) % nf
+        return remote(windowed(m), w_buf.at[m, f], z_send.at[d - 1, m], z_recv.at[d - 1, m], fsdp=to)
+
+    def aside(d, m):
+        owner = (f + nf - 2 * d) % nf
+        source = w_buf.at[m, owner] if d else windowed(m)
+        return remote(source, w_buf.at[m, owner], h_send.at[d, m], h_recv.at[d, m], fsdp=beside)
+
+    def vec_copy(d):
+        return remote(vec, vec_buf.at[f], vec_send.at[d - 1], vec_recv.at[d - 1], fsdp=(f + d) % nf)
+
+    def far_copy(c):
+        at = pl.ds(c * chunk, chunk)
+        return remote(states.at[at], x_buf.at[2, at], far_send.at[c], far_recv.at[c], seq=far)
+
+    def pass_copy(c):
+        at = pl.ds(c * chunk, chunk)
+        return remote(
+            x_buf.at[2, at], x_buf.at[3, at], pass_send.at[c], pass_recv.at[c], seq=near
+        )
+
+    near_copy = remote(states, x_buf.at[1], near_send, near_recv, seq=near)
+    for d in range(1, stages):
+        for m in range(3):
+            along(d, m).start()
+    for m in range(3):
+        aside(0, m).start()
+    for c in range(parts):
+        far_copy(c).start()
+    near_copy.start()
+    for d in range(1, nf):
+        vec_copy(d).start()
+    local = [
+        pltpu.make_async_copy(states, x_buf.at[0], local_sem.at[0]),
+        pltpu.make_async_copy(vec, vec_buf.at[f], local_sem.at[1]),
+    ]
+    for m in range(3):
+        local.append(pltpu.make_async_copy(windowed(m), w_buf.at[m, f], local_sem.at[2 + m]))
+    mine = [
+        pltpu.make_async_copy(shards[w], outs[w].at[f], copy_sem.at[w]) for w in range(len(shards))
+    ]
+    for copy in local + mine:
+        copy.start()
+    for copy in local:
+        copy.wait()
+    kept = []
+
+    def keep(slot, index):
+        copy = pltpu.make_async_copy(x_buf.at[slot], x_out.at[index], x_sem.at[slot])
+        copy.start()
+        kept.append(copy)
+
+    def pass_on(c):
+        far_copy(c).wait_recv()
+        pass_copy(c).start()
+
+    def turn_aside(d):
+        for m in range(3):
+            along(d, m).wait_recv()
+            aside(d, m).start()
+
+    keep(0, s)
+    passed = 0
+    for d in range(1, stages):
+        turn_aside(d)
+        if d != 2 and passed < parts - 2:
+            pass_on(passed)
+            passed += 1
+    for w in range(len(shards)):
+        ring_start(w)
+    for d in range(1, nf):
+        vec_copy(d).wait_recv()
+    for d in range(stages):
+        for m in range(3):
+            aside(d, m).wait_recv()
+
+    turn = (window - (own_width * s) % LANE) % window
+    share = own_width // rows
+    wide = lax.broadcasted_iota(jnp.int32, (1, window), 1)
+    biases = []
+    for row in (0, 1):
+        line = jnp.zeros((1, window), f32)
+        for i in range(share):
+            piece = vec_buf[share * s + i][row : row + 1, :].astype(f32)
+            piece = jnp.concatenate([piece, jnp.zeros((1, window - LANE), f32)], axis=1)
+            if i:
+                piece = pltpu.roll(piece, i * rows, 1)
+            line = jnp.where((wide >= i * rows) & (wide < (i + 1) * rows), piece, line)
+        biases.append(line)
+    length = length_ref[0]
+    mats = [w_buf[m].reshape(nf * rows, window) for m in range(3)]
+    small = lax.broadcasted_iota(jnp.int32, (chunk, LANE), 1)
+    q_tail = jnp.where(small == 64, 1.0, 0.0)
+    v_tail = jnp.where((small >= 64) & (small < 67), 1.0, 0.0)
+
+    def heads_of(values, tail):
+        found = []
+        for h in range(heads):
+            tile = values[:, (h // 2) * LANE : (h // 2 + 1) * LANE]
+            if h % 2:
+                tile = pltpu.roll(tile, 64, 1)
+            found.append(jnp.where(small < 64, tile, tail).astype(bf16))
+        return found
+
+    def compute(slot, index, part):
+        x = x_buf[slot, pl.ds(pl.multiple_of(part * chunk, chunk), chunk), :]
+        start = pl.multiple_of(index * tokens + part * chunk, chunk)
+        where = start + lax.broadcasted_iota(jnp.int32, (chunk, LANE), 0)
+        queries = pltpu.roll(dims(x, mats[0], NN), turn, 1) + biases[0]
+        keys = pltpu.roll(dims(x, mats[1], NN), turn, 1)
+        k_tail = jnp.where(
+            small == 64,
+            jnp.where(where < length, 0.0, -1e9),
+            jnp.where((small > 64) & (small < 68), 1.0, 0.0),
+        )
+        values = pltpu.roll(dims(x, mats[2], NN), turn, 1) + biases[1]
+        at = pl.ds(start, chunk)
+        for ref, found in (
+            (q_buf, heads_of(queries * (LOG2E * 0.125), q_tail)),
+            (k_buf, heads_of(keys, k_tail)),
+            (v_buf, heads_of(values, v_tail)),
+        ):
+            for h in range(heads):
+                ref[h, at, :] = found[h]
+
+    def whole(slot, index, low, high):
+        def body(part, carry):
+            compute(slot, index, part)
+            return carry
+
+        lax.fori_loop(low, high, body, 0)
+
+    whole(0, s, 0, parts)
+    for c in range(passed, parts - 1):
+        pass_on(c)
+    near_copy.wait_recv()
+    keep(1, near)
+    whole(1, near, 0, parts)
+    for w in range(len(shards)):
+        ring_hop(w, 0)
+    whole(2, far, 0, parts - 1)
+    pass_on(parts - 1)
+    whole(2, far, parts - 1, parts)
+    keep(2, far)
+    for c in range(parts):
+        pass_copy(c).wait_recv()
+    keep(3, cross)
+    whole(3, cross, 0, parts)
+    saved = [
+        pltpu.make_async_copy(k_buf, k_out, kv_sem.at[0]),
+        pltpu.make_async_copy(v_buf, v_out, kv_sem.at[1]),
+        pltpu.make_async_copy(vec_buf, vec_out, kv_sem.at[2]),
+    ]
+    for copy in saved:
+        copy.start()
+
+    lane = lax.broadcasted_iota(jnp.int32, (block, LANE), 1)
+
+    def partner(round_):
+        relation = 3 - round_
+        return ((s // 2 + relation // 2) % 2) * 2 + (s % 2 + relation % 2) % 2
+
+    def ctx_copy(step):
+        at = pl.ds(pl.multiple_of(step % per * block, block), block)
+        return remote(
+            ctx_buf.at[step],
+            ctx_out.at[s, at],
+            ctx_send.at[step],
+            ctx_recv.at[step],
+            seq=partner(step // per),
+        )
+
+    def rows_of(step):
+        base = partner(step // per) * tokens + step % per * block
+        return pl.ds(pl.multiple_of(base, block), block)
+
+    def keep_copies(step):
+        at = rows_of(step)
+        return (
+            pltpu.make_async_copy(qb_buf.at[:, at], qb_out.at[:, at], keep_sem.at[0, step]),
+            pltpu.make_async_copy(o_buf.at[:, at], o_out.at[:, at], keep_sem.at[1, step]),
+        )
+
+    def attend(step, carry):
+        at = rows_of(step)
+        results = []
+        for h in range(heads):
+            q = q_buf[h, at, :]
+            scores = []
+            top = None
+            for c in range(slots // key_chunk):
+                scores.append(dims(q, k_buf[h, c * key_chunk : (c + 1) * key_chunk, :], NT))
+                for j in range(key_chunk // LANE):
+                    tile = scores[-1][:, j * LANE : (j + 1) * LANE]
+                    top = tile if top is None else jnp.maximum(top, tile)
+            top = jnp.max(top, axis=1, keepdims=True)
+            total = None
+            for c in range(slots // key_chunk):
+                probs = jnp.exp2(scores[c] - top).astype(bf16)
+                term = dims(probs, v_buf[h, c * key_chunk : (c + 1) * key_chunk, :], NN)
+                total = term if total is None else total + term
+            weight = total[:, 64:65]
+            result = jnp.where(lane < 64, total * (1.0 / weight), 0.0)
+            o_buf[h, at, :] = result.astype(bf16)
+            high, middle, low = thirds(-(top + jnp.log2(weight)))
+            qb_buf[h, at, :] = with_lanes(
+                q.astype(f32), ((65, high), (66, middle), (67, low))
+            ).astype(bf16)
+            results.append(result)
+        for t in range((heads + 1) // 2):
+            tile = results[2 * t]
+            if 2 * t + 1 < heads:
+                tile = tile + pltpu.roll(results[2 * t + 1], 64, 1)
+            ctx_buf[step, :, t * LANE : (t + 1) * LANE] = tile.astype(bf16)
+
+        @pl.when(step < 3 * per)
+        def _():
+            ctx_copy(step).start()
+
+        for copy in keep_copies(step):
+            copy.start()
+        for g in range(2):
+            @pl.when((step % 2 == g) & (step // 2 + 1 < nf - 1))
+            def _():
+                for w in groups[g]:
+                    ring_hop(w, step // 2 + 1)
+
+        return carry
+
+    lax.fori_loop(0, 4 * per, attend, 0)
+    owns = []
+    for i in range(per):
+        owns.append(
+            pltpu.make_async_copy(
+                ctx_buf.at[3 * per + i], ctx_out.at[s, pl.ds(i * block, block)], own_sem.at[i]
+            )
+        )
+        owns[-1].start()
+
+    def rest(h, carry):
+        for w in range(len(shards)):
+            ring_hop(w, h)
+        return carry
+
+    lax.fori_loop(min(2 * per + 1, nf - 1), nf - 1, rest, 0)
+
+    def settle(step, carry):
+        @pl.when(step < 3 * per)
+        def _():
+            ctx_copy(step).wait()
+
+        for copy in keep_copies(step):
+            copy.wait()
+        return carry
+
+    lax.fori_loop(0, 4 * per, settle, 0)
+    for d in range(1, stages):
+        for m in range(3):
+            along(d, m).wait_send()
+    for d in range(stages):
+        for m in range(3):
+            aside(d, m).wait_send()
+    for d in range(1, nf):
+        vec_copy(d).wait_send()
+    for c in range(parts):
+        far_copy(c).wait_send()
+        pass_copy(c).wait_send()
+    near_copy.wait_send()
+    for copy in owns + mine + kept + saved:
+        copy.wait()
+
+    def close(h, carry):
+        for w in range(len(shards)):
+            ring_finish(w, h)
+        return carry
+
+    lax.fori_loop(0, nf - 1, close, 0)
+
+
+def front(nf, heads, length, states, wq, wk, wv, vec, wout, up, down, block, key_chunk):
+    tokens, width = states.shape
+    rows = wq.shape[0]
+    slots = 4 * tokens
+    parts = 4
+    window = 256
+    shards = (wout, up, down)
+    halves = tuple((1, w.shape[1] // 2) for w in shards)
+    wide = -(-heads // 2) * LANE
+    steps = slots // block
+    shape = jax.ShapeDtypeStruct
+    head_shape = shape((heads, slots, LANE), bf16)
+    head_buf = pltpu.VMEM((heads, slots, LANE), bf16)
+    hops = DMA((3, nf - 1))
+    stage = DMA((nf // 2 - 1, 3))
+    stage_aside = DMA((nf // 2, 3))
+    peers = DMA((nf - 1,))
+    fine = DMA((parts,))
+    return pl.pallas_call(
+        functools.partial(front_kernel, nf, block, key_chunk, halves, ((1,), (0, 2))),
+        out_shape=[head_shape] * 4
+        + [
+            shape((4, tokens, width), bf16),
+            shape((nf,) + vec.shape, bf16),
+            shape((4, tokens, wide), bf16),
+        ]
+        + [shape((nf,) + w.shape, bf16) for w in shards],
+        in_specs=[IN_SMEM] + [ANY] * 8,
+        out_specs=[ANY] * 10,
+        scratch_shapes=[head_buf] * 5
+        + [
+            pltpu.VMEM((steps, block, wide), bf16),
+            pltpu.VMEM((4, tokens, width), bf16),
+            pltpu.VMEM((3, nf, rows, window), bf16),
+            pltpu.VMEM((nf,) + vec.shape, bf16),
+            DMA((5,)),
+            DMA((4,)),
+            DMA((3,)),
+            DMA((2, steps)),
+            peers, peers, stage, stage, stage_aside, stage_aside,
+            DMA(()), DMA(()), fine, fine, fine, fine,
+            hops, hops, hops, hops,
+            DMA((steps,)), DMA((steps,)),
+            DMA((tokens // block,)),
+            DMA((3,)),
+        ],
+        compiler_params=params(1),
+        name="front",
+    )(length, states, wq, wk, wv, vec, wout, up, down)
+
+
+def plane_gather(nf, shards, outs, z_send, z_recv, h_send, h_recv, n_send, n_recv):
+    f = lax.axis_index("fsdp")
+    s, near, _, _ = seq_peers()
+    side = s % 2
+    beside = f + 1 - 2 * (f % 2)
+    stages = nf // 2
+    count = len(shards)
+
+    def half(ref):
+        size = ref.shape[1] // 2
+        return ref.at[:, pl.ds(pl.multiple_of(side * size, size), size)]
+
+    def along(d, m):
+        return remote(
+            half(shards[m]), half(outs[m].at[f]), z_send.at[d - 1, m], z_recv.at[d - 1, m],
+            fsdp=(f + 2 * d) % nf,
+        )
+
+    def aside(d, m):
+        owner = (f + nf - 2 * d) % nf
+        source = outs[m].at[owner] if d else shards[m]
+        return remote(
+            half(source), half(outs[m].at[owner]), h_send.at[d, m], h_recv.at[d, m], fsdp=beside
+        )
+
+    def share(e, m):
+        owner = (f + nf - 2 * e) % nf if e < stages else (beside + nf - 2 * (e - stages)) % nf
+        piece = half(outs[m].at[owner])
+        return remote(piece, piece, n_send.at[e - 1, m], n_recv.at[e - 1, m], seq=near)
+
+    def start():
+        for d in range(1, stages):
+            for m in range(count):
+                along(d, m).start()
+        for m in range(count):
+            aside(0, m).start()
+
+    def first():
+        for d in range(1, stages):
+            for m in range(count):
+                along(d, m).wait_recv()
+                aside(d, m).start()
+                share(d, m).start()
+
+    def second():
+        for d in range(stages):
+            for m in range(count):
+                aside(d, m).wait_recv()
+                share(stages + d, m).start()
+
+    def finish():
+        for m in range(count):
+            for d in range(1, stages):
+                along(d, m).wait_send()
+            for d in range(stages):
+                aside(d, m).wait_send()
+            for e in range(1, nf):
+                share(e, m).wait()
+
+    return start, first, second, finish
+
+
+def feed_kernel(
+    nf, block, part, length_ref, states, ctx, wout, vec, upb, up_hbm, down_hbm, cot_hbm,
+    wq_s, wk_s, wv_s,
+    out, first_grad_out, gctx, up_sum, down_sum, wout_sum, gvec, wq, wk, wv,
+    up, down, cot, out_buf, first_buf, act_buf, pre_buf, slope_buf, low_t, down_t, branch_buf,
+    g_buf, up_give, down_give, wout_give, up_take, down_take, wout_take,
+    load_sem, keep_sem, g_send, g_recv, own_sem, give_send, give_recv, sum_sem, shard_sem,
+    z_send, z_recv, h_send, h_recv, n_send, n_recv,
+):
+    f = lax.axis_index("fsdp")
+    s, near, far, cross = seq_peers()
+    side = s % 2
+    beside = f + 1 - 2 * (f % 2)
+    tokens, width = states.shape
+    hidden = up.shape[1]
+    own = wout.shape[0] // 4
+    steps = tokens // block
+    wide = ctx.shape[2]
+    loads = [
+        pltpu.make_async_copy(up_hbm, up, load_sem.at[0]),
+        pltpu.make_async_copy(down_hbm, down, load_sem.at[1]),
+        pltpu.make_async_copy(cot_hbm, cot, load_sem.at[2]),
+    ]
+    for copy in loads:
+        copy.start()
+    shards, outs = (wq_s, wk_s, wv_s), (wq, wk, wv)
+    gather = plane_gather(nf, shards, outs, z_send, z_recv, h_send, h_recv, n_send, n_recv)
+    greet(
+        [{"fsdp": (f + 2 * d) % nf} for d in range(1, nf // 2)]
+        + [{"fsdp": beside}, {"seq": near}, {"seq": far}, {"seq": cross}]
+    )
+    gather[0]()
+    kept = [pltpu.make_async_copy(shards[m], outs[m].at[f], shard_sem.at[m]) for m in range(3)]
+    for copy in kept:
+        copy.start()
+    length = length_ref[0]
+    gvec[...] = jnp.zeros_like(gvec)
+    peers = (s, near, far, cross)
+
+    def line(row):
+        return vec[row : row + 1, :]
+
+    def add_line(row, values):
+        gvec[row : row + 1, :] += jnp.sum(values, axis=0, keepdims=True)
+
+    def norm(values):
+        centred = values - jnp.mean(values, axis=1, keepdims=True)
+        scale = lax.rsqrt(jnp.mean(centred * centred, axis=1, keepdims=True) + eps)
+        return centred * scale, scale
+
+    def norm_back(grad, gain, normed, scale):
+        grad = grad * gain
+        return scale * (
+            grad
+            - jnp.mean(grad, axis=1, keepdims=True)
+            - normed * jnp.mean(grad * normed, axis=1, keepdims=True)
+        )
+
+    def rows_of(i):
+        return pl.ds(pl.multiple_of(i * block, block), block)
+
+    def send(relation, i):
+        at = rows_of(i)
+        return remote(
+            g_buf.at[relation, at],
+            gctx.at[s, at],
+            g_send.at[relation - 1, i],
+            g_recv.at[relation - 1, i],
+            seq=peers[relation],
+        )
+
+    def keep(i):
+        at = rows_of(i)
+        return (
+            pltpu.make_async_copy(out_buf.at[at], out.at[at], keep_sem.at[0, i]),
+            pltpu.make_async_copy(first_buf.at[at], first_grad_out.at[at], keep_sem.at[1, i]),
+        )
+
+    def body(i, carry):
+        at = rows_of(i)
+        attended = None
+        for j in range(4):
+            term = dims(ctx[j, at, :own], wout[own * j : own * (j + 1), :], NN)
+            attended = term if attended is None else attended + term
+        normed_first, scale_first = norm(states[at, :].astype(f32) + (attended + line(2)))
+        first = normed_first * line(3) + line(4)
+        low = first.astype(bf16)
+        low_t[:, at] = jnp.transpose(low)
+
+        @pl.when(i == 0)
+        def _():
+            for copy in loads:
+                copy.wait()
+
+        fed = None
+        for c in range(hidden // part):
+            cut = slice(c * part, (c + 1) * part)
+            pre = dims(low, up[:, cut], NN) + upb[:, cut]
+            share = 0.5 + 0.5 * lax.erf(pre * (2.0**-0.5))
+            slope_buf[:, cut] = share + pre * jnp.exp(-0.5 * pre * pre) * (2.0 * math.pi) ** -0.5
+            act = (pre * share).astype(bf16)
+            act_buf[at, cut] = act
+            term = dims(act, down[cut, :], NN)
+            fed = term if fed is None else fed + term
+        normed, scale = norm(first + (fed + line(5)))
+        place = s * tokens + i * block + lax.broadcasted_iota(jnp.int32, (block, 1), 0)
+        valid = jnp.where(place < length, 1.0, 0.0)
+        out_buf[at, :] = ((normed * line(6) + line(7)) * valid).astype(bf16)
+        grad = cot[at, :].astype(f32) * valid
+        add_line(6, grad * normed)
+        add_line(7, grad)
+        second_grad = norm_back(grad, line(6), normed, scale)
+        down_in = second_grad.astype(bf16)
+        add_line(5, down_in.astype(f32))
+        down_t[:, at] = jnp.transpose(down_in)
+        back = second_grad
+        for c in range(hidden // part):
+            cut = slice(c * part, (c + 1) * part)
+            pre_grad = (dims(down_in, down[cut, :], NT) * slope_buf[:, cut]).astype(bf16)
+            pre_buf[at, cut] = pre_grad
+            row = 8 + c * part // width
+            col = c * part % width
+            gvec[row : row + 1, col : col + part] += jnp.sum(
+                pre_grad.astype(f32), axis=0, keepdims=True
+            )
+            back = back + dims(pre_grad, up[:, cut], NT)
+        add_line(3, back * normed_first)
+        add_line(4, back)
+        first_grad = norm_back(back, line(3), normed_first, scale_first)
+        first_buf[at, :] = first_grad
+        branch = first_grad.astype(bf16)
+        branch_buf[at, :] = branch
+        add_line(2, branch.astype(f32))
+        for relation in range(4):
+            rows = pl.ds(pl.multiple_of(peers[relation] * own, 64), own)
+            g_buf[relation, at, :own] = dims(branch, wout[rows, :], NT).astype(bf16)
+            if wide > own:
+                g_buf[relation, at, own:] = jnp.zeros((block, wide - own), bf16)
+            if relation:
+                send(relation, i).start()
+        for copy in keep(i):
+            copy.start()
+
+        @pl.when(i == min(1, steps - 1))
+        def _():
+            gather[1]()
+
+        return carry
+
+    lax.fori_loop(0, steps, body, 0)
+    mine = pltpu.make_async_copy(g_buf.at[0], gctx.at[s], own_sem)
+    mine.start()
+
+    pieces = give_send.shape[1]
+    up_cut = hidden // 2 // pieces
+    down_cut = hidden // pieces
+
+    def up_part(which, c):
+        cut = pl.ds(pl.multiple_of(which * (hidden // 2) + c * up_cut, up_cut), up_cut)
+        return dims(low_t[...], pre_buf[:, cut], NN)
+
+    def down_part(which, c):
+        rows = pl.ds(pl.multiple_of(which * (width // 2), width // 2), width // 2)
+        cut = pl.ds(pl.multiple_of(c * down_cut, down_cut), down_cut)
+        return dims(down_t[rows, :], act_buf[:, cut], NN)
+
+    def wout_part(which, j):
+        cut = pl.ds(pl.multiple_of(which * (width // 2), width // 2), width // 2)
+        return dims(ctx[j, :, :own], branch_buf[:, cut], TN)
+
+    def cols(c, size):
+        return (slice(None), pl.ds(pl.multiple_of(c * size, size), size))
+
+    def give(w, c):
+        if w == 2:
+            pair = wout_give, wout_take
+        else:
+            at = cols(c, (up_cut, down_cut)[w])
+            pair = (up_give, down_give)[w].at[at], (up_take, down_take)[w].at[at]
+        return remote(*pair, give_send.at[w, c], give_recv.at[w, c], seq=near)
+
+    def give_away(c, carry):
+        up_give[cols(c, up_cut)] = up_part(1 - side, c).astype(bf16)
+        give(0, c).start()
+        down_give[cols(c, down_cut)] = down_part(1 - side, c).astype(bf16)
+        give(1, c).start()
+        return carry
+
+    def add_own(c, carry):
+        at = cols(c, up_cut)
+        total = up_part(side, c)
+        give(0, c).wait()
+        up_give[at] = (total + up_take[at].astype(f32)).astype(bf16)
+        at = cols(c, down_cut)
+        total = down_part(side, c)
+        give(1, c).wait()
+        down_give[at] = (total + down_take[at].astype(f32)).astype(bf16)
+        return carry
+
+    lax.fori_loop(0, pieces, give_away, 0)
+    for j in range(4):
+        wout_give[own * j : own * (j + 1), :] = wout_part(1 - side, j).astype(bf16)
+    give(2, 0).start()
+    lax.fori_loop(0, pieces, add_own, 0)
+    sums = [
+        pltpu.make_async_copy(up_give, up_sum, sum_sem.at[0]),
+        pltpu.make_async_copy(down_give, down_sum, sum_sem.at[1]),
+    ]
+    for copy in sums:
+        copy.start()
+    gather[2]()
+    totals = [wout_part(side, j) for j in range(4)]
+    give(2, 0).wait()
+    for j in range(4):
+        at = slice(own * j, own * (j + 1))
+        wout_give[at, :] = (totals[j] + wout_take[at, :].astype(f32)).astype(bf16)
+    sums.append(pltpu.make_async_copy(wout_give, wout_sum, sum_sem.at[2]))
+    sums[-1].start()
+    for relation in range(1, 4):
+        for i in range(steps):
+            send(relation, i).wait()
+    for i in range(steps):
+        for copy in keep(i):
+            copy.wait()
+    gather[3]()
+    for copy in [mine] + kept + sums:
+        copy.wait()
+
+
+def feed(nf, length, states, cot, ctx, wout, up, down, vec, upb, shards, block=256, part=768):
+    tokens, width = states.shape
+    hidden = up.shape[1]
+    wide = ctx.shape[2]
+    pieces = 3
+    shape = jax.ShapeDtypeStruct
+    halves = ((width, hidden // 2), (width // 2, hidden), (width, width // 2))
+    vmem = lambda *size: pltpu.VMEM(size, bf16)
+    steps = tokens // block
+    staged = DMA((nf // 2 - 1, 3))
+    staged_aside = DMA((nf // 2, 3))
+    return pl.pallas_call(
+        functools.partial(feed_kernel, nf, block, part),
+        out_shape=[
+            shape((tokens, width), bf16),
+            shape((tokens, width), f32),
+            shape((4, tokens, wide), bf16),
+        ]
+        + [shape(x, bf16) for x in halves]
+        + [shape((16, width), f32)]
+        + [shape((nf,) + w.shape, bf16) for w in shards],
+        in_specs=[IN_SMEM] + [IN_VMEM] * 5 + [ANY] * 6,
+        out_specs=[ANY] * 6 + [IN_VMEM] + [ANY] * 3,
+        scratch_shapes=[
+            vmem(width, hidden),
+            vmem(hidden, width),
+            vmem(tokens, width),
+            vmem(tokens, width),
+            pltpu.VMEM((tokens, width), f32),
+            vmem(tokens, hidden),
+            vmem(tokens, hidden),
+            pltpu.VMEM((block, hidden), f32),
+            vmem(width, tokens),
+            vmem(width, tokens),
+            vmem(tokens, width),
+            vmem(4, tokens, wide),
+        ]
+        + [vmem(*x) for x in halves] * 2
+        + [
+            DMA((3,)),
+            DMA((2, steps)),
+            DMA((3, steps)),
+            DMA((3, steps)),
+            DMA(()),
+            DMA((3, pieces)),
+            DMA((3, pieces)),
+            DMA((3,)),
+            DMA((3,)),
+            staged, staged, staged_aside, staged_aside,
+            DMA((nf - 1, 3)), DMA((nf - 1, 3)),
+        ],
+        compiler_params=params(3),
+        name="feed",
+    )(length, states, ctx, wout, vec, upb, up, down, cot, *shards)
+
+
+def back_kernel(
+    nf, key_block, groups, q_ref, k_ref, v_ref, o_ref, gctx_ref,
+    up_sum, down_sum, wout_sum, x_hbm, wq_hbm, wk_hbm, wv_hbm, first_hbm, gvec_hbm,
+    states_grad, up_out, down_out, wout_out, qkv_out, vec_out, upb_out,
+    k_t, k_acc, v_acc, d_out, g_all, x_all, w_all, first_grad,
+    own_up, own_dn, own_wo, ring_up, ring_dn, ring_wo, y_up, y_dn, y_wo, z_up, z_dn, z_wo,
+    w_buf, w_came, w_sum, w_parts, v_own, v_came, v_sum, v_parts,
+    load_sem, late_sem, hop_send, hop_recv, y_send, y_recv, z_send, z_recv,
+    d_send, d_recv, d_own, w_send, w_recv, p_send, p_recv, l_send, l_recv, m_send, m_recv,
+):
+    h, i = pl.program_id(0), pl.program_id(1)
+    heads, blocks = pl.num_programs(0), pl.num_programs(1)
+    count = w_buf.shape[0]
+    step = h * blocks + i
+    final = heads * blocks - 1
+    f = lax.axis_index("fsdp")
+    s, near, far, cross = seq_peers()
+    peers = (s, near, far, cross)
+    side = s % 2
+    way = 1 - 2 * side
+    place = place_of(f, nf)
+    ahead = index_at((place + way + nf) % nf, nf)
+    block = q_ref.shape[1]
+    slots = k_ref.shape[1]
+    tokens = slots // 4
+    width = x_all.shape[2]
+    rows = width // nf
+    width_own = count * 64
+    full = (up_sum, down_sum, wout_sum)
+    own = (own_up, own_dn, own_wo)
+    came = (ring_up, ring_dn, ring_wo)
+    y_buf = (y_up, y_dn, y_wo)
+    z_buf = (z_up, z_dn, z_wo)
+    outs = (up_out, down_out, wout_out)
+    by_cols = (False, True, False)
+
+    def chunk_at(w, chunk):
+        size = came[w].shape[1 + by_cols[w]]
+        cut = pl.ds(pl.multiple_of(chunk * size, size), size)
+        return (slice(None), cut) if by_cols[w] else (cut, slice(None))
+
+    def hop(w, t, source):
+        return remote(source, came[w].at[t], hop_send.at[w, t], hop_recv.at[w, t], fsdp=ahead)
+
+    def chunk_of(t):
+        return index_at((place + 2 * nf - way * (1 + t)) % nf, nf)
+
+    def to_far(w):
+        return remote(came[w].at[nf - 2], y_buf[w], y_send.at[w], y_recv.at[w], seq=far)
+
+    def to_near(w):
+        return remote(y_buf[w], z_buf[w], z_send.at[w], z_recv.at[w], seq=near)
+
+    def loads():
+        return [pltpu.make_async_copy(full[w], own[w], load_sem.at[w]) for w in range(3)]
+
+    def late():
+        return [
+            pltpu.make_async_copy(x_hbm, x_all, late_sem.at[0]),
+            pltpu.make_async_copy(wq_hbm, w_all.at[0], late_sem.at[1]),
+            pltpu.make_async_copy(wk_hbm, w_all.at[1], late_sem.at[2]),
+            pltpu.make_async_copy(wv_hbm, w_all.at[2], late_sem.at[3]),
+            pltpu.make_async_copy(first_hbm, first_grad, late_sem.at[4]),
+            pltpu.make_async_copy(gvec_hbm, v_own, late_sem.at[5]),
+        ]
+
+    @pl.when(step == 0)
+    def _():
+        greet(
+            [{"fsdp": (f + d) % nf} for d in range(1, nf)]
+            + [{"seq": near}, {"seq": far}, {"seq": cross}]
+        )
+        for w in range(3):
+            hop(w, 0, full[w].at[chunk_at(w, chunk_of(0))]).start()
+        for copy in loads() + late():
+            copy.start()
+
+    @pl.when(i == 0)
+    def _():
+        k_acc[...] = jnp.zeros_like(k_acc)
+        v_acc[...] = jnp.zeros_like(v_acc)
+        k_t[...] = jnp.transpose(k_ref[0])[:64, :]
+
+    lane = lax.broadcasted_iota(jnp.int32, (block, LANE), 1)
+    first = gctx_ref[:, :LANE].astype(f32)
+    second = gctx_ref[:, LANE:].astype(f32)
+    grad = jnp.where(h == 0, first, jnp.where(h == 1, pltpu.roll(first, 64, 1), second))
+    grad = jnp.where(lane < 64, grad, 0.0)
+    delta = jnp.sum(grad * o_ref[0].astype(f32), axis=1, keepdims=True)
+    high, middle, low = thirds(-delta)
+    grad = with_lanes(grad, ((64, high), (65, middle), (66, low))).astype(bf16)
+    q = q_ref[0]
+    q_total = None
+    for c in range(slots // key_block):
+        ks = slice(c * key_block, (c + 1) * key_block)
+        probs = jnp.exp2(dims(k_ref[0, ks, :], q, NT))
+        score = (probs * dims(v_ref[0, ks, :], grad, NT)).astype(bf16)
+        v_acc[ks, :] += dims(probs.astype(bf16), grad, NN)
+        k_acc[ks, :] += dims(score, q, NN)
+        term = dims(k_t[:, ks], score, NN)
+        q_total = term if q_total is None else q_total + term
+    at_head = pl.ds(pl.multiple_of(h * 64, 64), 64)
+    d_out[0, at_head, pl.ds(pl.multiple_of(i * block, block), block)] = (q_total * 0.125).astype(bf16)
+
+    @pl.when(step == 1)
+    def _():
+        for copy in loads():
+            copy.wait()
+
+    for g in range(2):
+        t = step // 2
+
+        @pl.when((step % 2 == g) & (t > 0) & (t < nf - 1))
+        def _():
+            for w in groups[g]:
+                hop(w, t - 1, came[w].at[t - 1]).wait_recv()
+                here = own[w][chunk_at(w, chunk_of(t))].astype(f32)
+                came[w][t - 1] = (here + came[w][t - 1].astype(f32)).astype(bf16)
+                hop(w, t, came[w].at[t - 1]).start()
+
+        @pl.when((step % 2 == g) & (t == nf - 1))
+        def _():
+            for w in groups[g]:
+                hop(w, nf - 2, came[w].at[nf - 2]).wait_recv()
+                here = own[w][chunk_at(w, f)].astype(f32)
+                came[w][nf - 2] = (here + came[w][nf - 2].astype(f32)).astype(bf16)
+                to_far(w).start()
+
+    def part(relation, m, head):
+        to = peers[relation]
+        source = d_out.at[
+            m, pl.ds(pl.multiple_of(head * 64, 64), 64), pl.ds(pl.multiple_of(to * tokens, tokens), tokens)
+        ]
+        target = g_all.at[m, pl.ds(pl.multiple_of(s * width_own + head * 64, 64), 64), :]
+        return source, target
+
+    def d_copy(relation, m, head):
+        source, target = part(relation, m, head)
+        return remote(
+            source, target, d_send.at[relation - 1, m, head], d_recv.at[relation - 1, m, head],
+            seq=peers[relation],
+        )
+
+    def d_local(m, head):
+        source, target = part(0, m, head)
+        return pltpu.make_async_copy(source, target, d_own.at[m, head])
+
+    def w_copy(head, d):
+        to = (f + d) % nf
+        at = pl.ds(pl.multiple_of(to * rows, rows), rows)
+        return remote(
+            w_buf.at[head, at], w_came.at[head, d - 1], w_send.at[head, d - 1],
+            w_recv.at[head, d - 1], fsdp=to,
+        )
+
+    def p_copy(head, relation):
+        return remote(
+            w_sum.at[head], w_parts.at[s, head], p_send.at[head, relation - 1],
+            p_recv.at[head, relation - 1], seq=peers[relation],
+        )
+
+    def v_copy(d):
+        return remote(
+            v_own, v_came.at[d], l_send.at[d - 1], l_recv.at[d - 1], fsdp=(f + d) % nf
+        )
+
+    def m_copy(relation):
+        return remote(
+            v_sum, v_parts.at[s], m_send.at[relation - 1], m_recv.at[relation - 1],
+            seq=peers[relation],
+        )
+
+    def settle_head(head):
+        for d in range(1, nf):
+            w_copy(head, d).wait()
+        total = w_buf[head, pl.ds(pl.multiple_of(f * rows, rows), rows), :].astype(f32)
+        for d in range(1, nf):
+            total = total + w_came[head, d - 1].astype(f32)
+        w_sum[head] = total.astype(bf16)
+        for relation in (3, 2, 1):
+            p_copy(head, relation).start()
+        w_parts[s, head] = total.astype(bf16)
+
+    @pl.when(i == blocks - 1)
+    def _():
+        d_out[1, at_head, :] = jnp.transpose((k_acc[...] * LN2).astype(bf16))[:64, :]
+        d_out[2, at_head, :] = jnp.transpose(v_acc[...].astype(bf16))[:64, :]
+        for m in range(3):
+            for relation in (3, 2, 1):
+                d_copy(relation, m, h).start()
+            d_local(m, h).start()
+
+        @pl.when(h == 0)
+        def _():
+            for copy in late():
+                copy.wait()
+
+        left = jnp.concatenate([d_out[m, at_head, :] for m in range(3)], axis=0)
+        total = None
+        for j in range(4):
+            term = dims(left[:, j * tokens : (j + 1) * tokens], x_all[j], NN)
+            total = term if total is None else total + term
+        w_buf[h] = jnp.transpose(total).astype(bf16)
+        for d in range(1, nf):
+            w_copy(h, d).start()
+
+        @pl.when(h > 0)
+        def _():
+            settle_head(h - 1)
+
+    @pl.when(step == final)
+    def _():
+        ones = jnp.ones((8, slots), bf16)
+        for row, m in ((0, 0), (1, 2)):
+            line = dims(ones, d_out[m], NT)
+            line = jnp.concatenate([line, jnp.zeros((8, width - width_own), f32)], axis=1)
+            v_own[row : row + 1, :] = pltpu.roll(line, s * width_own, 1)[0:1, :]
+        for d in range(1, nf):
+            v_copy(d).start()
+        for w in range(3):
+            to_far(w).wait()
+            y_buf[w][...] = (
+                came[w][nf - 2].astype(f32) + y_buf[w][...].astype(f32)
+            ).astype(bf16)
+            to_near(w).start()
+        for d in range(1, nf):
+            v_copy(d).wait()
+        v_came[0] = v_own[...]
+        total = None
+        for j in range(nf):
+            term = v_came[(f + nf - j) % nf]
+            total = term if total is None else total + term
+        v_sum[...] = total
+        for relation in (3, 2, 1):
+            m_copy(relation).start()
+        v_parts[s] = total
+        settle_head(count - 1)
+        for w in range(3):
+            for t in range(nf - 1):
+                hop(w, t, came[w].at[t]).wait_send()
+            to_near(w).wait()
+            mine, theirs = y_buf[w][...], z_buf[w][...]
+            out = outs[w]
+            size = out.shape[1] // 2
+            if by_cols[w]:
+                mine, theirs = jnp.transpose(mine), jnp.transpose(theirs)
+            out[:, pl.ds(pl.multiple_of(side * size, size), size)] = mine
+            out[:, pl.ds(pl.multiple_of((1 - side) * size, size), size)] = theirs
+
+        def settle(head, carry):
+            for m in range(3):
+                for relation in range(1, 4):
+                    d_copy(relation, m, head).wait()
+                d_local(m, head).wait()
+            return carry
+
+        lax.fori_loop(0, count, settle, 0)
+        cut_size = 256
+        mats = [w_all[m].reshape(width, width) for m in range(3)]
+        for c in range(width // cut_size):
+            cut = slice(c * cut_size, (c + 1) * cut_size)
+            total = None
+            for m in range(3):
+                term = dims(mats[m][cut, :], g_all[m], NN)
+                total = term if total is None else total + term
+            states_grad[:, cut] = (first_grad[:, cut] + jnp.transpose(total)).astype(bf16)
+        for relation in range(1, 4):
+            m_copy(relation).wait()
+        total = v_parts[0] + v_parts[1] + v_parts[2] + v_parts[3]
+        vec_out[...] = pltpu.roll(total, (width - rows * f) % width, 1)[:, :LANE]
+        cols = 4 * rows
+        lead = f * cols // width
+        line = jnp.zeros((1, width), f32)
+        for r in range(4):
+            line = jnp.where(lead == r, total[8 + r : 9 + r, :], line)
+        line = jnp.broadcast_to(line, (8, width))
+        upb_out[...] = pltpu.roll(line, (width - f * cols % width) % width, 1)[:, :cols]
+        for head in range(count):
+            for relation in range(1, 4):
+                p_copy(head, relation).wait()
+        for m in range(3):
+            qkv_out[m] = jnp.concatenate(
+                [
+                    w_parts[j, head][:, m * 64 : (m + 1) * 64].astype(f32)
+                    for j in range(4)
+                    for head in range(count)
+                ],
+                axis=1,
+            ).astype(bf16)
+
+
+def back(nf, qb, k, v, o, gctx, sums, x_all, mats, first_grad, gvec, block, key_block):
+    heads, slots, _ = qb.shape
+    tokens = slots // 4
+    width = x_all.shape[2]
+    hidden = sums[0].shape[1] * 2
+    rows, cols = width // nf, hidden // nf
+    shape = jax.ShapeDtypeStruct
+    per_block = pl.BlockSpec((1, block, LANE), lambda h, i: (h, i, 0))
+    per_head = pl.BlockSpec((1, slots, LANE), lambda h, i: (h, 0, 0))
+    chunk = ((rows, hidden // 2), (width // 2, cols), (rows, width // 2))
+    vmem = lambda *size: pltpu.VMEM(size, bf16)
+    triple = DMA((3,))
+    hops = DMA((3, nf - 1))
+    own = heads * 64
+    results = [
+        shape((tokens, width), bf16),
+        shape((rows, hidden), bf16),
+        shape((cols, width), bf16),
+        shape((rows, width), bf16),
+        shape((3, rows, width), bf16),
+        shape((16, LANE), f32),
+        shape((8, cols), f32),
+    ]
+    return pl.pallas_call(
+        functools.partial(back_kernel, nf, key_block, ((0,), (1, 2))),
+        grid=(heads, slots // block),
+        out_shape=results,
+        in_specs=[
+            per_block,
+            per_head,
+            per_head,
+            per_block,
+            pl.BlockSpec((block, gctx.shape[1]), lambda h, i: (i, 0)),
+        ]
+        + [ANY] * 9,
+        out_specs=[
+            pl.BlockSpec(x.shape, functools.partial(lambda n, h, i: (0,) * n, len(x.shape)))
+            for x in results
+        ],
+        scratch_shapes=[
+            vmem(64, slots),
+            pltpu.VMEM((slots, LANE), f32),
+            pltpu.VMEM((slots, LANE), f32),
+            vmem(3, own, slots),
+            vmem(3, width, tokens),
+            vmem(4, tokens, width),
+            vmem(3, nf, rows, width),
+            pltpu.VMEM((tokens, width), f32),
+        ]
+        + [vmem(*x.shape) for x in sums]
+        + [vmem(nf - 1, *x) for x in chunk]
+        + [vmem(*x) for x in chunk] * 2
+        + [
+            vmem(heads, width, 192),
+            vmem(heads, nf - 1, rows, 192),
+            vmem(heads, rows, 192),
+            vmem(4, heads, rows, 192),
+            pltpu.VMEM((16, width), f32),
+            pltpu.VMEM((nf, 16, width), f32),
+            pltpu.VMEM((16, width), f32),
+            pltpu.VMEM((4, 16, width), f32),
+            triple, DMA((6,)), hops, hops, triple, triple, triple, triple,
+            DMA((3, 3, heads)), DMA((3, 3, heads)), DMA((3, heads)),
+            DMA((heads, nf - 1)), DMA((heads, nf - 1)), DMA((heads, 3)), DMA((heads, 3)),
+            DMA((nf - 1,)), DMA((nf - 1,)), triple, triple,
+        ],
+        compiler_params=params(4),
+        name="back",
+    )(qb, k, v, o, gctx, *sums, x_all, *mats, first_grad, gvec)
+
+
+def results_kernel(rows, output, states_grad, up, down, wout, qkv, vec, upb, *outs):
+    outs[0][...] = output[...]
+    outs[1][...] = states_grad[...]
+    for m in range(3):
+        outs[2 + m][...] = qkv[m].astype(f32)
+    outs[5][...] = wout[...].astype(f32)
+    outs[6][...] = up[...].astype(f32)
+    outs[7][...] = down[...].astype(f32)
+    for r in range(8):
+        outs[8 + r][...] = vec[r : r + 1, :rows]
+    outs[16][...] = upb[0:1, :]
+
+
+def results(rows, output, states_grad, up, down, wout, qkv, vec, upb):
+    shape = jax.ShapeDtypeStruct
+    pieces = 3
+    grads = [shape(qkv.shape[1:], f32)] * 3 + [shape(x.shape, f32) for x in (wout, up, down)]
+    outs = [shape(output.shape, bf16)] * 2 + grads
+    lines = [shape((1, rows), f32)] * 8 + [shape((1, upb.shape[1]), f32)]
+
+    def cut(x):
+        n = len(x.shape)
+        size = x.shape[: n - 2] + (x.shape[n - 2] // pieces, x.shape[n - 1])
+        return pl.BlockSpec(size, functools.partial(lambda n, i: (0,) * (n - 2) + (i, 0), n))
+
+    def same(x):
+        return pl.BlockSpec(x.shape, lambda i: (0, 0))
+
+    return pl.pallas_call(
+        functools.partial(results_kernel, rows),
+        grid=(pieces,),
+        out_shape=outs + lines,
+        in_specs=[cut(x) for x in (output, states_grad, up, down, wout, qkv)] + [same(vec), same(upb)],
+        out_specs=[cut(x) for x in outs] + [same(x) for x in lines],
+        compiler_params=params(),
+        name="results",
+    )(output, states_grad, up, down, wout, qkv, vec, upb)
+
+
+def fused_device(
+    nf, states, query_weight, key_weight, value_weight, out_weight, query_bias, value_bias,
+    out_bias, first_gain, first_shift, up_weight, up_bias, down_weight, down_bias, second_gain,
+    second_shift, lengths, cotangent,
+):
+    tokens, width = states.shape
+    rows = width // nf
+    hidden = up_weight.shape[1]
+    heads = width // 4 // 64
+    lines = jnp.concatenate(
+        [
+            x.reshape(-1, rows)
+            for x in (
+                query_bias, value_bias, out_bias, first_gain, first_shift, down_bias, second_gain,
+                second_shift, up_bias,
+            )
+        ],
+        axis=0,
+    )
+    vec = jnp.pad(lines, ((0, 16 - lines.shape[0]), (0, LANE - rows)))
+    qb, o, k, v, x_all, vec_all, ctx, wout, up, down = front(
+        nf, heads, lengths, states, query_weight, key_weight, value_weight, vec, out_weight,
+        up_weight, down_weight, block=256, key_chunk=1024,
+    )
+    vec_all = vec_all[:, :, :rows].astype(f32)
+    full = vec_all[:, :8].transpose(1, 0, 2).reshape(8, width)
+    full_up = vec_all[:, 8:12].reshape(1, hidden)
+    output, first_grad, gctx, up_sum, down_sum, wout_sum, gvec, wq, wk, wv = feed(
+        nf, lengths, states, cotangent, ctx, wout.reshape(width, width),
+        up.reshape(width, hidden), down.reshape(hidden, width), full, full_up,
+        (query_weight, key_weight, value_weight),
+    )
+    states_grad, up_grad, down_grad, out_grad, qkv, vec_grad, upb_grad = back(
+        nf, qb, k, v, o, gctx.reshape(4 * tokens, -1), (up_sum, down_sum, wout_sum), x_all,
+        (wq, wk, wv), first_grad, gvec, block=512, key_block=512,
+    )
+    done = results(rows, output, states_grad, up_grad, down_grad, out_grad, qkv, vec_grad, upb_grad)
+    output, states_grad, q_grad, k_grad, v_grad, out_grad, up_grad, down_grad = done[:8]
+    lines = [x.reshape(-1) for x in done[8:]]
+    return (
+        output, states_grad, q_grad, k_grad, v_grad, out_grad, *lines[:5], up_grad, lines[8],
+        down_grad, *lines[5:8],
+    )
+
+
 def solution(mesh):
+    nf, ns = mesh.shape["fsdp"], mesh.shape["seq"]
+
+    def choose(states, query_weight, *rest):
+        rows, width = query_weight.shape
+        fits = ns == 4 and nf in (4, 6, 8) and rows % 16 == 0 and width == 768 and states.shape[0] % 768 == 0
+        device = functools.partial(fused_device, nf) if fits else per_device
+        return device(states, query_weight, *rest)
+
     return jax.shard_map(
-        per_device,
+        choose,
         mesh=mesh,
         in_specs=(
             P(("fsdp", "seq"), None),

time: 1490 us -> 262 us (0.18)
  waiting for transfers between devices: 540 us -> 0 us
  matrix products: 417 us -> 0 us
  Pallas kernels: 0 us -> 255 us
  other arithmetic: 188 us -> 1.98 us
  blocking collectives: 163 us -> 0 us
  local copies, waits for them, and re-layouts: 130 us -> 3.58 us
  starting transfers between devices: 20.7 us -> 0 us
  between operations: 17.8 us -> 1.34 us
    dot_general x60 -> x0, matrix products: 417 us -> none  [the longest x6 79.6 us: backward_step(): jnp.einsum('qhd,khd->hqk', grad_block, values_heads, preferred_element_ty...]
    reduce_scatter x3 -> x0, waiting for transfers between devices: 328 us -> none  [the longest x1 164 us: per_device(): lax.psum_scatter(up_weight_grad, 'fsdp', scatter_dimension=0, tiled=True)]
    pallas_call x0 -> x4, Pallas kernels: none -> 255 us  [the longest x1 120 us: back(): pl.pallas_call(functools.partial(back_kernel, nf, key_block, ((0,), (1, 2...]
    unnamed x16 -> x0, waiting for transfers between devices: 129 us -> none
    convert_element_type x33 -> x1, other arithmetic: 101 us -> 0.76 us  [fused_device(): vec_all = vec_all[:, :, :rows].astype(f32)]
    reduce_sum x14 -> x0, other arithmetic: 75.7 us -> none  [the longest x6 66.1 us: forward_block(): totals = jnp.sum(exponent, axis=-1, keepdims=True)]
    unnamed x2 -> x0, blocking collectives: 75.5 us -> none
    all_gather x6 -> x0, waiting for transfers between devices: 65 us -> none  [the longest x1 35.1 us: per_device(): lax.all_gather(key_weight, 'fsdp', axis=0, tiled=True)]
  transfers between devices with their start and end apart: 18 -> 0, of which waited for: 8 -> 0; matrix products, arithmetic and copies ran while one was open for 42% -> 0% of each run, Pallas kernels for 0% -> 0%
where the time goes in v2:
time: 262 us
  Pallas kernels  255 us (97%)
  local copies, waits for them, and re-layouts  3.58 us (1%)
    pallas_call x1, Pallas kernels, back(): pl.pallas_call(functools.partial(back_kernel, nf, key_block, ((0,), (1, 2...  120 us
    pallas_call x1, Pallas kernels, front(): pl.pallas_call(functools.partial(front_kernel, nf, block, key_chunk, halv...  82.1 us
    pallas_call x1, Pallas kernels, feed(): pl.pallas_call(functools.partial(feed_kernel, nf, block, part), out_shape...  47.6 us
    pallas_call x1, Pallas kernels, results(): pl.pallas_call(functools.partial(results_kernel, rows), grid=(pieces,), o...  5.32 us

profile of v2, /device:TPU:0, one launch (start us, length us, event | category | flops | bytes accessed | tf_op | source)
XLA Modules:
  0.0 261.7 jit_solution(10093368236205752471)
XLA Ops:
  1.3 0.8 reshape.114
  2.1 0.8 concatenate.3
  2.9 0.6 pad.4.vec
  3.5 82.1 %front.1 = (bf16[3,3072,128]{2,1,0:T(8,128)(2,1)}, bf16[3,3072,128]{2,1,0:T(8,128)(2,1)}, bf16[3,3072,128]{2,1,0:T(8,128)(2,1)}, bf16[3,3072,128]{2,1,0:T(8,128)...) custom-call(s32[1]{0:T(128)S(6)} %copy.36.length_ref, ...), custom_call_target="tpu_custom_call" | custom-call | tf_op jit(solution)/shard_map/front/pallas_call | solution.py:754
  85.6 0.8 slice_convert_fusion
  86.3 0.7 reshape.117.upb
  87.0 0.7 reshape.116.vec
  87.7 47.6 %feed.1 = (bf16[768,768]{1,0:T(8,128)(2,1)}, f32[768,768]{1,0:T(8,128)}, bf16[4,768,256]{2,1,0:T(8,128)(2,1)}, bf16[768,1536]{1,0:T(8,128)(2,1)}, bf16[384,3072]...) custom-call(s32[1]{0:T(128)S(6)} %copy.36.length_ref, ...), custom_call_target="tpu_custom_call" | custom-call | tf_op jit(solution)/shard_map/feed/pallas_call | solution.py:1089
  135.4 119.8 %back.1 = (bf16[768,768]{1,0:T(8,128)(2,1)}, bf16[96,3072]{1,0:T(8,128)(2,1)}, bf16[384,768]{1,0:T(8,128)(2,1)}, bf16[96,768]{1,0:T(8,128)(2,1)}, bf16[3,96,768]...) custom-call(bf16[3,3072,128]{2,1,0:T(8,128)(2,1)} %get-tuple-element.67.q_ref, ...), custom_call_target="tpu_custom_call" | custom-call | tf_op jit(solution)/shard_map/back/pallas_call | solution.py:1448
  255.1 5.3 %results.1 = (bf16[768,768]{1,0:T(8,128)(2,1)}, bf16[768,768]{1,0:T(8,128)(2,1)}, f32[96,768]{1,0:T(8,128)}, f32[96,768]{1,0:T(8,128)}, f32[96,768]{1,0:T(8,128)...) custom-call(bf16[768,768]{1,0:T(8,128)(2,1)} %get-tuple-element.66.o, ...), custom_call_target="tpu_custom_call" | custom-call | tf_op jit(solution)/shard_map/results/pallas_call | solution.py:1524
  260.5 1.2 reduce
  (3 shorter events, 0.0 us)

commit v3 on v2

--- a/solution.py
+++ b/solution.py
@@ -323,11 +323,19 @@
     )
 
 
-def greet(partners):
+def hail(partners):
     barrier = pltpu.get_barrier_semaphore()
     for where in partners:
         pl.semaphore_signal(barrier, inc=1, device_id=where, device_id_type=pl.DeviceIdType.MESH)
-    pl.semaphore_wait(barrier, len(partners))
+
+
+def hailed(partners):
+    pl.semaphore_wait(pltpu.get_barrier_semaphore(), len(partners))
+
+
+def greet(partners):
+    hail(partners)
+    hailed(partners)
 
 
 def seq_peers():
@@ -422,7 +430,7 @@
     nf, block, key_chunk, halves, groups,
     length_ref, states, wq, wk, wv, vec, wout_s, up_s, down_s,
     qb_out, o_out, k_out, v_out, x_out, vec_out, ctx_out, wout, up, down,
-    q_buf, k_buf, v_buf, qb_buf, o_buf, ctx_buf, x_buf, w_buf, vec_buf,
+    q_buf, k_buf, v_buf, qb_buf, o_buf, s_buf, top_buf, ctx_buf, x_buf, w_buf, vec_buf,
     local_sem, x_sem, kv_sem, keep_sem, vec_send, vec_recv, z_send, z_recv, h_send, h_recv,
     near_send, near_recv, far_send, far_recv, pass_send, pass_recv,
     ring_send, ring_recv, pair_send, pair_recv, ctx_send, ctx_recv, own_sem, copy_sem,
@@ -486,6 +494,8 @@
     near_copy.start()
     for d in range(1, nf):
         vec_copy(d).start()
+    for w in groups[0] + groups[1]:
+        ring_start(w)
     local = [
         pltpu.make_async_copy(states, x_buf.at[0], local_sem.at[0]),
         pltpu.make_async_copy(vec, vec_buf.at[f], local_sem.at[1]),
@@ -522,8 +532,6 @@
         if d != 2 and passed < parts - 2:
             pass_on(passed)
             passed += 1
-    for w in range(len(shards)):
-        ring_start(w)
     for d in range(1, nf):
         vec_copy(d).wait_recv()
     for d in range(stages):
@@ -586,22 +594,29 @@
 
         lax.fori_loop(low, high, body, 0)
 
+    def hops(g, h):
+        for w in groups[g]:
+            ring_hop(w, h)
+
+    hops(0, 0)
+    hops(1, 0)
     whole(0, s, 0, parts)
     for c in range(passed, parts - 1):
         pass_on(c)
     near_copy.wait_recv()
     keep(1, near)
     whole(1, near, 0, parts)
-    for w in range(len(shards)):
-        ring_hop(w, 0)
+    hops(0, 1)
     whole(2, far, 0, parts - 1)
     pass_on(parts - 1)
+    hops(1, 1)
     whole(2, far, parts - 1, parts)
     keep(2, far)
     for c in range(parts):
         pass_copy(c).wait_recv()
     keep(3, cross)
     whole(3, cross, 0, parts)
+    hops(0, 2)
     saved = [
         pltpu.make_async_copy(k_buf, k_out, kv_sem.at[0]),
         pltpu.make_async_copy(v_buf, v_out, kv_sem.at[1]),
@@ -637,32 +652,54 @@
             pltpu.make_async_copy(o_buf.at[:, at], o_out.at[:, at], keep_sem.at[1, step]),
         )
 
+    chunks = slots // key_chunk
+
+    def score(h, at, c):
+        return dims(q_buf[h, at, :], k_buf[h, c * key_chunk : (c + 1) * key_chunk, :], NT)
+
+    def highest(values, top):
+        for j in range(key_chunk // LANE):
+            tile = values[:, j * LANE : (j + 1) * LANE]
+            top = tile if top is None else jnp.maximum(top, tile)
+        return top
+
+    top = None
+    for c in range(chunks):
+        scores = score(0, rows_of(0), c)
+        s_buf[:, c * key_chunk : (c + 1) * key_chunk] = scores
+        top = highest(scores, top)
+    top_buf[...] = top
+
     def attend(step, carry):
         at = rows_of(step)
+        after = rows_of(jnp.minimum(step + 1, 4 * per - 1))
         results = []
+        current = [s_buf[:, c * key_chunk : (c + 1) * key_chunk] for c in range(chunks)]
+        top = top_buf[...]
         for h in range(heads):
-            q = q_buf[h, at, :]
-            scores = []
+            peak = jnp.max(top, axis=1, keepdims=True)
+            total = None
+            coming = []
             top = None
-            for c in range(slots // key_chunk):
-                scores.append(dims(q, k_buf[h, c * key_chunk : (c + 1) * key_chunk, :], NT))
-                for j in range(key_chunk // LANE):
-                    tile = scores[-1][:, j * LANE : (j + 1) * LANE]
-                    top = tile if top is None else jnp.maximum(top, tile)
-            top = jnp.max(top, axis=1, keepdims=True)
-            total = None
-            for c in range(slots // key_chunk):
-                probs = jnp.exp2(scores[c] - top).astype(bf16)
+            for c in range(chunks):
+                scores = score(h + 1, at, c) if h + 1 < heads else score(0, after, c)
+                coming.append(scores)
+                top = highest(scores, top)
+                probs = jnp.exp2(current[c] - peak).astype(bf16)
                 term = dims(probs, v_buf[h, c * key_chunk : (c + 1) * key_chunk, :], NN)
                 total = term if total is None else total + term
+            current = coming
             weight = total[:, 64:65]
             result = jnp.where(lane < 64, total * (1.0 / weight), 0.0)
             o_buf[h, at, :] = result.astype(bf16)
-            high, middle, low = thirds(-(top + jnp.log2(weight)))
+            high, middle, low = thirds(-(peak + jnp.log2(weight)))
             qb_buf[h, at, :] = with_lanes(
-                q.astype(f32), ((65, high), (66, middle), (67, low))
+                q_buf[h, at, :].astype(f32), ((65, high), (66, middle), (67, low))
             ).astype(bf16)
             results.append(result)
+        for c in range(chunks):
+            s_buf[:, c * key_chunk : (c + 1) * key_chunk] = current[c]
+        top_buf[...] = top
         for t in range((heads + 1) // 2):
             tile = results[2 * t]
             if 2 * t + 1 < heads:
@@ -676,10 +713,11 @@
         for copy in keep_copies(step):
             copy.start()
         for g in range(2):
-            @pl.when((step % 2 == g) & (step // 2 + 1 < nf - 1))
+            late = 2 * (1 - g)
+            h = (2 * step - late + 1) // 5
+            @pl.when(((5 * h + late) // 2 == step) & (h + 3 - g < nf - 1))
             def _():
-                for w in groups[g]:
-                    ring_hop(w, step // 2 + 1)
+                hops(g, h + 3 - g)
 
         return carry
 
@@ -698,7 +736,7 @@
             ring_hop(w, h)
         return carry
 
-    lax.fori_loop(min(2 * per + 1, nf - 1), nf - 1, rest, 0)
+    lax.fori_loop(min(7, nf - 1), nf - 1, rest, 0)
 
     def settle(step, carry):
         @pl.when(step < 3 * per)
@@ -764,6 +802,8 @@
         out_specs=[ANY] * 10,
         scratch_shapes=[head_buf] * 5
         + [
+            pltpu.VMEM((block, slots), f32),
+            pltpu.VMEM((block, LANE), f32),
             pltpu.VMEM((steps, block, wide), bf16),
             pltpu.VMEM((4, tokens, width), bf16),
             pltpu.VMEM((3, nf, rows, window), bf16),
@@ -1135,17 +1175,14 @@
     nf, key_block, groups, q_ref, k_ref, v_ref, o_ref, gctx_ref,
     up_sum, down_sum, wout_sum, x_hbm, wq_hbm, wk_hbm, wv_hbm, first_hbm, gvec_hbm,
     states_grad, up_out, down_out, wout_out, qkv_out, vec_out, upb_out,
-    k_t, k_acc, v_acc, d_out, g_all, x_all, w_all, first_grad,
+    k_acc, v_acc, q_acc, g_buf, q_turned, g_turned, d_out, g_all, x_all, w_all, first_grad,
     own_up, own_dn, own_wo, ring_up, ring_dn, ring_wo, y_up, y_dn, y_wo, z_up, z_dn, z_wo,
-    w_buf, w_came, w_sum, w_parts, v_own, v_came, v_sum, v_parts,
+    w_buf, w_came, w_sum, w_parts, v_own, v_cut, v_came, v_sum, v_parts,
     load_sem, late_sem, hop_send, hop_recv, y_send, y_recv, z_send, z_recv,
     d_send, d_recv, d_own, w_send, w_recv, p_send, p_recv, l_send, l_recv, m_send, m_recv,
 ):
-    h, i = pl.program_id(0), pl.program_id(1)
-    heads, blocks = pl.num_programs(0), pl.num_programs(1)
+    half, h = pl.program_id(0), pl.program_id(1)
     count = w_buf.shape[0]
-    step = h * blocks + i
-    final = heads * blocks - 1
     f = lax.axis_index("fsdp")
     s, near, far, cross = seq_peers()
     peers = (s, near, far, cross)
@@ -1153,9 +1190,9 @@
     way = 1 - 2 * side
     place = place_of(f, nf)
     ahead = index_at((place + way + nf) % nf, nf)
-    block = q_ref.shape[1]
     slots = k_ref.shape[1]
     tokens = slots // 4
+    block = tokens
     width = x_all.shape[2]
     rows = width // nf
     width_own = count * 64
@@ -1197,67 +1234,17 @@
             pltpu.make_async_copy(gvec_hbm, v_own, late_sem.at[5]),
         ]
 
-    @pl.when(step == 0)
+    friends = [{"fsdp": (f + d) % nf} for d in range(1, nf)] + [{"seq": p} for p in peers[1:]]
+
+    @pl.when((half == 0) & (h == 0))
     def _():
-        greet(
-            [{"fsdp": (f + d) % nf} for d in range(1, nf)]
-            + [{"seq": near}, {"seq": far}, {"seq": cross}]
-        )
-        for w in range(3):
-            hop(w, 0, full[w].at[chunk_at(w, chunk_of(0))]).start()
+        hail(friends)
         for copy in loads() + late():
             copy.start()
 
-    @pl.when(i == 0)
-    def _():
-        k_acc[...] = jnp.zeros_like(k_acc)
-        v_acc[...] = jnp.zeros_like(v_acc)
-        k_t[...] = jnp.transpose(k_ref[0])[:64, :]
-
-    lane = lax.broadcasted_iota(jnp.int32, (block, LANE), 1)
-    first = gctx_ref[:, :LANE].astype(f32)
-    second = gctx_ref[:, LANE:].astype(f32)
-    grad = jnp.where(h == 0, first, jnp.where(h == 1, pltpu.roll(first, 64, 1), second))
-    grad = jnp.where(lane < 64, grad, 0.0)
-    delta = jnp.sum(grad * o_ref[0].astype(f32), axis=1, keepdims=True)
-    high, middle, low = thirds(-delta)
-    grad = with_lanes(grad, ((64, high), (65, middle), (66, low))).astype(bf16)
-    q = q_ref[0]
-    q_total = None
-    for c in range(slots // key_block):
-        ks = slice(c * key_block, (c + 1) * key_block)
-        probs = jnp.exp2(dims(k_ref[0, ks, :], q, NT))
-        score = (probs * dims(v_ref[0, ks, :], grad, NT)).astype(bf16)
-        v_acc[ks, :] += dims(probs.astype(bf16), grad, NN)
-        k_acc[ks, :] += dims(score, q, NN)
-        term = dims(k_t[:, ks], score, NN)
-        q_total = term if q_total is None else q_total + term
+    k_acc[...] = jnp.zeros_like(k_acc)
+    v_acc[...] = jnp.zeros_like(v_acc)
     at_head = pl.ds(pl.multiple_of(h * 64, 64), 64)
-    d_out[0, at_head, pl.ds(pl.multiple_of(i * block, block), block)] = (q_total * 0.125).astype(bf16)
-
-    @pl.when(step == 1)
-    def _():
-        for copy in loads():
-            copy.wait()
-
-    for g in range(2):
-        t = step // 2
-
-        @pl.when((step % 2 == g) & (t > 0) & (t < nf - 1))
-        def _():
-            for w in groups[g]:
-                hop(w, t - 1, came[w].at[t - 1]).wait_recv()
-                here = own[w][chunk_at(w, chunk_of(t))].astype(f32)
-                came[w][t - 1] = (here + came[w][t - 1].astype(f32)).astype(bf16)
-                hop(w, t, came[w].at[t - 1]).start()
-
-        @pl.when((step % 2 == g) & (t == nf - 1))
-        def _():
-            for w in groups[g]:
-                hop(w, nf - 2, came[w].at[nf - 2]).wait_recv()
-                here = own[w][chunk_at(w, f)].astype(f32)
-                came[w][nf - 2] = (here + came[w][nf - 2].astype(f32)).astype(bf16)
-                to_far(w).start()
 
     def part(relation, m, head):
         to = peers[relation]
@@ -1280,9 +1267,8 @@
 
     def w_copy(head, d):
         to = (f + d) % nf
-        at = pl.ds(pl.multiple_of(to * rows, rows), rows)
         return remote(
-            w_buf.at[head, at], w_came.at[head, d - 1], w_send.at[head, d - 1],
+            w_buf.at[head, to], w_came.at[head, d - 1], w_send.at[head, d - 1],
             w_recv.at[head, d - 1], fsdp=to,
         )
 
@@ -1293,9 +1279,8 @@
         )
 
     def v_copy(d):
-        return remote(
-            v_own, v_came.at[d], l_send.at[d - 1], l_recv.at[d - 1], fsdp=(f + d) % nf
-        )
+        to = (f + d) % nf
+        return remote(v_cut.at[to], v_came.at[d], l_send.at[d - 1], l_recv.at[d - 1], fsdp=to)
 
     def m_copy(relation):
         return remote(
@@ -1306,7 +1291,7 @@
     def settle_head(head):
         for d in range(1, nf):
             w_copy(head, d).wait()
-        total = w_buf[head, pl.ds(pl.multiple_of(f * rows, rows), rows), :].astype(f32)
+        total = w_buf[head, f].astype(f32)
         for d in range(1, nf):
             total = total + w_came[head, d - 1].astype(f32)
         w_sum[head] = total.astype(bf16)
@@ -1314,13 +1299,109 @@
             p_copy(head, relation).start()
         w_parts[s, head] = total.astype(bf16)
 
-    @pl.when(i == blocks - 1)
+    base = (s // 2 + 1 + half) % 2 * (2 * tokens)
+
+    def round_(turn, carry):
+        step = (half * count + h) * 4 + turn
+        relation = (1 - turn // 2) * (turn + 2) + turn // 2 * (3 - turn)
+        owner = ((s // 2 + relation // 2) % 2) * 2 + (s % 2 + relation % 2) % 2
+        at = pl.ds(pl.multiple_of(owner * tokens, tokens), tokens)
+
+        @pl.when(half == 0)
+        def _():
+            lane = lax.broadcasted_iota(jnp.int32, (block, LANE), 1)
+            first = gctx_ref[at, :LANE].astype(f32)
+            second = gctx_ref[at, LANE:].astype(f32)
+            grad = jnp.where(h == 0, first, jnp.where(h == 1, pltpu.roll(first, 64, 1), second))
+            grad = jnp.where(lane < 64, grad, 0.0)
+            delta = jnp.sum(grad * o_ref[0, at, :].astype(f32), axis=1, keepdims=True)
+            high, middle, low = thirds(-delta)
+            grad = with_lanes(grad, ((64, high), (65, middle), (66, low))).astype(bf16)
+            g_buf[h, at, :] = grad
+            g_turned[h, :, at] = jnp.transpose(grad)[:64, :]
+            q_turned[h, :, at] = jnp.transpose(q_ref[0, at, :])[:64, :]
+
+        q, grad = q_ref[0, at, :], g_buf[h, at, :]
+        q_side, g_side = q_turned[h, :, at], g_turned[h, :, at]
+        q_total = None
+        for c in range(2 * tokens // key_block):
+            ks = slice(c * key_block, (c + 1) * key_block)
+            keys = pl.ds(pl.multiple_of(base + c * key_block, LANE), key_block)
+            k = k_ref[0, keys, :]
+            probs = jnp.exp2(dims(q, k, NT))
+            score = (probs * dims(grad, v_ref[0, keys, :], NT)).astype(bf16)
+            v_acc[:, ks] += dims(g_side, probs.astype(bf16), NN)
+            k_acc[:, ks] += dims(q_side, score, NN)
+            term = dims(score, k, NN)
+            q_total = term if q_total is None else q_total + term
+        q_total = jnp.transpose(q_total)[:64, :]
+
+        @pl.when(half == 0)
+        def _():
+            q_acc[h, :, at] = q_total
+
+        @pl.when(half == 1)
+        def _():
+            d_out[0, at_head, at] = ((q_acc[h, :, at] + q_total) * 0.125).astype(bf16)
+
+        @pl.when(step == 0)
+        def _():
+            hailed(friends)
+            for w in range(3):
+                hop(w, 0, full[w].at[chunk_at(w, chunk_of(0))]).start()
+
+        @pl.when(step == 1)
+        def _():
+            for copy in loads():
+                copy.wait()
+
+        for g in range(2):
+            t = (2 * (step - g) + 1) // 5
+            due = 5 * t // 2 == step - g
+
+            @pl.when(due & (t > 0) & (t < nf - 1))
+            def _():
+                for w in groups[g]:
+                    hop(w, t - 1, came[w].at[t - 1]).wait_recv()
+                    here = own[w][chunk_at(w, chunk_of(t))].astype(f32)
+                    came[w][t - 1] = (here + came[w][t - 1].astype(f32)).astype(bf16)
+                    hop(w, t, came[w].at[t - 1]).start()
+
+            @pl.when(due & (t == nf - 1))
+            def _():
+                for w in groups[g]:
+                    hop(w, nf - 2, came[w].at[nf - 2]).wait_recv()
+                    here = own[w][chunk_at(w, f)].astype(f32)
+                    came[w][nf - 2] = (here + came[w][nf - 2].astype(f32)).astype(bf16)
+                    to_far(w).start()
+
+        for stage, kind in enumerate((2, 3, 1)):
+            @pl.when((half == 1) & (turn == stage))
+            def _():
+                d_copy(kind, 0, h).start()
+
+        @pl.when((half == 1) & (h > 0) & (turn == 1))
+        def _():
+            settle_head(h - 1)
+
+        return carry
+
+    lax.fori_loop(0, 4, round_, 0)
+    keys = pl.ds(pl.multiple_of(base, 2 * tokens), 2 * tokens)
+    d_out[1, at_head, keys] = (k_acc[...] * LN2).astype(bf16)
+    d_out[2, at_head, keys] = v_acc[...].astype(bf16)
+
+    @pl.when(half == 0)
     def _():
-        d_out[1, at_head, :] = jnp.transpose((k_acc[...] * LN2).astype(bf16))[:64, :]
-        d_out[2, at_head, :] = jnp.transpose(v_acc[...].astype(bf16))[:64, :]
+        for m in (1, 2):
+            for kind in (2, 3):
+                d_copy(kind, m, h).start()
+
+    @pl.when(half == 1)
+    def _():
         for m in range(3):
-            for relation in (3, 2, 1):
-                d_copy(relation, m, h).start()
+            if m:
+                d_copy(1, m, h).start()
             d_local(m, h).start()
 
         @pl.when(h == 0)
@@ -1333,21 +1414,39 @@
         for j in range(4):
             term = dims(left[:, j * tokens : (j + 1) * tokens], x_all[j], NN)
             total = term if total is None else total + term
-        w_buf[h] = jnp.transpose(total).astype(bf16)
+        total = jnp.transpose(total).astype(bf16)
+        for j in range(nf):
+            w_buf[h, j] = jnp.concatenate(
+                [total[rows * j + rows // 2 * e : rows * j + rows // 2 * (e + 1)] for e in range(2)],
+                axis=1,
+            )
         for d in range(1, nf):
             w_copy(h, d).start()
 
-        @pl.when(h > 0)
-        def _():
-            settle_head(h - 1)
-
-    @pl.when(step == final)
+    @pl.when((half == 1) & (h == count - 1))
     def _():
         ones = jnp.ones((8, slots), bf16)
         for row, m in ((0, 0), (1, 2)):
             line = dims(ones, d_out[m], NT)
             line = jnp.concatenate([line, jnp.zeros((8, width - width_own), f32)], axis=1)
             v_own[row : row + 1, :] = pltpu.roll(line, s * width_own, 1)[0:1, :]
+        lines = v_own[...]
+        flat = jnp.concatenate([lines[8 + r : 9 + r, :] for r in range(4)], axis=1)
+        for j in range(nf):
+            piece = lines if j == 0 else pltpu.roll(lines, width - rows * j, 1)
+            v_cut[j, 0:8, :] = piece[0:8, :LANE]
+            for r in range(4):
+                start = rows * (4 * j + r)
+                shift = start % LANE
+                tile = start - shift
+                both = jnp.concatenate(
+                    [flat[:, tile : tile + LANE], flat[:, min(tile + LANE, flat.shape[1] - LANE) :][:, :LANE]],
+                    axis=1,
+                )
+                if shift:
+                    both = pltpu.roll(both, 2 * LANE - shift, 1)
+                v_cut[j, 8 + r : 9 + r, :] = both[:, :LANE]
+            v_cut[j, 12:16, :] = jnp.zeros((4, LANE), f32)
         for d in range(1, nf):
             v_copy(d).start()
         for w in range(3):
@@ -1356,16 +1455,34 @@
                 came[w][nf - 2].astype(f32) + y_buf[w][...].astype(f32)
             ).astype(bf16)
             to_near(w).start()
+
+        def settle(head, carry):
+            for m in range(3):
+                for kind in range(1, 4):
+                    d_copy(kind, m, head).wait()
+                d_local(m, head).wait()
+            return carry
+
+        lax.fori_loop(0, count, settle, 0)
+        cut_size = 256
+        mats = [w_all[m].reshape(width, width) for m in range(3)]
+        for c in range(width // cut_size):
+            cut = slice(c * cut_size, (c + 1) * cut_size)
+            total = None
+            for m in range(3):
+                term = dims(mats[m][cut, :], g_all[m], NN)
+                total = term if total is None else total + term
+            states_grad[:, cut] = (first_grad[:, cut] + jnp.transpose(total)).astype(bf16)
         for d in range(1, nf):
             v_copy(d).wait()
-        v_came[0] = v_own[...]
+        v_came[0] = v_cut[f]
         total = None
         for j in range(nf):
             term = v_came[(f + nf - j) % nf]
             total = term if total is None else total + term
         v_sum[...] = total
-        for relation in (3, 2, 1):
-            m_copy(relation).start()
+        for kind in (3, 2, 1):
+            m_copy(kind).start()
         v_parts[s] = total
         settle_head(count - 1)
         for w in range(3):
@@ -1379,63 +1496,50 @@
                 mine, theirs = jnp.transpose(mine), jnp.transpose(theirs)
             out[:, pl.ds(pl.multiple_of(side * size, size), size)] = mine
             out[:, pl.ds(pl.multiple_of((1 - side) * size, size), size)] = theirs
-
-        def settle(head, carry):
-            for m in range(3):
-                for relation in range(1, 4):
-                    d_copy(relation, m, head).wait()
-                d_local(m, head).wait()
-            return carry
-
-        lax.fori_loop(0, count, settle, 0)
-        cut_size = 256
-        mats = [w_all[m].reshape(width, width) for m in range(3)]
-        for c in range(width // cut_size):
-            cut = slice(c * cut_size, (c + 1) * cut_size)
-            total = None
-            for m in range(3):
-                term = dims(mats[m][cut, :], g_all[m], NN)
-                total = term if total is None else total + term
-            states_grad[:, cut] = (first_grad[:, cut] + jnp.transpose(total)).astype(bf16)
         for relation in range(1, 4):
             m_copy(relation).wait()
         total = v_parts[0] + v_parts[1] + v_parts[2] + v_parts[3]
-        vec_out[...] = pltpu.roll(total, (width - rows * f) % width, 1)[:, :LANE]
-        cols = 4 * rows
-        lead = f * cols // width
-        line = jnp.zeros((1, width), f32)
+        vec_out[...] = total
+        lane = lax.broadcasted_iota(jnp.int32, (1, 4 * rows), 1)
+        line = jnp.zeros((1, 4 * rows), f32)
         for r in range(4):
-            line = jnp.where(lead == r, total[8 + r : 9 + r, :], line)
-        line = jnp.broadcast_to(line, (8, width))
-        upb_out[...] = pltpu.roll(line, (width - f * cols % width) % width, 1)[:, :cols]
+            piece = jnp.concatenate(
+                [total[8 + r : 9 + r, :], jnp.zeros((1, 4 * rows - LANE), f32)], axis=1
+            )
+            if r:
+                piece = pltpu.roll(piece, rows * r, 1)
+            line = jnp.where((lane >= rows * r) & (lane < rows * (r + 1)), piece, line)
+        upb_out[...] = jnp.broadcast_to(line, upb_out.shape)
         for head in range(count):
             for relation in range(1, 4):
                 p_copy(head, relation).wait()
+        parts = [
+            [
+                jnp.concatenate([both[:, : 3 * 64], both[:, 3 * 64 :]], axis=0)
+                for both in [w_parts[j, head].astype(f32) for head in range(count)]
+            ]
+            for j in range(4)
+        ]
         for m in range(3):
             qkv_out[m] = jnp.concatenate(
-                [
-                    w_parts[j, head][:, m * 64 : (m + 1) * 64].astype(f32)
-                    for j in range(4)
-                    for head in range(count)
-                ],
-                axis=1,
+                [part[:, m * 64 : (m + 1) * 64] for group in parts for part in group], axis=1
             ).astype(bf16)
 
 
-def back(nf, qb, k, v, o, gctx, sums, x_all, mats, first_grad, gvec, block, key_block):
+def back(nf, qb, k, v, o, gctx, sums, x_all, mats, first_grad, gvec, key_block):
     heads, slots, _ = qb.shape
     tokens = slots // 4
     width = x_all.shape[2]
     hidden = sums[0].shape[1] * 2
     rows, cols = width // nf, hidden // nf
     shape = jax.ShapeDtypeStruct
-    per_block = pl.BlockSpec((1, block, LANE), lambda h, i: (h, i, 0))
-    per_head = pl.BlockSpec((1, slots, LANE), lambda h, i: (h, 0, 0))
+    per_head = pl.BlockSpec((1, slots, LANE), lambda p, h: (h, 0, 0))
     chunk = ((rows, hidden // 2), (width // 2, cols), (rows, width // 2))
     vmem = lambda *size: pltpu.VMEM(size, bf16)
     triple = DMA((3,))
     hops = DMA((3, nf - 1))
     own = heads * 64
+    packed = (rows // 2, 6 * 64)
     results = [
         shape((tokens, width), bf16),
         shape((rows, hidden), bf16),
@@ -1447,24 +1551,20 @@
     ]
     return pl.pallas_call(
         functools.partial(back_kernel, nf, key_block, ((0,), (1, 2))),
-        grid=(heads, slots // block),
+        grid=(2, heads),
         out_shape=results,
-        in_specs=[
-            per_block,
-            per_head,
-            per_head,
-            per_block,
-            pl.BlockSpec((block, gctx.shape[1]), lambda h, i: (i, 0)),
-        ]
-        + [ANY] * 9,
+        in_specs=[per_head] * 4 + [IN_VMEM] + [ANY] * 9,
         out_specs=[
-            pl.BlockSpec(x.shape, functools.partial(lambda n, h, i: (0,) * n, len(x.shape)))
+            pl.BlockSpec(x.shape, functools.partial(lambda n, *_: (0,) * n, len(x.shape)))
             for x in results
         ],
         scratch_shapes=[
-            vmem(64, slots),
-            pltpu.VMEM((slots, LANE), f32),
-            pltpu.VMEM((slots, LANE), f32),
+            pltpu.VMEM((64, slots // 2), f32),
+            pltpu.VMEM((64, slots // 2), f32),
+            pltpu.VMEM((heads, 64, slots), f32),
+            vmem(heads, slots, LANE),
+            vmem(heads, 64, slots),
+            vmem(heads, 64, slots),
             vmem(3, own, slots),
             vmem(3, width, tokens),
             vmem(4, tokens, width),
@@ -1475,14 +1575,15 @@
         + [vmem(nf - 1, *x) for x in chunk]
         + [vmem(*x) for x in chunk] * 2
         + [
-            vmem(heads, width, 192),
-            vmem(heads, nf - 1, rows, 192),
-            vmem(heads, rows, 192),
-            vmem(4, heads, rows, 192),
+            vmem(heads, nf, *packed),
+            vmem(heads, nf - 1, *packed),
+            vmem(heads, *packed),
+            vmem(4, heads, *packed),
             pltpu.VMEM((16, width), f32),
-            pltpu.VMEM((nf, 16, width), f32),
-            pltpu.VMEM((16, width), f32),
-            pltpu.VMEM((4, 16, width), f32),
+            pltpu.VMEM((nf, 16, LANE), f32),
+            pltpu.VMEM((nf, 16, LANE), f32),
+            pltpu.VMEM((16, LANE), f32),
+            pltpu.VMEM((4, 16, LANE), f32),
             triple, DMA((6,)), hops, hops, triple, triple, triple, triple,
             DMA((3, 3, heads)), DMA((3, 3, heads)), DMA((3, heads)),
             DMA((heads, nf - 1)), DMA((heads, nf - 1)), DMA((heads, 3)), DMA((heads, 3)),
@@ -1554,7 +1655,7 @@
     vec = jnp.pad(lines, ((0, 16 - lines.shape[0]), (0, LANE - rows)))
     qb, o, k, v, x_all, vec_all, ctx, wout, up, down = front(
         nf, heads, lengths, states, query_weight, key_weight, value_weight, vec, out_weight,
-        up_weight, down_weight, block=256, key_chunk=1024,
+        up_weight, down_weight, block=256, key_chunk=512,
     )
     vec_all = vec_all[:, :, :rows].astype(f32)
     full = vec_all[:, :8].transpose(1, 0, 2).reshape(8, width)
@@ -1566,7 +1667,7 @@
     )
     states_grad, up_grad, down_grad, out_grad, qkv, vec_grad, upb_grad = back(
         nf, qb, k, v, o, gctx.reshape(4 * tokens, -1), (up_sum, down_sum, wout_sum), x_all,
-        (wq, wk, wv), first_grad, gvec, block=512, key_block=512,
+        (wq, wk, wv), first_grad, gvec, key_block=384,
     )
     done = results(rows, output, states_grad, up_grad, down_grad, out_grad, qkv, vec_grad, upb_grad)
     output, states_grad, q_grad, k_grad, v_grad, out_grad, up_grad, down_grad = done[:8]

time: 262 us -> 254 us (0.969)
  Pallas kernels: 255 us -> 246 us
    pallas_call x1, Pallas kernels: 120 us -> 113 us  [back(): pl.pallas_call(functools.partial(back_kernel, nf, key_block, ((0,), (1, 2...]
where the time goes in v3:
time: 254 us; the launch traced here: 253 us
  Pallas kernels  246 us (97%)
  local copies, waits for them, and re-layouts  3.58 us (1%)
    pallas_call x1, Pallas kernels, back(): pl.pallas_call(functools.partial(back_kernel, nf, key_block, ((0,), (1, 2...  113 us
    pallas_call x1, Pallas kernels, front(): pl.pallas_call(functools.partial(front_kernel, nf, block, key_chunk, halv...  80.6 us
    pallas_call x1, Pallas kernels, feed(): pl.pallas_call(functools.partial(feed_kernel, nf, block, part), out_shape...  47.2 us
    pallas_call x1, Pallas kernels, results(): pl.pallas_call(functools.partial(results_kernel, rows), grid=(pieces,), o...  5.32 us

profile of v3, /device:TPU:0, one launch (start us, length us, event | category | flops | bytes accessed | tf_op | source)
XLA Modules:
  0.0 253.3 jit_solution(9639846765786128217)
XLA Ops:
  1.3 0.8 reshape.114
  2.1 0.8 concatenate.3
  2.9 0.6 pad.4.vec
  3.5 80.6 %front.1 = (bf16[3,3072,128]{2,1,0:T(8,128)(2,1)}, bf16[3,3072,128]{2,1,0:T(8,128)(2,1)}, bf16[3,3072,128]{2,1,0:T(8,128)(2,1)}, bf16[3,3072,128]{2,1,0:T(8,128)...) custom-call(s32[1]{0:T(128)S(6)} %copy.36.length_ref, ...), custom_call_target="tpu_custom_call" | custom-call | tf_op jit(solution)/shard_map/front/pallas_call | solution.py:792
  84.1 0.8 slice_convert_fusion
  84.8 0.7 reshape.117.upb
  85.5 0.7 reshape.116.vec
  86.2 47.2 %feed.1 = (bf16[768,768]{1,0:T(8,128)(2,1)}, f32[768,768]{1,0:T(8,128)}, bf16[4,768,256]{2,1,0:T(8,128)(2,1)}, bf16[768,1536]{1,0:T(8,128)(2,1)}, bf16[384,3072]...) custom-call(s32[1]{0:T(128)S(6)} %copy.36.length_ref, ...), custom_call_target="tpu_custom_call" | custom-call | tf_op jit(solution)/shard_map/feed/pallas_call | solution.py:1129
  133.4 113.3 %back.1 = (bf16[768,768]{1,0:T(8,128)(2,1)}, bf16[96,3072]{1,0:T(8,128)(2,1)}, bf16[384,768]{1,0:T(8,128)(2,1)}, bf16[96,768]{1,0:T(8,128)(2,1)}, bf16[3,96,768]...) custom-call(bf16[3,3072,128]{2,1,0:T(8,128)(2,1)} %get-tuple-element.67.q_ref, ...), custom_call_target="tpu_custom_call" | custom-call | tf_op jit(solution)/shard_map/back/pallas_call | solution.py:1552
  246.8 5.3 %results.1 = (bf16[768,768]{1,0:T(8,128)(2,1)}, bf16[768,768]{1,0:T(8,128)(2,1)}, f32[96,768]{1,0:T(8,128)}, f32[96,768]{1,0:T(8,128)}, f32[96,768]{1,0:T(8,128)...) custom-call(bf16[768,768]{1,0:T(8,128)(2,1)} %get-tuple-element.66.o, ...), custom_call_target="tpu_custom_call" | custom-call | tf_op jit(solution)/shard_map/results/pallas_call | solution.py:1625
  252.1 1.2 reduce
  (3 shorter events, 0.0 us)

commit v4 on v3

--- a/solution.py
+++ b/solution.py
@@ -428,19 +428,23 @@
 
 def front_kernel(
     nf, block, key_chunk, halves, groups,
-    length_ref, states, wq, wk, wv, vec, wout_s, up_s, down_s,
-    qb_out, o_out, k_out, v_out, x_out, vec_out, ctx_out, wout, up, down,
-    q_buf, k_buf, v_buf, qb_buf, o_buf, s_buf, top_buf, ctx_buf, x_buf, w_buf, vec_buf,
-    local_sem, x_sem, kv_sem, keep_sem, vec_send, vec_recv, z_send, z_recv, h_send, h_recv,
-    near_send, near_recv, far_send, far_recv, pass_send, pass_recv,
-    ring_send, ring_recv, pair_send, pair_recv, ctx_send, ctx_recv, own_sem, copy_sem,
+    length_ref, states, wq, wk, wv, wout_s, up_s, down_s, *refs,
 ):
+    small_params, refs = refs[:9], refs[9:]
+    (
+qb_out, o_out, k_out, v_out, x_out, vec_out, ctx_out, wout, up, down,
+        q_buf, k_buf, v_buf, qb_buf, o_buf, s_buf, top_buf, ctx_buf, x_buf, w_buf, w_own, packed, vec_own, vec_buf,
+        wout_buf, up_buf, down_buf, local_sem, x_sem, kv_sem, keep_sem, vec_send, vec_recv, z_send, z_recv, h_send, h_recv,
+        near_send, near_recv, far_send, far_recv, pass_send, pass_recv,
+        ring_send, ring_recv, pair_send, pair_recv, ctx_send, ctx_recv, own_sem, copy_sem,
+    ) = refs
     f = lax.axis_index("fsdp")
     s, near, far, cross = seq_peers()
     tokens, width = states.shape
     heads, slots, _ = q_buf.shape
     rows = wq.shape[0]
-    window = w_buf.shape[3]
+    window = w_buf.shape[2]
+    vec_rows = vec_buf.shape[1]
     own_width = heads * 64
     parts = far_send.shape[0]
     chunk = tokens // parts
@@ -453,25 +457,24 @@
     ring_start, ring_hop, ring_finish = ring_gather(
         nf, shards, halves, outs, ring_send, ring_recv, pair_send, pair_recv
     )
-    greet(
-        [{"fsdp": (f + d) % nf} for d in range(1, nf)]
-        + [{"seq": near}, {"seq": far}, {"seq": cross}]
-    )
-
-    def windowed(m):
-        return weights[m].at[:, pl.ds(first_lane, window)]
-
-    def along(d, m):
+    friends = [{"fsdp": (f + d) % nf} for d in range(1, nf)] + [
+        {"seq": near}, {"seq": far}, {"seq": cross},
+    ]
+    hail(friends)
+
+    def along(d):
         to = (f + 2 * d) % nf
-        return remote(windowed(m), w_buf.at[m, f], z_send.at[d - 1, m], z_recv.at[d - 1, m], fsdp=to)
-
-    def aside(d, m):
+        return remote(packed.at[f], packed.at[f], z_send.at[d - 1], z_recv.at[d - 1], fsdp=to)
+
+    def aside(d):
         owner = (f + nf - 2 * d) % nf
-        source = w_buf.at[m, owner] if d else windowed(m)
-        return remote(source, w_buf.at[m, owner], h_send.at[d, m], h_recv.at[d, m], fsdp=beside)
+        return remote(packed.at[owner], packed.at[owner], h_send.at[d], h_recv.at[d], fsdp=beside)
 
     def vec_copy(d):
-        return remote(vec, vec_buf.at[f], vec_send.at[d - 1], vec_recv.at[d - 1], fsdp=(f + d) % nf)
+        return remote(
+            vec_buf.at[f], vec_buf.at[f], vec_send.at[d - 1], vec_recv.at[d - 1],
+            fsdp=(f + d) % nf,
+        )
 
     def far_copy(c):
         at = pl.ds(c * chunk, chunk)
@@ -484,11 +487,33 @@
         )
 
     near_copy = remote(states, x_buf.at[1], near_send, near_recv, seq=near)
+    windows = [
+        pltpu.make_async_copy(
+            weights[m].at[:, pl.ds(first_lane, window)], w_own.at[m], local_sem.at[1 + m]
+        )
+        for m in range(3)
+    ]
+    local = [pltpu.make_async_copy(states, x_buf.at[0], local_sem.at[0])]
+    for copy in windows + local:
+        copy.start()
+    vec_own[...] = jnp.zeros_like(vec_own)
+    for r in range(8):
+        vec_own[r : r + 1, :rows] = small_params[r][...].astype(f32).reshape(1, rows)
+    line = small_params[8][...].astype(f32).reshape(1, 4 * rows)
+    for r in range(4):
+        vec_own[8 + r : 9 + r, :rows] = line[:, rows * r : rows * (r + 1)]
+    vec_buf[f] = vec_own[...].astype(bf16)
+    turn = (window - (own_width * s) % LANE) % window
+    for m in range(3):
+        windows[m].wait()
+        columns = pltpu.roll(w_own[m].astype(f32), turn, 1)[:, :own_width]
+        packed[f, m] = jnp.concatenate(
+            [columns[: rows // 2], columns[rows // 2 :]], axis=1
+        ).astype(bf16)
+    hailed(friends)
     for d in range(1, stages):
-        for m in range(3):
-            along(d, m).start()
-    for m in range(3):
-        aside(0, m).start()
+        along(d).start()
+    aside(0).start()
     for c in range(parts):
         far_copy(c).start()
     near_copy.start()
@@ -496,16 +521,11 @@
         vec_copy(d).start()
     for w in groups[0] + groups[1]:
         ring_start(w)
-    local = [
-        pltpu.make_async_copy(states, x_buf.at[0], local_sem.at[0]),
-        pltpu.make_async_copy(vec, vec_buf.at[f], local_sem.at[1]),
+    held = (wout_buf, up_buf, down_buf)
+    mine = [
+        pltpu.make_async_copy(shards[w], held[w], copy_sem.at[0, w]) for w in range(len(shards))
     ]
-    for m in range(3):
-        local.append(pltpu.make_async_copy(windowed(m), w_buf.at[m, f], local_sem.at[2 + m]))
-    mine = [
-        pltpu.make_async_copy(shards[w], outs[w].at[f], copy_sem.at[w]) for w in range(len(shards))
-    ]
-    for copy in local + mine:
+    for copy in mine:
         copy.start()
     for copy in local:
         copy.wait()
@@ -521,11 +541,17 @@
         pass_copy(c).start()
 
     def turn_aside(d):
-        for m in range(3):
-            along(d, m).wait_recv()
-            aside(d, m).start()
+        along(d).wait_recv()
+        aside(d).start()
 
     keep(0, s)
+    for copy in mine:
+        copy.wait()
+    mine = [
+        pltpu.make_async_copy(held[w], outs[w].at[f], copy_sem.at[1, w]) for w in range(len(shards))
+    ]
+    for copy in mine:
+        copy.start()
     passed = 0
     for d in range(1, stages):
         turn_aside(d)
@@ -535,10 +561,15 @@
     for d in range(1, nf):
         vec_copy(d).wait_recv()
     for d in range(stages):
+        aside(d).wait_recv()
+    gap = jnp.zeros((rows // 2, window - own_width), f32)
+    for j in range(nf):
         for m in range(3):
-            aside(d, m).wait_recv()
-
-    turn = (window - (own_width * s) % LANE) % window
+            both = packed[j, m].astype(f32)
+            for e in range(2):
+                at = pl.ds(rows * j + rows // 2 * e, rows // 2)
+                columns = both[:, own_width * e : own_width * (e + 1)]
+                w_buf[m, at, :] = jnp.concatenate([columns, gap], axis=1).astype(bf16)
     share = own_width // rows
     wide = lax.broadcasted_iota(jnp.int32, (1, window), 1)
     biases = []
@@ -552,7 +583,7 @@
             line = jnp.where((wide >= i * rows) & (wide < (i + 1) * rows), piece, line)
         biases.append(line)
     length = length_ref[0]
-    mats = [w_buf[m].reshape(nf * rows, window) for m in range(3)]
+    mats = [w_buf[m] for m in range(3)]
     small = lax.broadcasted_iota(jnp.int32, (chunk, LANE), 1)
     q_tail = jnp.where(small == 64, 1.0, 0.0)
     v_tail = jnp.where((small >= 64) & (small < 67), 1.0, 0.0)
@@ -570,14 +601,14 @@
         x = x_buf[slot, pl.ds(pl.multiple_of(part * chunk, chunk), chunk), :]
         start = pl.multiple_of(index * tokens + part * chunk, chunk)
         where = start + lax.broadcasted_iota(jnp.int32, (chunk, LANE), 0)
-        queries = pltpu.roll(dims(x, mats[0], NN), turn, 1) + biases[0]
-        keys = pltpu.roll(dims(x, mats[1], NN), turn, 1)
+        queries = dims(x, mats[0], NN) + biases[0]
+        keys = dims(x, mats[1], NN)
         k_tail = jnp.where(
             small == 64,
             jnp.where(where < length, 0.0, -1e9),
             jnp.where((small > 64) & (small < 68), 1.0, 0.0),
         )
-        values = pltpu.roll(dims(x, mats[2], NN), turn, 1) + biases[1]
+        values = dims(x, mats[2], NN) + biases[1]
         at = pl.ds(start, chunk)
         for ref, found in (
             (q_buf, heads_of(queries * (LOG2E * 0.125), q_tail)),
@@ -749,11 +780,9 @@
 
     lax.fori_loop(0, 4 * per, settle, 0)
     for d in range(1, stages):
-        for m in range(3):
-            along(d, m).wait_send()
+        along(d).wait_send()
     for d in range(stages):
-        for m in range(3):
-            aside(d, m).wait_send()
+        aside(d).wait_send()
     for d in range(1, nf):
         vec_copy(d).wait_send()
     for c in range(parts):
@@ -771,7 +800,7 @@
     lax.fori_loop(0, nf - 1, close, 0)
 
 
-def front(nf, heads, length, states, wq, wk, wv, vec, wout, up, down, block, key_chunk):
+def front(nf, heads, length, states, wq, wk, wv, wout, up, down, small_params, block, key_chunk):
     tokens, width = states.shape
     rows = wq.shape[0]
     slots = 4 * tokens
@@ -785,8 +814,8 @@
     head_shape = shape((heads, slots, LANE), bf16)
     head_buf = pltpu.VMEM((heads, slots, LANE), bf16)
     hops = DMA((3, nf - 1))
-    stage = DMA((nf // 2 - 1, 3))
-    stage_aside = DMA((nf // 2, 3))
+    stage = DMA((nf // 2 - 1,))
+    stage_aside = DMA((nf // 2,))
     peers = DMA((nf - 1,))
     fine = DMA((parts,))
     return pl.pallas_call(
@@ -794,11 +823,11 @@
         out_shape=[head_shape] * 4
         + [
             shape((4, tokens, width), bf16),
-            shape((nf,) + vec.shape, bf16),
+            shape((nf, 16, LANE), bf16),
             shape((4, tokens, wide), bf16),
         ]
         + [shape((nf,) + w.shape, bf16) for w in shards],
-        in_specs=[IN_SMEM] + [ANY] * 8,
+        in_specs=[IN_SMEM] + [ANY] * 7 + [IN_VMEM] * 9,
         out_specs=[ANY] * 10,
         scratch_shapes=[head_buf] * 5
         + [
@@ -806,8 +835,14 @@
             pltpu.VMEM((block, LANE), f32),
             pltpu.VMEM((steps, block, wide), bf16),
             pltpu.VMEM((4, tokens, width), bf16),
-            pltpu.VMEM((3, nf, rows, window), bf16),
-            pltpu.VMEM((nf,) + vec.shape, bf16),
+            pltpu.VMEM((3, width, window), bf16),
+            pltpu.VMEM((3, rows, window), bf16),
+            pltpu.VMEM((nf, 3, rows // 2, heads * 128), bf16),
+            pltpu.VMEM((16, LANE), f32),
+            pltpu.VMEM((nf, 16, LANE), bf16),
+        ]
+        + [pltpu.VMEM(w.shape, bf16) for w in shards]
+        + [
             DMA((5,)),
             DMA((4,)),
             DMA((3,)),
@@ -817,11 +852,11 @@
             hops, hops, hops, hops,
             DMA((steps,)), DMA((steps,)),
             DMA((tokens // block,)),
-            DMA((3,)),
+            DMA((2, 3)),
         ],
         compiler_params=params(1),
         name="front",
-    )(length, states, wq, wk, wv, vec, wout, up, down)
+    )(length, states, wq, wk, wv, wout, up, down, *small_params)
 
 
 def plane_gather(nf, shards, outs, z_send, z_recv, h_send, h_recv, n_send, n_recv):
@@ -887,10 +922,10 @@
 
 
 def feed_kernel(
-    nf, block, part, length_ref, states, ctx, wout, vec, upb, up_hbm, down_hbm, cot_hbm,
+    nf, block, part, length_ref, states, ctx, wout, vec_all, up_hbm, down_hbm, cot_hbm,
     wq_s, wk_s, wv_s,
     out, first_grad_out, gctx, up_sum, down_sum, wout_sum, gvec, wq, wk, wv,
-    up, down, cot, out_buf, first_buf, act_buf, pre_buf, slope_buf, low_t, down_t, branch_buf,
+    up, down, cot, held, vec, upb, out_buf, first_buf, act_buf, pre_buf, slope_buf, low_t, down_t, branch_buf,
     g_buf, up_give, down_give, wout_give, up_take, down_take, wout_take,
     load_sem, keep_sem, g_send, g_recv, own_sem, give_send, give_recv, sum_sem, shard_sem,
     z_send, z_recv, h_send, h_recv, n_send, n_recv,
@@ -913,14 +948,36 @@
         copy.start()
     shards, outs = (wq_s, wk_s, wv_s), (wq, wk, wv)
     gather = plane_gather(nf, shards, outs, z_send, z_recv, h_send, h_recv, n_send, n_recv)
-    greet(
-        [{"fsdp": (f + 2 * d) % nf} for d in range(1, nf // 2)]
-        + [{"fsdp": beside}, {"seq": near}, {"seq": far}, {"seq": cross}]
-    )
-    gather[0]()
-    kept = [pltpu.make_async_copy(shards[m], outs[m].at[f], shard_sem.at[m]) for m in range(3)]
+    friends = [{"fsdp": (f + 2 * d) % nf} for d in range(1, nf // 2)] + [
+        {"fsdp": beside}, {"seq": near}, {"seq": far}, {"seq": cross},
+    ]
+    hail(friends)
+    rows = width // nf
+    short = lax.broadcasted_iota(jnp.int32, vec_all.shape[1:], 1) < rows
+    lines = jnp.zeros((vec_all.shape[1], width), f32)
+    blank = jnp.zeros((vec_all.shape[1], width - LANE), f32)
+    tiles = [jnp.zeros((1, LANE), f32) for _ in range(hidden // LANE)]
+    for j in range(nf):
+        piece = jnp.where(short, vec_all[j].astype(f32), 0.0)
+        both = jnp.concatenate([piece, blank], axis=1)
+        lines = lines + (pltpu.roll(both, rows * j, 1) if j else both)
+        for r in range(4):
+            first_lane = rows * (4 * j + r)
+            tile, shift = first_lane // LANE, first_lane % LANE
+            both = jnp.concatenate([piece[8 + r : 9 + r, :], blank[:1, :LANE]], axis=1)
+            if shift:
+                both = pltpu.roll(both, shift, 1)
+            tiles[tile] = tiles[tile] + both[:, :LANE]
+            if tile + 1 < len(tiles):
+                tiles[tile + 1] = tiles[tile + 1] + both[:, LANE:]
+    vec[...] = lines[:8]
+    upb[...] = jnp.concatenate(tiles, axis=1)
+    kept = [pltpu.make_async_copy(shards[m], held.at[m], shard_sem.at[0, m]) for m in range(3)]
     for copy in kept:
         copy.start()
+    kept_out = [
+        pltpu.make_async_copy(held.at[m], outs[m].at[f], shard_sem.at[1, m]) for m in range(3)
+    ]
     length = length_ref[0]
     gvec[...] = jnp.zeros_like(gvec)
     peers = (s, near, far, cross)
@@ -977,8 +1034,12 @@
 
         @pl.when(i == 0)
         def _():
-            for copy in loads:
+            hailed(friends)
+            gather[0]()
+            for copy in kept + loads:
                 copy.wait()
+            for copy in kept_out:
+                copy.start()
 
         fed = None
         for c in range(hidden // part):
@@ -1111,11 +1172,11 @@
         for copy in keep(i):
             copy.wait()
     gather[3]()
-    for copy in [mine] + kept + sums:
+    for copy in [mine] + kept_out + sums:
         copy.wait()
 
 
-def feed(nf, length, states, cot, ctx, wout, up, down, vec, upb, shards, block=256, part=768):
+def feed(nf, length, states, cot, ctx, wout, up, down, vec_all, shards, block=256, part=768):
     tokens, width = states.shape
     hidden = up.shape[1]
     wide = ctx.shape[2]
@@ -1136,12 +1197,15 @@
         + [shape(x, bf16) for x in halves]
         + [shape((16, width), f32)]
         + [shape((nf,) + w.shape, bf16) for w in shards],
-        in_specs=[IN_SMEM] + [IN_VMEM] * 5 + [ANY] * 6,
+        in_specs=[IN_SMEM] + [IN_VMEM] * 4 + [ANY] * 6,
         out_specs=[ANY] * 6 + [IN_VMEM] + [ANY] * 3,
         scratch_shapes=[
             vmem(width, hidden),
             vmem(hidden, width),
             vmem(tokens, width),
+            vmem(3, *shards[0].shape),
+            pltpu.VMEM((8, width), f32),
+            pltpu.VMEM((1, hidden), f32),
             vmem(tokens, width),
             pltpu.VMEM((tokens, width), f32),
             vmem(tokens, hidden),
@@ -1162,13 +1226,13 @@
             DMA((3, pieces)),
             DMA((3, pieces)),
             DMA((3,)),
-            DMA((3,)),
+            DMA((2, 3)),
             staged, staged, staged_aside, staged_aside,
             DMA((nf - 1, 3)), DMA((nf - 1, 3)),
         ],
         compiler_params=params(3),
         name="feed",
-    )(length, states, ctx, wout, vec, upb, up, down, cot, *shards)
+    )(length, states, ctx, wout, vec_all, up, down, cot, *shards)
 
 
 def back_kernel(
@@ -1603,8 +1667,8 @@
     outs[6][...] = up[...].astype(f32)
     outs[7][...] = down[...].astype(f32)
     for r in range(8):
-        outs[8 + r][...] = vec[r : r + 1, :rows]
-    outs[16][...] = upb[0:1, :]
+        outs[8 + r][...] = vec[r, :rows]
+    outs[16][...] = upb[0, :]
 
 
 def results(rows, output, states_grad, up, down, wout, qkv, vec, upb):
@@ -1612,7 +1676,7 @@
     pieces = 3
     grads = [shape(qkv.shape[1:], f32)] * 3 + [shape(x.shape, f32) for x in (wout, up, down)]
     outs = [shape(output.shape, bf16)] * 2 + grads
-    lines = [shape((1, rows), f32)] * 8 + [shape((1, upb.shape[1]), f32)]
+    lines = [shape((rows,), f32)] * 8 + [shape((upb.shape[1],), f32)]
 
     def cut(x):
         n = len(x.shape)
@@ -1620,7 +1684,7 @@
         return pl.BlockSpec(size, functools.partial(lambda n, i: (0,) * (n - 2) + (i, 0), n))
 
     def same(x):
-        return pl.BlockSpec(x.shape, lambda i: (0, 0))
+        return pl.BlockSpec(x.shape, lambda i: (0,) * len(x.shape))
 
     return pl.pallas_call(
         functools.partial(results_kernel, rows),
@@ -1642,27 +1706,18 @@
     rows = width // nf
     hidden = up_weight.shape[1]
     heads = width // 4 // 64
-    lines = jnp.concatenate(
-        [
-            x.reshape(-1, rows)
-            for x in (
-                query_bias, value_bias, out_bias, first_gain, first_shift, down_bias, second_gain,
-                second_shift, up_bias,
-            )
-        ],
-        axis=0,
-    )
-    vec = jnp.pad(lines, ((0, 16 - lines.shape[0]), (0, LANE - rows)))
     qb, o, k, v, x_all, vec_all, ctx, wout, up, down = front(
-        nf, heads, lengths, states, query_weight, key_weight, value_weight, vec, out_weight,
-        up_weight, down_weight, block=256, key_chunk=512,
-    )
-    vec_all = vec_all[:, :, :rows].astype(f32)
-    full = vec_all[:, :8].transpose(1, 0, 2).reshape(8, width)
-    full_up = vec_all[:, 8:12].reshape(1, hidden)
+        nf, heads, lengths, states, query_weight, key_weight, value_weight, out_weight, up_weight,
+        down_weight,
+        (
+            query_bias, value_bias, out_bias, first_gain, first_shift, down_bias, second_gain,
+            second_shift, up_bias,
+        ),
+        block=256, key_chunk=512,
+    )
     output, first_grad, gctx, up_sum, down_sum, wout_sum, gvec, wq, wk, wv = feed(
         nf, lengths, states, cotangent, ctx, wout.reshape(width, width),
-        up.reshape(width, hidden), down.reshape(hidden, width), full, full_up,
+        up.reshape(width, hidden), down.reshape(hidden, width), vec_all,
         (query_weight, key_weight, value_weight),
     )
     states_grad, up_grad, down_grad, out_grad, qkv, vec_grad, upb_grad = back(
@@ -1671,7 +1726,7 @@
     )
     done = results(rows, output, states_grad, up_grad, down_grad, out_grad, qkv, vec_grad, upb_grad)
     output, states_grad, q_grad, k_grad, v_grad, out_grad, up_grad, down_grad = done[:8]
-    lines = [x.reshape(-1) for x in done[8:]]
+    lines = done[8:]
     return (
         output, states_grad, q_grad, k_grad, v_grad, out_grad, *lines[:5], up_grad, lines[8],
         down_grad, *lines[5:8],

time: 254 us -> 246 us (0.969)
  local copies, waits for them, and re-layouts: 3.58 us -> 0 us
where the time goes in v4:
time: 246 us
  Pallas kernels  244 us (99%)
    pallas_call x1, Pallas kernels, back(): pl.pallas_call(functools.partial(back_kernel, nf, key_block, ((0,), (1, 2...  114 us
    pallas_call x1, Pallas kernels, front(): pl.pallas_call(functools.partial(front_kernel, nf, block, key_chunk, halv...  78.1 us
    pallas_call x1, Pallas kernels, feed(): pl.pallas_call(functools.partial(feed_kernel, nf, block, part), out_shape...  46.9 us
    pallas_call x1, Pallas kernels, results(): pl.pallas_call(functools.partial(results_kernel, rows), grid=(pieces,), o...  5.32 us

profile of v4, /device:TPU:0, one launch (start us, length us, event | category | flops | bytes accessed | tf_op | source)
XLA Modules:
  0.0 245.6 jit_solution(17436777527574625803)
XLA Ops:
  1.3 78.1 %front.1 = (bf16[3,3072,128]{2,1,0:T(8,128)(2,1)}, bf16[3,3072,128]{2,1,0:T(8,128)(2,1)}, bf16[3,3072,128]{2,1,0:T(8,128)(2,1)}, bf16[3,3072,128]{2,1,0:T(8,128)...) custom-call(s32[1]{0:T(128)S(6)} %copy.35.length_ref, ...), custom_call_target="tpu_custom_call" | custom-call | tf_op jit(solution)/shard_map/front/pallas_call | solution.py:821
  79.4 46.9 %feed.1 = (bf16[768,768]{1,0:T(8,128)(2,1)}, f32[768,768]{1,0:T(8,128)}, bf16[4,768,256]{2,1,0:T(8,128)(2,1)}, bf16[768,1536]{1,0:T(8,128)(2,1)}, bf16[384,3072]...) custom-call(s32[1]{0:T(128)S(6)} %copy.35.length_ref, ...), custom_call_target="tpu_custom_call" | custom-call | tf_op jit(solution)/shard_map/feed/pallas_call | solution.py:1190
  126.4 113.7 %back.1 = (bf16[768,768]{1,0:T(8,128)(2,1)}, bf16[96,3072]{1,0:T(8,128)(2,1)}, bf16[384,768]{1,0:T(8,128)(2,1)}, bf16[96,768]{1,0:T(8,128)(2,1)}, bf16[3,96,768]...) custom-call(bf16[3,3072,128]{2,1,0:T(8,128)(2,1)} %get-tuple-element.67.q_ref, ...), custom_call_target="tpu_custom_call" | custom-call | tf_op jit(solution)/shard_map/back/pallas_call | solution.py:1616
  240.1 5.3 %results.1 = (bf16[768,768]{1,0:T(8,128)(2,1)}, bf16[768,768]{1,0:T(8,128)(2,1)}, f32[96,768]{1,0:T(8,128)}, f32[96,768]{1,0:T(8,128)}, f32[96,768]{1,0:T(8,128)...) custom-call(bf16[768,768]{1,0:T(8,128)(2,1)} %get-tuple-element.66.o, ...), custom_call_target="tpu_custom_call" | custom-call | tf_op jit(solution)/shard_map/results/pallas_call | solution.py:1689

commit v5 on v4

--- a/solution.py
+++ b/solution.py
@@ -922,10 +922,10 @@
 
 
 def feed_kernel(
-    nf, block, part, length_ref, states, ctx, wout, vec_all, up_hbm, down_hbm, cot_hbm,
+    nf, block, part, length_ref, vec_all, states_hbm, ctx_hbm, wout_hbm, up_hbm, down_hbm, cot_hbm,
     wq_s, wk_s, wv_s,
     out, first_grad_out, gctx, up_sum, down_sum, wout_sum, gvec, wq, wk, wv,
-    up, down, cot, held, vec, upb, out_buf, first_buf, act_buf, pre_buf, slope_buf, low_t, down_t, branch_buf,
+    states, ctx, wout, up, down, cot, held, vec, upb, out_buf, first_buf, act_buf, pre_buf, slope_buf, low_t, down_t, branch_buf,
     g_buf, up_give, down_give, wout_give, up_take, down_take, wout_take,
     load_sem, keep_sem, g_send, g_recv, own_sem, give_send, give_recv, sum_sem, shard_sem,
     z_send, z_recv, h_send, h_recv, n_send, n_recv,
@@ -944,7 +944,12 @@
         pltpu.make_async_copy(down_hbm, down, load_sem.at[1]),
         pltpu.make_async_copy(cot_hbm, cot, load_sem.at[2]),
     ]
-    for copy in loads:
+    early = [
+        pltpu.make_async_copy(wout_hbm, wout, load_sem.at[3]),
+        pltpu.make_async_copy(ctx_hbm, ctx, load_sem.at[4]),
+        pltpu.make_async_copy(states_hbm, states, load_sem.at[5]),
+    ]
+    for copy in early + loads:
         copy.start()
     shards, outs = (wq_s, wk_s, wv_s), (wq, wk, wv)
     gather = plane_gather(nf, shards, outs, z_send, z_recv, h_send, h_recv, n_send, n_recv)
@@ -1096,6 +1101,8 @@
 
         return carry
 
+    for copy in early:
+        copy.wait()
     lax.fori_loop(0, steps, body, 0)
     mine = pltpu.make_async_copy(g_buf.at[0], gctx.at[s], own_sem)
     mine.start()
@@ -1150,6 +1157,7 @@
     for j in range(4):
         wout_give[own * j : own * (j + 1), :] = wout_part(1 - side, j).astype(bf16)
     give(2, 0).start()
+    gather[2]()
     lax.fori_loop(0, pieces, add_own, 0)
     sums = [
         pltpu.make_async_copy(up_give, up_sum, sum_sem.at[0]),
@@ -1157,7 +1165,6 @@
     ]
     for copy in sums:
         copy.start()
-    gather[2]()
     totals = [wout_part(side, j) for j in range(4)]
     give(2, 0).wait()
     for j in range(4):
@@ -1197,9 +1204,12 @@
         + [shape(x, bf16) for x in halves]
         + [shape((16, width), f32)]
         + [shape((nf,) + w.shape, bf16) for w in shards],
-        in_specs=[IN_SMEM] + [IN_VMEM] * 4 + [ANY] * 6,
+        in_specs=[IN_SMEM, IN_VMEM] + [ANY] * 9,
         out_specs=[ANY] * 6 + [IN_VMEM] + [ANY] * 3,
         scratch_shapes=[
+            vmem(*states.shape),
+            vmem(*ctx.shape),
+            vmem(*wout.shape),
             vmem(width, hidden),
             vmem(hidden, width),
             vmem(tokens, width),
@@ -1218,7 +1228,7 @@
         ]
         + [vmem(*x) for x in halves] * 2
         + [
-            DMA((3,)),
+            DMA((6,)),
             DMA((2, steps)),
             DMA((3, steps)),
             DMA((3, steps)),
@@ -1232,7 +1242,7 @@
         ],
         compiler_params=params(3),
         name="feed",
-    )(length, states, ctx, wout, vec_all, up, down, cot, *shards)
+    )(length, vec_all, states, ctx, wout, up, down, cot, *shards)
 
 
 def back_kernel(
@@ -1365,14 +1375,14 @@
 
     base = (s // 2 + 1 + half) % 2 * (2 * tokens)
 
-    def round_(turn, carry):
+    def round_(early, turn, carry):
         step = (half * count + h) * 4 + turn
         relation = (1 - turn // 2) * (turn + 2) + turn // 2 * (3 - turn)
         owner = ((s // 2 + relation // 2) % 2) * 2 + (s % 2 + relation % 2) % 2
         at = pl.ds(pl.multiple_of(owner * tokens, tokens), tokens)
 
-        @pl.when(half == 0)
-        def _():
+        q = q_ref[0, at, :]
+        if early:
             lane = lax.broadcasted_iota(jnp.int32, (block, LANE), 1)
             first = gctx_ref[at, :LANE].astype(f32)
             second = gctx_ref[at, LANE:].astype(f32)
@@ -1381,12 +1391,14 @@
             delta = jnp.sum(grad * o_ref[0, at, :].astype(f32), axis=1, keepdims=True)
             high, middle, low = thirds(-delta)
             grad = with_lanes(grad, ((64, high), (65, middle), (66, low))).astype(bf16)
+            g_side = jnp.transpose(grad)[:64, :]
+            q_side = jnp.transpose(q)[:64, :]
             g_buf[h, at, :] = grad
-            g_turned[h, :, at] = jnp.transpose(grad)[:64, :]
-            q_turned[h, :, at] = jnp.transpose(q_ref[0, at, :])[:64, :]
-
-        q, grad = q_ref[0, at, :], g_buf[h, at, :]
-        q_side, g_side = q_turned[h, :, at], g_turned[h, :, at]
+            g_turned[h, :, at] = g_side
+            q_turned[h, :, at] = q_side
+        else:
+            grad = g_buf[h, at, :]
+            g_side, q_side = g_turned[h, :, at], q_turned[h, :, at]
         q_total = None
         for c in range(2 * tokens // key_block):
             ks = slice(c * key_block, (c + 1) * key_block)
@@ -1400,24 +1412,22 @@
             q_total = term if q_total is None else q_total + term
         q_total = jnp.transpose(q_total)[:64, :]
 
-        @pl.when(half == 0)
-        def _():
+        if early:
             q_acc[h, :, at] = q_total
-
-        @pl.when(half == 1)
-        def _():
-            d_out[0, at_head, at] = ((q_acc[h, :, at] + q_total) * 0.125).astype(bf16)
-
-        @pl.when(step == 0)
-        def _():
-            hailed(friends)
-            for w in range(3):
-                hop(w, 0, full[w].at[chunk_at(w, chunk_of(0))]).start()
-
-        @pl.when(step == 1)
-        def _():
-            for copy in loads():
-                copy.wait()
+        else:
+            d_out[0, at_head, at] = ((q_total + q_acc[h, :, at]) * 0.125).astype(bf16)
+
+        if early:
+            @pl.when(step == 0)
+            def _():
+                hailed(friends)
+                for w in range(3):
+                    hop(w, 0, full[w].at[chunk_at(w, chunk_of(0))]).start()
+
+            @pl.when(step == 1)
+            def _():
+                for copy in loads():
+                    copy.wait()
 
         for g in range(2):
             t = (2 * (step - g) + 1) // 5
@@ -1431,6 +1441,9 @@
                     came[w][t - 1] = (here + came[w][t - 1].astype(f32)).astype(bf16)
                     hop(w, t, came[w].at[t - 1]).start()
 
+            if early:
+                continue
+
             @pl.when(due & (t == nf - 1))
             def _():
                 for w in groups[g]:
@@ -1439,18 +1452,24 @@
                     came[w][nf - 2] = (here + came[w][nf - 2].astype(f32)).astype(bf16)
                     to_far(w).start()
 
+        if early:
+            return carry
         for stage, kind in enumerate((2, 3, 1)):
-            @pl.when((half == 1) & (turn == stage))
+            @pl.when(turn == stage)
             def _():
                 d_copy(kind, 0, h).start()
 
-        @pl.when((half == 1) & (h > 0) & (turn == 1))
+        @pl.when((h > 0) & (turn == 1))
         def _():
             settle_head(h - 1)
 
         return carry
 
-    lax.fori_loop(0, 4, round_, 0)
+    for early in (True, False):
+        @pl.when(half == (0 if early else 1))
+        def _():
+            lax.fori_loop(0, 4, functools.partial(round_, early), 0)
+
     keys = pl.ds(pl.multiple_of(base, 2 * tokens), 2 * tokens)
     d_out[1, at_head, keys] = (k_acc[...] * LN2).astype(bf16)
     d_out[2, at_head, keys] = v_acc[...].astype(bf16)
@@ -1673,7 +1692,7 @@
 
 def results(rows, output, states_grad, up, down, wout, qkv, vec, upb):
     shape = jax.ShapeDtypeStruct
-    pieces = 3
+    pieces = 2
     grads = [shape(qkv.shape[1:], f32)] * 3 + [shape(x.shape, f32) for x in (wout, up, down)]
     outs = [shape(output.shape, bf16)] * 2 + grads
     lines = [shape((rows,), f32)] * 8 + [shape((upb.shape[1],), f32)]
@@ -1738,7 +1757,7 @@
 
     def choose(states, query_weight, *rest):
         rows, width = query_weight.shape
-        fits = ns == 4 and nf in (4, 6, 8) and rows % 16 == 0 and width == 768 and states.shape[0] % 768 == 0
+        fits = ns == 4 and nf == 8 and rows % 16 == 0 and width == 768 and states.shape[0] % 768 == 0
         device = functools.partial(fused_device, nf) if fits else per_device
         return device(states, query_weight, *rest)
 

time: 246 us -> 241 us (0.980)
  Pallas kernels: 244 us -> 240 us
    pallas_call x1, Pallas kernels: 114 us -> 110 us  [back(): pl.pallas_call(functools.partial(back_kernel, nf, key_block, ((0,), (1, 2...]
where the time goes in v5:
time: 241 us
  Pallas kernels  240 us (100%)
    pallas_call x1, Pallas kernels, back(): pl.pallas_call(functools.partial(back_kernel, nf, key_block, ((0,), (1, 2...  110 us
    pallas_call x1, Pallas kernels, front(): pl.pallas_call(functools.partial(front_kernel, nf, block, key_chunk, halv...  78.1 us
    pallas_call x1, Pallas kernels, feed(): pl.pallas_call(functools.partial(feed_kernel, nf, block, part), out_shape...  47.6 us

profile of v5, /device:TPU:0, one launch (start us, length us, event | category | flops | bytes accessed | tf_op | source)
XLA Modules:
  0.0 241.2 jit_solution(3157104859608724428)
XLA Ops:
  1.3 78.1 %front.1 = (bf16[3,3072,128]{2,1,0:T(8,128)(2,1)}, bf16[3,3072,128]{2,1,0:T(8,128)(2,1)}, bf16[3,3072,128]{2,1,0:T(8,128)(2,1)}, bf16[3,3072,128]{2,1,0:T(8,128)...) custom-call(s32[1]{0:T(128)S(6)} %copy.35.length_ref, ...), custom_call_target="tpu_custom_call" | custom-call | tf_op jit(solution)/shard_map/front/pallas_call | solution.py:821
  79.4 47.6 %feed.1 = (bf16[768,768]{1,0:T(8,128)(2,1)}, f32[768,768]{1,0:T(8,128)}, bf16[4,768,256]{2,1,0:T(8,128)(2,1)}, bf16[768,1536]{1,0:T(8,128)(2,1)}, bf16[384,3072]...) custom-call(s32[1]{0:T(128)S(6)} %copy.35.length_ref, ...), custom_call_target="tpu_custom_call" | custom-call | tf_op jit(solution)/shard_map/feed/pallas_call | solution.py:1197
  127.0 109.7 %back.1 = (bf16[768,768]{1,0:T(8,128)(2,1)}, bf16[96,3072]{1,0:T(8,128)(2,1)}, bf16[384,768]{1,0:T(8,128)(2,1)}, bf16[96,768]{1,0:T(8,128)(2,1)}, bf16[3,96,768]...) custom-call(bf16[3,3072,128]{2,1,0:T(8,128)(2,1)} %get-tuple-element.67.q_ref, ...), custom_call_target="tpu_custom_call" | custom-call | tf_op jit(solution)/shard_map/back/pallas_call | solution.py:1635
  236.7 4.3 %results.1 = (bf16[768,768]{1,0:T(8,128)(2,1)}, bf16[768,768]{1,0:T(8,128)(2,1)}, f32[96,768]{1,0:T(8,128)}, f32[96,768]{1,0:T(8,128)}, f32[96,768]{1,0:T(8,128)...) custom-call(bf16[768,768]{1,0:T(8,128)(2,1)} %get-tuple-element.66.o, ...), custom_call_target="tpu_custom_call" | custom-call | tf_op jit(solution)/shard_map/results/pallas_call | solution.py:1708

commit v6 on v5

--- a/solution.py
+++ b/solution.py
@@ -1430,8 +1430,8 @@
                     copy.wait()
 
         for g in range(2):
-            t = (2 * (step - g) + 1) // 5
-            due = 5 * t // 2 == step - g
+            t = (4 * (step - g) + 3) // 11
+            due = 11 * t // 4 == step - g
 
             @pl.when(due & (t > 0) & (t < nf - 1))
             def _():
@@ -1459,7 +1459,7 @@
             def _():
                 d_copy(kind, 0, h).start()
 
-        @pl.when((h > 0) & (turn == 1))
+        @pl.when((h > 0) & (turn == 3))
         def _():
             settle_head(h - 1)
 

time: 241 us -> 236 us (0.979)
  Pallas kernels: 240 us -> 235 us
    pallas_call x1, Pallas kernels: 110 us -> 105 us  [back(): pl.pallas_call(functools.partial(back_kernel, nf, key_block, ((0,), (1, 2...]
where the time goes in v6:
time: 236 us
  Pallas kernels  235 us (100%)
    pallas_call x1, Pallas kernels, back(): pl.pallas_call(functools.partial(back_kernel, nf, key_block, ((0,), (1, 2...  105 us
    pallas_call x1, Pallas kernels, front(): pl.pallas_call(functools.partial(front_kernel, nf, block, key_chunk, halv...  78.1 us
    pallas_call x1, Pallas kernels, feed(): pl.pallas_call(functools.partial(feed_kernel, nf, block, part), out_shape...  47.6 us

profile of v6, /device:TPU:0, one launch (start us, length us, event | category | flops | bytes accessed | tf_op | source)
XLA Modules:
  0.0 236.2 jit_solution(9299219508786712173)
XLA Ops:
  1.3 78.1 %front.1 = (bf16[3,3072,128]{2,1,0:T(8,128)(2,1)}, bf16[3,3072,128]{2,1,0:T(8,128)(2,1)}, bf16[3,3072,128]{2,1,0:T(8,128)(2,1)}, bf16[3,3072,128]{2,1,0:T(8,128)...) custom-call(s32[1]{0:T(128)S(6)} %copy.35.length_ref, ...), custom_call_target="tpu_custom_call" | custom-call | tf_op jit(solution)/shard_map/front/pallas_call | solution.py:821
  79.4 47.6 %feed.1 = (bf16[768,768]{1,0:T(8,128)(2,1)}, f32[768,768]{1,0:T(8,128)}, bf16[4,768,256]{2,1,0:T(8,128)(2,1)}, bf16[768,1536]{1,0:T(8,128)(2,1)}, bf16[384,3072]...) custom-call(s32[1]{0:T(128)S(6)} %copy.35.length_ref, ...), custom_call_target="tpu_custom_call" | custom-call | tf_op jit(solution)/shard_map/feed/pallas_call | solution.py:1197
  127.0 104.7 %back.1 = (bf16[768,768]{1,0:T(8,128)(2,1)}, bf16[96,3072]{1,0:T(8,128)(2,1)}, bf16[384,768]{1,0:T(8,128)(2,1)}, bf16[96,768]{1,0:T(8,128)(2,1)}, bf16[3,96,768]...) custom-call(bf16[3,3072,128]{2,1,0:T(8,128)(2,1)} %get-tuple-element.67.q_ref, ...), custom_call_target="tpu_custom_call" | custom-call | tf_op jit(solution)/shard_map/back/pallas_call | solution.py:1635
  231.7 4.3 %results.1 = (bf16[768,768]{1,0:T(8,128)(2,1)}, bf16[768,768]{1,0:T(8,128)(2,1)}, f32[96,768]{1,0:T(8,128)}, f32[96,768]{1,0:T(8,128)}, f32[96,768]{1,0:T(8,128)...) custom-call(bf16[768,768]{1,0:T(8,128)(2,1)} %get-tuple-element.66.o, ...), custom_call_target="tpu_custom_call" | custom-call | tf_op jit(solution)/shard_map/results/pallas_call | solution.py:1708

commit v7 on v6

--- a/solution.py
+++ b/solution.py
@@ -1187,7 +1187,7 @@
     tokens, width = states.shape
     hidden = up.shape[1]
     wide = ctx.shape[2]
-    pieces = 3
+    pieces = 2
     shape = jax.ShapeDtypeStruct
     halves = ((width, hidden // 2), (width // 2, hidden), (width, width // 2))
     vmem = lambda *size: pltpu.VMEM(size, bf16)

time: 236 us -> 238 us (level)
  no operation moved by 1% of the time
where the time goes in v7:
time: 238 us
  Pallas kernels  236 us (99%)
    pallas_call x1, Pallas kernels, back(): pl.pallas_call(functools.partial(back_kernel, nf, key_block, ((0,), (1, 2...  106 us
    pallas_call x1, Pallas kernels, front(): pl.pallas_call(functools.partial(front_kernel, nf, block, key_chunk, halv...  78.1 us
    pallas_call x1, Pallas kernels, feed(): pl.pallas_call(functools.partial(feed_kernel, nf, block, part), out_shape...  48.4 us

profile of v7, /device:TPU:0, one launch (start us, length us, event | category | flops | bytes accessed | tf_op | source)
XLA Modules:
  0.0 237.9 jit_solution(10281105799978674308)
XLA Ops:
  1.3 78.1 %front.1 = (bf16[3,3072,128]{2,1,0:T(8,128)(2,1)}, bf16[3,3072,128]{2,1,0:T(8,128)(2,1)}, bf16[3,3072,128]{2,1,0:T(8,128)(2,1)}, bf16[3,3072,128]{2,1,0:T(8,128)...) custom-call(s32[1]{0:T(128)S(6)} %copy.35.length_ref, ...), custom_call_target="tpu_custom_call" | custom-call | tf_op jit(solution)/shard_map/front/pallas_call | solution.py:821
  79.4 48.4 %feed.1 = (bf16[768,768]{1,0:T(8,128)(2,1)}, f32[768,768]{1,0:T(8,128)}, bf16[4,768,256]{2,1,0:T(8,128)(2,1)}, bf16[768,1536]{1,0:T(8,128)(2,1)}, bf16[384,3072]...) custom-call(s32[1]{0:T(128)S(6)} %copy.35.length_ref, ...), custom_call_target="tpu_custom_call" | custom-call | tf_op jit(solution)/shard_map/feed/pallas_call | solution.py:1197
  127.9 105.6 %back.1 = (bf16[768,768]{1,0:T(8,128)(2,1)}, bf16[96,3072]{1,0:T(8,128)(2,1)}, bf16[384,768]{1,0:T(8,128)(2,1)}, bf16[96,768]{1,0:T(8,128)(2,1)}, bf16[3,96,768]...) custom-call(bf16[3,3072,128]{2,1,0:T(8,128)(2,1)} %get-tuple-element.67.q_ref, ...), custom_call_target="tpu_custom_call" | custom-call | tf_op jit(solution)/shard_map/back/pallas_call | solution.py:1635
  233.5 4.3 %results.1 = (bf16[768,768]{1,0:T(8,128)(2,1)}, bf16[768,768]{1,0:T(8,128)(2,1)}, f32[96,768]{1,0:T(8,128)}, f32[96,768]{1,0:T(8,128)}, f32[96,768]{1,0:T(8,128)...) custom-call(bf16[768,768]{1,0:T(8,128)(2,1)} %get-tuple-element.66.o, ...), custom_call_target="tpu_custom_call" | custom-call | tf_op jit(solution)/shard_map/results/pallas_call | solution.py:1708
